TPU v7x, 32 devices: a whole 2x2x4 slice. The times are simulated.
32 devices in a mesh: ctx: 8 (over y, x, core), wa: 4 (over z).
Axes of the slice: x: 2, y: 2, z: 4, core: 2. Of those that a mesh axis runs over, the one named last changes fastest.
Arguments:
- tokens: bfloat16 [4, 3072, 768], P('wa', 'ctx'), may hold values from -6 to 6
- cotangent: bfloat16 [4, 3072, 768], P('wa', 'ctx'), may hold values from -6 to 6
- segment_ids: int32 [4, 3072], P('wa', 'ctx'), may hold values from 0 to 3, never falling along the last dimension, each value on 1 to 1536 neighbouring positions
- token_types: int32 [4, 3072], P('wa', 'ctx'), may hold values 0 or 1
- query_wordword: bfloat16 [768, 768], P('wa'), may hold values from -0.21875 to 0.21875
- query_wordentity: bfloat16 [768, 768], P('wa'), may hold values from -0.21875 to 0.21875
- query_entityword: bfloat16 [768, 768], P('wa'), may hold values from -0.21875 to 0.21875
- query_entityentity: bfloat16 [768, 768], P('wa'), may hold values from -0.21875 to 0.21875
- bias_wordword: bfloat16 [768], P('wa'), may hold values from -3 to 3
- bias_wordentity: bfloat16 [768], P('wa'), may hold values from -3 to 3
- bias_entityword: bfloat16 [768], P('wa'), may hold values from -3 to 3
- bias_entityentity: bfloat16 [768], P('wa'), may hold values from -3 to 3
- key_weight: bfloat16 [768, 768], P('wa'), may hold values from -0.21875 to 0.21875
- value_weight: bfloat16 [768, 768], P('wa'), may hold values from -0.21875 to 0.21875
- value_bias: bfloat16 [768], P('wa'), may hold values from -0.4375 to 0.4375
- output_weight: bfloat16 [768, 768], P('wa'), may hold values from -4 to 4
- output_bias: bfloat16 [768], P('wa'), may hold values from -3 to 3
- first_gain: bfloat16 [768], P('wa'), may hold values from 0.5 to 1.5
- first_bias: bfloat16 [768], P('wa'), may hold values from -3 to 3
- inner_weight: bfloat16 [768, 3072], P('wa'), may hold values from -0.21875 to 0.21875
- inner_bias: bfloat16 [3072], P('wa'), may hold values from -3 to 3
- outer_weight: bfloat16 [3072, 768], P('wa'), may hold values from -0.109375 to 0.109375
- outer_bias: bfloat16 [768], P('wa'), may hold values from -3 to 3
- second_gain: bfloat16 [768], P('wa'), may hold values from 0.5 to 1.5
- second_bias: bfloat16 [768], P('wa'), may hold values from -3 to 3
Outputs:
- outputs: bfloat16 [4, 3072, 768], P('wa', 'ctx')
- token_grads: float32 [4, 3072, 768], P('wa', 'ctx')
- grad_query_wordword: float32 [768, 768], P('wa')
- grad_query_wordentity: float32 [768, 768], P('wa')
- grad_query_entityword: float32 [768, 768], P('wa')
- grad_query_entityentity: float32 [768, 768], P('wa')
- grad_bias_wordword: float32 [768], P('wa')
- grad_bias_wordentity: float32 [768], P('wa')
- grad_bias_entityword: float32 [768], P('wa')
- grad_bias_entityentity: float32 [768], P('wa')
- grad_key_weight: float32 [768, 768], P('wa')
- grad_value_weight: float32 [768, 768], P('wa')
- grad_value_bias: float32 [768], P('wa')
- grad_output_weight: float32 [768, 768], P('wa')
- grad_output_bias: float32 [768], P('wa')
- grad_first_gain: float32 [768], P('wa')
- grad_first_bias: float32 [768], P('wa')
- grad_inner_weight: float32 [768, 3072], P('wa')
- grad_inner_bias: float32 [3072], P('wa')
- grad_outer_weight: float32 [3072, 768], P('wa')
- grad_outer_bias: float32 [768], P('wa')
- grad_second_gain: float32 [768], P('wa')
- grad_second_bias: float32 [768], P('wa')
Inputs may be any that keep to these rules, and one draw needn't show every extreme that they name: `segment_ids`: within each sequence the numbers never fall; a document holds 1 to 1536 tokens, and one document of each sequence holds exactly 1536.
All inputs are finite; a program needn't handle non-finite values. No bound on the sum of `token_types` on one device may be relied on, other than what follows from the above.
Results may differ from a plain program's by a relative error of at most 0.019.
Values may be sent and summed in bfloat16 or wider, within the bound.
No kernel may reach another device: no remote copies, remote signals or barrier semaphores. Data moves between devices by JAX's collectives and lax.ppermute only.
A program may use at most 192 MiB of HBM per device.

v0:
```python
import jax
import jax.numpy as jnp
from jax import lax
from jax.sharding import PartitionSpec as P

HD = 64


EPSILON = 1e-12
MASKED = -1e30


def as_sent(shard):
    return jax.tree.map(lambda a: a.astype(jnp.bfloat16) if a.dtype == jnp.float32 else a, shard)


def passed_along(value, axis, steps):
    count = lax.axis_size(axis)
    leading, last = (max(0, -steps), min(count, count - steps))
    return lax.ppermute(value, axis, [(source, source + steps) for source in range(leading, last)])


def layer_norm(values, gain, shift):
    center = values - jnp.mean(values, axis=-1, keepdims=True)
    spread = jnp.mean(center * center, axis=-1, keepdims=True)
    return center * lax.rsqrt(spread + EPSILON) * gain + shift


def gelu_exact(values):
    return jax.nn.gelu(values, approximate=False)


def matmul(left, right):
    return jnp.dot(left, right, preferred_element_type=jnp.float32)


def left_product(left, right):
    return lax.dot_general(
        left, right, (((0,), (0,)), ((), ())), preferred_element_type=jnp.float32
    )


def right_product(left, right):
    return lax.dot_general(
        left, right, (((1,), (1,)), ((), ())), preferred_element_type=jnp.float32
    )


def column_sums(values):
    return jnp.sum(values.astype(jnp.float32), axis=0)


def columns(values, start):
    return lax.dynamic_slice_in_dim(values, start, HD, 1)


def head_scores(query_word, query_entity, keys_head, key_entity, allowed, scale):
    word_scores = right_product(query_word, keys_head)
    entity_scores = right_product(query_entity, keys_head)
    raw = jnp.where(key_entity[None, :], entity_scores, word_scores) * scale
    return jnp.where(allowed, raw, MASKED)


def merge_heads(stacked):
    return jnp.transpose(stacked, (1, 0, 2)).reshape(
        stacked.shape[1], stacked.shape[0] * stacked.shape[2]
    )


def per_device(
    tokens,
    cotangent,
    segment_ids,
    token_types,
    query_wordword,
    query_wordentity,
    query_entityword,
    query_entityentity,
    bias_wordword,
    bias_wordentity,
    bias_entityword,
    bias_entityentity,
    key_weight,
    value_weight,
    value_bias,
    output_weight,
    output_bias,
    first_gain,
    first_bias,
    inner_weight,
    inner_bias,
    outer_weight,
    outer_bias,
    second_gain,
    second_bias,
):
    attention = (
        lax.all_gather(query_wordword, "wa", axis=0, tiled=True),
        lax.all_gather(query_wordentity, "wa", axis=0, tiled=True),
        lax.all_gather(query_entityword, "wa", axis=0, tiled=True),
        lax.all_gather(query_entityentity, "wa", axis=0, tiled=True),
        lax.all_gather(bias_wordword, "wa", axis=0, tiled=True),
        lax.all_gather(bias_wordentity, "wa", axis=0, tiled=True),
        lax.all_gather(bias_entityword, "wa", axis=0, tiled=True),
        lax.all_gather(bias_entityentity, "wa", axis=0, tiled=True),
        lax.all_gather(key_weight, "wa", axis=0, tiled=True),
        lax.all_gather(value_weight, "wa", axis=0, tiled=True),
        lax.all_gather(value_bias, "wa", axis=0, tiled=True),
        lax.all_gather(output_weight, "wa", axis=0, tiled=True),
        lax.all_gather(output_bias, "wa", axis=0, tiled=True),
        lax.all_gather(first_gain, "wa", axis=0, tiled=True),
        lax.all_gather(first_bias, "wa", axis=0, tiled=True),
    )
    (
        full_ww,
        full_we,
        full_ew,
        full_ee,
        shift_ww,
        shift_we,
        shift_ew,
        shift_ee,
        full_key,
        full_value,
        shift_value,
        full_output,
        shift_output,
        gain_one,
        shift_one,
    ) = attention
    feedforward = (
        lax.all_gather(inner_weight, "wa", axis=0, tiled=True),
        lax.all_gather(inner_bias, "wa", axis=0, tiled=True),
        lax.all_gather(outer_weight, "wa", axis=0, tiled=True),
        lax.all_gather(outer_bias, "wa", axis=0, tiled=True),
        lax.all_gather(second_gain, "wa", axis=0, tiled=True),
        lax.all_gather(second_bias, "wa", axis=0, tiled=True),
    )
    full_inner, shift_inner, full_outer, shift_outer, gain_two, shift_two = feedforward
    inputs = tokens[0]
    seg = segment_ids[0]
    types = token_types[0]
    tok = inputs.shape[0]
    dmod = inputs.shape[1]
    heads = dmod // HD
    scale = HD ** (-0.5)
    length = tok * lax.axis_size("ctx")
    doc_max = min(2048, 4 * tok, length // 2)
    reach = (doc_max - 2) // tok + 1
    entity = (types == 1)[:, None]
    proj_ww = matmul(inputs, full_ww) + shift_ww
    proj_we = matmul(inputs, full_we) + shift_we
    proj_ew = matmul(inputs, full_ew) + shift_ew
    proj_ee = matmul(inputs, full_ee) + shift_ee
    query_word = jnp.where(entity, proj_ew, proj_ww).astype(jnp.bfloat16)
    query_entity = jnp.where(entity, proj_ee, proj_we).astype(jnp.bfloat16)
    keys = matmul(inputs, full_key).astype(jnp.bfloat16)
    values = (matmul(inputs, full_value) + shift_value).astype(jnp.bfloat16)
    own_kv = jnp.concatenate([keys, values], axis=1)
    own_seg = seg + 1
    tags = own_seg * 2 + types

    def pass_left(packet, unused):
        moved = jax.tree.map(
            lambda part, own: part.astype(own.dtype),
            passed_along(as_sent(packet), "ctx", 1),
            packet,
        )
        return (moved, moved)

    def pass_right(packet, unused):
        moved = jax.tree.map(
            lambda part, own: part.astype(own.dtype),
            passed_along(as_sent(packet), "ctx", -1),
            packet,
        )
        return (moved, moved)

    _, (left_kv, left_tags) = lax.scan(pass_left, (own_kv, tags), None, length=reach)
    _, (right_kv, right_tags) = lax.scan(pass_right, (own_kv, tags), None, length=reach)
    window = jnp.concatenate(
        [jnp.flip(left_kv, 0).reshape(-1, 2 * dmod), own_kv, right_kv.reshape(-1, 2 * dmod)], axis=0
    )
    window_tags = jnp.concatenate(
        [jnp.flip(left_tags, 0).reshape(-1), tags, right_tags.reshape(-1)], axis=0
    )
    key_entity = window_tags % 2 == 1
    allowed = own_seg[:, None] == (window_tags // 2)[None, :]

    def head_forward(index):
        start = index * HD
        scores = head_scores(
            columns(query_word, start),
            columns(query_entity, start),
            columns(window, start),
            key_entity,
            allowed,
            scale,
        )
        top = jnp.max(scores, axis=1, keepdims=True)
        expo = jnp.exp(scores - top)
        total = jnp.sum(expo, axis=1, keepdims=True)
        probs = (expo / total).astype(jnp.bfloat16)
        return (matmul(probs, columns(window, dmod + start)), (top + jnp.log(total))[:, 0])

    head_context, lse = lax.map(head_forward, jnp.arange(heads))
    context = merge_heads(head_context).astype(jnp.bfloat16)
    branch = matmul(context, full_output) + shift_output
    first, pull_one = jax.vjp(
        layer_norm,
        inputs.astype(jnp.float32) + branch,
        gain_one.astype(jnp.float32),
        shift_one.astype(jnp.float32),
    )
    first_low = first.astype(jnp.bfloat16)
    inner = matmul(first_low, full_inner) + shift_inner
    activated, pull_gelu = jax.vjp(gelu_exact, inner)
    hidden = activated.astype(jnp.bfloat16)
    ffn = matmul(hidden, full_outer) + shift_outer
    result, pull_two = jax.vjp(
        layer_norm, first + ffn, gain_two.astype(jnp.float32), shift_two.astype(jnp.float32)
    )
    grad_sum_two, grad_gain_two, grad_shift_two = pull_two(cotangent[0].astype(jnp.float32))
    grad_ffn = grad_sum_two.astype(jnp.bfloat16)
    grad_outer = left_product(hidden, grad_ffn)
    grad_outer_shift = column_sums(grad_ffn)
    grad_inner = pull_gelu(right_product(grad_ffn, full_outer))[0].astype(jnp.bfloat16)
    grad_inner_full = left_product(first_low, grad_inner)
    grad_inner_shift = column_sums(grad_inner)
    grad_first = grad_sum_two + right_product(grad_inner, full_inner)
    grad_sum_one, grad_gain_one, grad_shift_one = pull_one(grad_first)
    grad_branch = grad_sum_one.astype(jnp.bfloat16)
    grad_output = left_product(context, grad_branch)
    grad_output_shift = column_sums(grad_branch)
    grad_context = right_product(grad_branch, full_output).astype(jnp.bfloat16)

    def head_backward(index):
        start = index * HD
        word_head = columns(query_word, start)
        entity_head = columns(query_entity, start)
        keys_head = columns(window, start)
        values_head = columns(window, dmod + start)
        context_head = columns(grad_context, start)
        scores = head_scores(word_head, entity_head, keys_head, key_entity, allowed, scale)
        probs = jnp.exp(scores - lse[index][:, None])
        grad_probs = right_product(context_head, values_head)
        delta = jnp.sum(probs * grad_probs, axis=1)
        grad_scores = (probs * (grad_probs - delta[:, None])).astype(jnp.bfloat16)
        zero = jnp.zeros_like(grad_scores)
        grad_word = jnp.where(key_entity[None, :], zero, grad_scores)
        grad_entity = jnp.where(key_entity[None, :], grad_scores, zero)
        grad_qword = matmul(grad_word, keys_head) * scale
        grad_qentity = matmul(grad_entity, keys_head) * scale
        grad_keys = (
            left_product(grad_word, word_head) + left_product(grad_entity, entity_head)
        ) * scale
        grad_values = left_product(probs.astype(jnp.bfloat16), context_head)
        return (grad_qword, grad_qentity, delta, grad_keys, grad_values)

    grad_qword, grad_qentity, delta, window_keys, window_values = lax.map(
        lambda index: head_backward(index), jnp.arange(heads)
    )
    parts_keys = merge_heads(window_keys).reshape(2 * reach + 1, tok, dmod)
    parts_values = merge_heads(window_values).reshape(2 * reach + 1, tok, dmod)

    def back_left(total, piece):
        return (
            (
                passed_along((total[0] + piece[0]).astype(jnp.bfloat16), "ctx", -1).astype(
                    jnp.float32
                ),
                passed_along((total[1] + piece[1]).astype(jnp.bfloat16), "ctx", -1).astype(
                    jnp.float32
                ),
            ),
            None,
        )

    def back_right(total, piece):
        return (
            (
                passed_along((total[0] + piece[0]).astype(jnp.bfloat16), "ctx", 1).astype(
                    jnp.float32
                ),
                passed_along((total[1] + piece[1]).astype(jnp.bfloat16), "ctx", 1).astype(
                    jnp.float32
                ),
            ),
            None,
        )

    empty = jnp.zeros((tok, dmod), jnp.float32)
    from_above, _ = lax.scan(back_left, (empty, empty), (parts_keys[:reach], parts_values[:reach]))
    from_below, _ = lax.scan(
        back_right,
        (empty, empty),
        (jnp.flip(parts_keys[reach + 1 :], 0), jnp.flip(parts_values[reach + 1 :], 0)),
    )
    own_keys = parts_keys[reach] + from_above[0] + from_below[0]
    own_values = parts_values[reach] + from_above[1] + from_below[1]
    grad_keys = own_keys.astype(jnp.bfloat16)
    grad_values = own_values.astype(jnp.bfloat16)
    grad_qword = merge_heads(grad_qword).astype(jnp.bfloat16)
    grad_qentity = merge_heads(grad_qentity).astype(jnp.bfloat16)
    zeros = jnp.zeros_like(grad_qword)
    grad_pww = jnp.where(entity, zeros, grad_qword)
    grad_pew = jnp.where(entity, grad_qword, zeros)
    grad_pwe = jnp.where(entity, zeros, grad_qentity)
    grad_pee = jnp.where(entity, grad_qentity, zeros)
    input_grads = grad_sum_one + right_product(grad_pww, full_ww) + right_product(grad_pwe, full_we)
    input_grads = input_grads + right_product(grad_pew, full_ew) + right_product(grad_pee, full_ee)
    input_grads = (
        input_grads + right_product(grad_keys, full_key) + right_product(grad_values, full_value)
    )
    local_grads = (
        left_product(inputs, grad_pww),
        left_product(inputs, grad_pwe),
        left_product(inputs, grad_pew),
        left_product(inputs, grad_pee),
        column_sums(grad_pww),
        column_sums(grad_pwe),
        column_sums(grad_pew),
        column_sums(grad_pee),
        left_product(inputs, grad_keys),
        left_product(inputs, grad_values),
        column_sums(grad_values),
        grad_output,
        grad_output_shift,
        grad_gain_one,
        grad_shift_one,
        grad_inner_full,
        grad_inner_shift,
        grad_outer,
        grad_outer_shift,
        grad_gain_two,
        grad_shift_two,
    )
    shards = (
        lax.psum_scatter(
            local_grads[0].astype(jnp.bfloat16), "wa", scatter_dimension=0, tiled=True
        ).astype(jnp.float32),
        lax.psum_scatter(
            local_grads[1].astype(jnp.bfloat16), "wa", scatter_dimension=0, tiled=True
        ).astype(jnp.float32),
        lax.psum_scatter(
            local_grads[2].astype(jnp.bfloat16), "wa", scatter_dimension=0, tiled=True
        ).astype(jnp.float32),
        lax.psum_scatter(
            local_grads[3].astype(jnp.bfloat16), "wa", scatter_dimension=0, tiled=True
        ).astype(jnp.float32),
        lax.psum_scatter(
            local_grads[4].astype(jnp.bfloat16), "wa", scatter_dimension=0, tiled=True
        ).astype(jnp.float32),
        lax.psum_scatter(
            local_grads[5].astype(jnp.bfloat16), "wa", scatter_dimension=0, tiled=True
        ).astype(jnp.float32),
        lax.psum_scatter(
            local_grads[6].astype(jnp.bfloat16), "wa", scatter_dimension=0, tiled=True
        ).astype(jnp.float32),
        lax.psum_scatter(
            local_grads[7].astype(jnp.bfloat16), "wa", scatter_dimension=0, tiled=True
        ).astype(jnp.float32),
        lax.psum_scatter(
            local_grads[8].astype(jnp.bfloat16), "wa", scatter_dimension=0, tiled=True
        ).astype(jnp.float32),
        lax.psum_scatter(
            local_grads[9].astype(jnp.bfloat16), "wa", scatter_dimension=0, tiled=True
        ).astype(jnp.float32),
        lax.psum_scatter(
            local_grads[10].astype(jnp.bfloat16), "wa", scatter_dimension=0, tiled=True
        ).astype(jnp.float32),
        lax.psum_scatter(
            local_grads[11].astype(jnp.bfloat16), "wa", scatter_dimension=0, tiled=True
        ).astype(jnp.float32),
        lax.psum_scatter(
            local_grads[12].astype(jnp.bfloat16), "wa", scatter_dimension=0, tiled=True
        ).astype(jnp.float32),
        lax.psum_scatter(
            local_grads[13].astype(jnp.bfloat16), "wa", scatter_dimension=0, tiled=True
        ).astype(jnp.float32),
        lax.psum_scatter(
            local_grads[14].astype(jnp.bfloat16), "wa", scatter_dimension=0, tiled=True
        ).astype(jnp.float32),
        lax.psum_scatter(
            local_grads[15].astype(jnp.bfloat16), "wa", scatter_dimension=0, tiled=True
        ).astype(jnp.float32),
        lax.psum_scatter(
            local_grads[16].astype(jnp.bfloat16), "wa", scatter_dimension=0, tiled=True
        ).astype(jnp.float32),
        lax.psum_scatter(
            local_grads[17].astype(jnp.bfloat16), "wa", scatter_dimension=0, tiled=True
        ).astype(jnp.float32),
        lax.psum_scatter(
            local_grads[18].astype(jnp.bfloat16), "wa", scatter_dimension=0, tiled=True
        ).astype(jnp.float32),
        lax.psum_scatter(
            local_grads[19].astype(jnp.bfloat16), "wa", scatter_dimension=0, tiled=True
        ).astype(jnp.float32),
        lax.psum_scatter(
            local_grads[20].astype(jnp.bfloat16), "wa", scatter_dimension=0, tiled=True
        ).astype(jnp.float32),
    )
    totals = lax.psum(
        (
            shards[0],
            shards[1],
            shards[2],
            shards[3],
            shards[4],
            shards[5],
            shards[6],
            shards[7],
            shards[8],
            shards[9],
            shards[10],
            shards[11],
            shards[12],
            shards[13],
            shards[14],
            shards[15],
            shards[16],
            shards[17],
            shards[18],
            shards[19],
            shards[20],
        ),
        "ctx",
    )
    return (
        result.astype(jnp.bfloat16)[None],
        input_grads[None],
        totals[0],
        totals[1],
        totals[2],
        totals[3],
        totals[4],
        totals[5],
        totals[6],
        totals[7],
        totals[8],
        totals[9],
        totals[10],
        totals[11],
        totals[12],
        totals[13],
        totals[14],
        totals[15],
        totals[16],
        totals[17],
        totals[18],
        totals[19],
        totals[20],
    )


def solution(mesh):
    in_specs = (
        P("wa", "ctx", None),
        P("wa", "ctx", None),
        P("wa", "ctx"),
        P("wa", "ctx"),
        P("wa", None),
        P("wa", None),
        P("wa", None),
        P("wa", None),
        P("wa"),
        P("wa"),
        P("wa"),
        P("wa"),
        P("wa", None),
        P("wa", None),
        P("wa"),
        P("wa", None),
        P("wa"),
        P("wa"),
        P("wa"),
        P("wa", None),
        P("wa"),
        P("wa", None),
        P("wa"),
        P("wa"),
        P("wa"),
    )
    out_specs = (
        P("wa", "ctx", None),
        P("wa", "ctx", None),
        P("wa", None),
        P("wa", None),
        P("wa", None),
        P("wa", None),
        P("wa"),
        P("wa"),
        P("wa"),
        P("wa"),
        P("wa", None),
        P("wa", None),
        P("wa"),
        P("wa", None),
        P("wa"),
        P("wa"),
        P("wa"),
        P("wa", None),
        P("wa"),
        P("wa", None),
        P("wa"),
        P("wa"),
        P("wa"),
    )
    return jax.shard_map(
        per_device, mesh=mesh, in_specs=in_specs, out_specs=out_specs, check_vma=False
    )
```

profile of v0, /device:TPU:9, one launch (start us, length us, event | category | flops | bytes accessed | tf_op | source)
XLA Modules:
  0.0 1736.8 jit_solution(9188000721755877949)
XLA Ops:
  19.0 13.2 all-reduce.25
  36.4 10.7 all-gather
  50.8 22.0 %all-gather.13.cloned.1.call-done = bf16[768,768]{1,0:T(8,128)(2,1)} async-done(((bf16[192,768]{1,0:T(8,128)(2,1)}), bf16[768,768]{1,0:T(8,128)(2,1)}) %all-gather.13.cloned.1.call-update) | async-done | bytes 1179664 | tf_op jit(solution)/shard_map/all_gather | solution.py:107
  79.1 84.4 %while.92 = (s32[]{:T(128)}, bf16[384,1536]{1,0:T(8,128)(2,1)}, s32[384]{0:T(512)S(1)}, bf16[4,384,1536]{2,1,0:T(8,128)(2,1)}, s32[4,384]{1,0:T(4,128)}, /*index=5*/s32[]{:T(128)}, s32[]{:T(128)}) while((s32[]{:T(128)}, bf16[384,1536]{1,0:T(8,128)(2,1)}, s32[384]{0:T(512)S(1)}, bf16[4,384,1536]{2,1,0:T(8,128)(2,1)}, s32[4,384]{1,0:T(4,128)}, ...), condition=%wide.region_1.2_spmd, body=%wide.region_0.1_spmd.sunk | while | flops 2 | bytes 9452717 | solution.py:179
  84.9 11.5 collective-permute-done.1
  106.2 11.5 collective-permute-done.1
  127.4 11.4 collective-permute-done.1
  149.6 10.5 collective-permute-done.1
  171.6 81.2 %while.93 = (s32[]{:T(128)}, bf16[384,1536]{1,0:T(8,128)(2,1)S(1)}, s32[384]{0:T(512)S(1)}, bf16[4,384,1536]{2,1,0:T(8,128)(2,1)}, s32[4,384]{1,0:T(4,128)}, /*index=5*/s32[]{:T(128)}, s32[]{:T(128)}) while((s32[]{:T(128)}, bf16[384,1536]{1,0:T(8,128)(2,1)S(1)}, s32[384]{0:T(512)S(1)}, bf16[4,384,1536]{2,1,0:T(8,128)(2,1)}, ...), condition=%wide.region_3.4_spmd, body=%wide.region_2.3_spmd.sunk | while | flops 2 | bytes 9452717 | solution.py:180
  175.4 14.3 collective-permute-done.3
  196.1 13.7 collective-permute-done.3
  216.2 13.7 collective-permute-done.3
  236.2 14.1 collective-permute-done.3
  254.9 9.9 pad_maximum_fusion
  273.6 171.7 %while.94 = (s32[]{:T(128)}, bf16[12,384,64]{1,2,0:T(8,128)(2,1)S(1)}, f32[12,384]{1,0:T(8,128)}, pred[3456]{0:T(1024)(128)(4,1)S(1)}, s32[12]{0:T(128)S(1)}, /*...) while((s32[]{:T(128)}, ...), condition=%wide.region_7.8_spmd.clone, body=%wide.region_4.7_spmd.clone.sunk | while | flops 522878592 | bytes 50767676 | solution.py:206
  448.4 15.9 multiply_convert_fusion.1
  487.3 350.2 %while.95 = (s32[]{:T(128)}, bf16[12,384,64]{1,2,0:T(8,128)(2,1)S(1)}, bf16[12,384,64]{1,2,0:T(8,128)(2,1)S(1)}, f32[12,3456,64]{1,2,0:T(8,128)}, f32[12,3456,64...) while((s32[]{:T(128)}, ...), condition=%wide.region_18.19_spmd.clone, body=%wide.region_16.18_spmd.clone.sunk | while | flops 1379352192 | bytes 80462256 | solution.py:260
  837.5 9.1 fusion.147
  855.1 8.8 fusion.146
  876.3 13.0 rev.17
  895.4 13.0 rev.18
  908.4 106.5 %while.96 = (s32[]{:T(128)}, f32[384,768]{1,0:T(8,128)}, f32[384,768]{1,0:T(8,128)}, f32[4,384,768]{1,0,2:T(4,128)}, f32[4,384,768]{1,0,2:T(4,128)}, /*index=5*/s32[]{:T(128)}, s32[]{:T(128)}) while((s32[]{:T(128)}, f32[384,768]{1,0:T(8,128)}, f32[384,768]{1,0:T(8,128)}, f32[4,384,768]{1,0,2:T(4,128)}, ...), condition=%wide.region_20.21_spmd.clone, body=%wide.region_19.20_spmd.clone.sunk | while | flops 2359299 | bytes 23593136 | solution.py:293
  1017.7 110.5 %while.97 = (s32[]{:T(128)}, f32[384,768]{1,0:T(8,128)S(1)}, f32[384,768]{1,0:T(8,128)}, f32[4,384,768]{1,0,2:T(4,128)}, f32[4,384,768]{1,0,2:T(4,128)}, /*index=5*/s32[]{:T(128)}, s32[]{:T(128)}) while((s32[]{:T(128)}, f32[384,768]{1,0:T(8,128)S(1)}, f32[384,768]{1,0:T(8,128)}, f32[4,384,768]{1,0,2:T(4,128)}, ...), condition=%wide.region_22.23_spmd.clone, body=%wide.region_21.22_spmd.clone.sunk | while | flops 2359299 | bytes 28311756 | solution.py:294
  1033.4 10.6 collective-permute-start.7
  1181.0 15.2 all-reduce.24
  1225.7 29.2 %reduce-scatter.30.cloned.1.call-done = bf16[192,768]{1,0:T(8,128)(2,1)} async-done(((bf16[768,768]{1,0:T(8,128)(2,1)}), bf16[192,768]{1,0:T(8,128)(2,1)}) %reduce-scatter.30.cloned.1.call-update) | async-done | bytes 294928
  1256.0 29.0 %reduce-scatter.32.cloned.1.call-done = bf16[192,768]{1,0:T(8,128)(2,1)} async-done(((bf16[768,768]{1,0:T(8,128)(2,1)}), bf16[192,768]{1,0:T(8,128)(2,1)}) %reduce-scatter.32.cloned.1.call-update) | async-done | bytes 294928
  1286.1 29.0 %reduce-scatter.34.cloned.1.call-done = bf16[192,768]{1,0:T(8,128)(2,1)} async-done(((bf16[768,768]{1,0:T(8,128)(2,1)}), bf16[192,768]{1,0:T(8,128)(2,1)}) %reduce-scatter.34.cloned.1.call-update) | async-done | bytes 294928
  1316.2 29.0 %reduce-scatter.22.cloned.1.call-done = bf16[192,768]{1,0:T(8,128)(2,1)} async-done(((bf16[768,768]{1,0:T(8,128)(2,1)}), bf16[192,768]{1,0:T(8,128)(2,1)}) %reduce-scatter.22.cloned.1.call-update) | async-done | bytes 294928 | tf_op jit(solution)/shard_map/reduce_scatter | solution.py:372
  1345.2 88.2 %reduce-scatter.24.cloned.1.call-done = bf16[192,3072]{1,0:T(8,128)(2,1)} async-done(((bf16[768,3072]{1,0:T(8,128)(2,1)}), bf16[192,3072]{1,0:T(8,128)(2,1)}) %reduce-scatter.24.cloned.1.call-update) | async-done | bytes 1179664 | tf_op jit(solution)/shard_map/reduce_scatter | solution.py:384
  1433.4 88.0 %reduce-scatter.26.cloned.1.call-done = bf16[768,768]{1,0:T(8,128)(2,1)} async-done(((bf16[3072,768]{1,0:T(8,128)(2,1)}), bf16[768,768]{1,0:T(8,128)(2,1)}) %reduce-scatter.26.cloned.1.call-update) | async-done | bytes 1179664 | tf_op jit(solution)/shard_map/reduce_scatter | solution.py:390
  1521.5 200.4 %all-reduce.27 = (f32[192,768]{0,1:T(8,128)}, f32[192,768]{0,1:T(8,128)}, f32[192,768]{0,1:T(8,128)}, f32[192,768]{0,1:T(8,128)}, f32[192]{0:T(256)}, /*index=5*...) all-reduce(bf16[192,768]{0,1:T(8,128)(2,1)S(1)} %copy.99, ...), channel_id=1, replica_groups=mesh['ctx'=8,'wa'=4] {'ctx'}, use_global_device_ids=true, to_apply=%region_24.25 | all-reduce | flops 2214720 | bytes 13294080 | tf_op jit(solution)/shard_map/psum | solution.py:403
  (909 shorter events, 942.1 us)
Async XLA Ops:
  7.2 41.7 %all-gather.11.cloned.1.call-start = ((), (), s32[]{:S(2)}) async-start(), calls=%async_computation.9 | async-start | bytes 1474560 | tf_op jit(solution)/shard_map/all_gather | solution.py:106
  7.9 64.9 %all-gather.13.cloned.1.call-start = ((), (), s32[]{:S(2)}) async-start(), calls=%async_computation.10 | async-start | bytes 1474560 | tf_op jit(solution)/shard_map/all_gather | solution.py:107
  8.7 256.2 %all-gather.21.cloned.1.call-start = ((), (), s32[]{:S(2)}) async-start(), calls=%async_computation.14 | async-start | bytes 1474560 | tf_op jit(solution)/shard_map/all_gather | solution.py:98
  9.4 258.2 %all-gather.17.cloned.1.call-start = ((), (), s32[]{:S(2)}) async-start(), calls=%async_computation.12 | async-start | bytes 1474560 | tf_op jit(solution)/shard_map/all_gather | solution.py:99
  10.0 259.6 %all-gather.19.cloned.1.call-start = ((), (), s32[]{:S(2)}) async-start(), calls=%async_computation.13 | async-start | bytes 1474560 | tf_op jit(solution)/shard_map/all_gather | solution.py:100
  10.6 261.0 %all-gather.15.cloned.1.call-start = ((), (), s32[]{:S(2)}) async-start(), calls=%async_computation.11 | async-start | bytes 1474560 | tf_op jit(solution)/shard_map/all_gather | solution.py:101
  11.3 434.1 %all-gather.23.cloned.1.call-start = ((), (), s32[]{:S(2)}) async-start(), calls=%async_computation.15 | async-start | bytes 1474560 | tf_op jit(solution)/shard_map/all_gather | solution.py:109
  12.1 436.3 %all-gather.25.cloned.1.call-start = ((), (), s32[]{:S(2)}) async-start(), calls=%async_computation.16 | async-start | bytes 5898240 | tf_op jit(solution)/shard_map/all_gather | solution.py:132
  12.8 451.4 %all-gather.27.cloned.1.call-start = ((), (), s32[]{:S(2)}) async-start(), calls=%async_computation.17 | async-start | bytes 5898240 | tf_op jit(solution)/shard_map/all_gather | solution.py:134
  13.5 1202.5 %reduce-scatter.36.cloned.1.call-start = ((), (), s32[]{:S(2)}) async-start(), calls=%async_computation.25 | async-start | bytes 1474560
  79.1 18.6 %collective-permute-start = (bf16[384,1536]{1,0:T(8,128)(2,1)}, bf16[384,1536]{1,0:T(8,128)(2,1)S(1)}, u32[]{:S(2)}, u32[]{:S(2)}) collective-permute-start(bf16[384,1536]{1,0:T(8,128)(2,1)} %get-tuple-element.1111), channel_id=1, source_target_pairs={{0,4},{4,8},{8,12},{12,16},{16,20},{20,24},{24,28},{1,5},{5,9},{9,... | collective-permute-start | bytes 3538952 | tf_op jit(solution)/shard_map/while/body/eval_jaxpr/ppermute | solution.py:20
  99.9 19.1 %collective-permute-start = (bf16[384,1536]{1,0:T(8,128)(2,1)}, bf16[384,1536]{1,0:T(8,128)(2,1)S(1)}, u32[]{:S(2)}, u32[]{:S(2)}) collective-permute-start(bf16[384,1536]{1,0:T(8,128)(2,1)} %get-tuple-element.1111), channel_id=1, source_target_pairs={{0,4},{4,8},{8,12},{12,16},{16,20},{20,24},{24,28},{1,5},{5,9},{9,... | collective-permute-start | bytes 3538952 | tf_op jit(solution)/shard_map/while/body/eval_jaxpr/ppermute | solution.py:20
  121.1 19.1 %collective-permute-start = (bf16[384,1536]{1,0:T(8,128)(2,1)}, bf16[384,1536]{1,0:T(8,128)(2,1)S(1)}, u32[]{:S(2)}, u32[]{:S(2)}) collective-permute-start(bf16[384,1536]{1,0:T(8,128)(2,1)} %get-tuple-element.1111), channel_id=1, source_target_pairs={{0,4},{4,8},{8,12},{12,16},{16,20},{20,24},{24,28},{1,5},{5,9},{9,... | collective-permute-start | bytes 3538952 | tf_op jit(solution)/shard_map/while/body/eval_jaxpr/ppermute | solution.py:20
  142.4 19.1 %collective-permute-start = (bf16[384,1536]{1,0:T(8,128)(2,1)}, bf16[384,1536]{1,0:T(8,128)(2,1)S(1)}, u32[]{:S(2)}, u32[]{:S(2)}) collective-permute-start(bf16[384,1536]{1,0:T(8,128)(2,1)} %get-tuple-element.1111), channel_id=1, source_target_pairs={{0,4},{4,8},{8,12},{12,16},{16,20},{20,24},{24,28},{1,5},{5,9},{9,... | collective-permute-start | bytes 3538952 | tf_op jit(solution)/shard_map/while/body/eval_jaxpr/ppermute | solution.py:20
  171.6 19.5 %collective-permute-start.2 = (bf16[384,1536]{1,0:T(8,128)(2,1)S(1)}, bf16[384,1536]{1,0:T(8,128)(2,1)S(1)}, u32[]{:S(2)}, u32[]{:S(2)}) collective-permute-start(bf16[384,1536]{1,0:T(8,128)(2,1)S(1)} %get-tuple-element.1090), channel_id=1, source_target_pairs={{4,0},{8,4},{12,8},{16,12},{20,16},{24,20},{28,24},{5,1},{9,5},{13... | collective-permute-start | bytes 3538952 | tf_op jit(solution)/shard_map/while/body/eval_jaxpr/ppermute | solution.py:20
  173.5 16.3 collective-permute-start.3
  192.3 18.8 %collective-permute-start.2 = (bf16[384,1536]{1,0:T(8,128)(2,1)S(1)}, bf16[384,1536]{1,0:T(8,128)(2,1)S(1)}, u32[]{:S(2)}, u32[]{:S(2)}) collective-permute-start(bf16[384,1536]{1,0:T(8,128)(2,1)S(1)} %get-tuple-element.1090), channel_id=1, source_target_pairs={{4,0},{8,4},{12,8},{16,12},{20,16},{24,20},{28,24},{5,1},{9,5},{13... | collective-permute-start | bytes 3538952 | tf_op jit(solution)/shard_map/while/body/eval_jaxpr/ppermute | solution.py:20
  194.2 15.6 collective-permute-start.3
  212.3 18.8 %collective-permute-start.2 = (bf16[384,1536]{1,0:T(8,128)(2,1)S(1)}, bf16[384,1536]{1,0:T(8,128)(2,1)S(1)}, u32[]{:S(2)}, u32[]{:S(2)}) collective-permute-start(bf16[384,1536]{1,0:T(8,128)(2,1)S(1)} %get-tuple-element.1090), channel_id=1, source_target_pairs={{4,0},{8,4},{12,8},{16,12},{20,16},{24,20},{28,24},{5,1},{9,5},{13... | collective-permute-start | bytes 3538952 | tf_op jit(solution)/shard_map/while/body/eval_jaxpr/ppermute | solution.py:20
  214.3 15.6 collective-permute-start.3
  232.4 19.2 %collective-permute-start.2 = (bf16[384,1536]{1,0:T(8,128)(2,1)S(1)}, bf16[384,1536]{1,0:T(8,128)(2,1)S(1)}, u32[]{:S(2)}, u32[]{:S(2)}) collective-permute-start(bf16[384,1536]{1,0:T(8,128)(2,1)S(1)} %get-tuple-element.1090), channel_id=1, source_target_pairs={{4,0},{8,4},{12,8},{16,12},{20,16},{24,20},{28,24},{5,1},{9,5},{13... | collective-permute-start | bytes 3538952 | tf_op jit(solution)/shard_map/while/body/eval_jaxpr/ppermute | solution.py:20
  234.3 16.0 collective-permute-start.3
  1023.7 20.4 %collective-permute-start.6 = (bf16[384,768]{1,0:T(8,128)(2,1)}, bf16[384,768]{1,0:T(8,128)(2,1)}, u32[]{:S(2)}, u32[]{:S(2)}) collective-permute-start(bf16[384,768]{1,0:T(8,128)(2,1)} %fusion.243), channel_id=1, source_target_pairs={{0,4},{4,8},{8,12},{12,16},{16,20},{20,24},{24,28},{1,5},{5,9},{9,... | collective-permute-start | bytes 1769480 | tf_op jit(solution)/shard_map/while/body/eval_jaxpr/ppermute | solution.py:20
  1033.4 17.4 %collective-permute-start.7 = (bf16[384,768]{1,0:T(8,128)(2,1)S(1)}, bf16[384,768]{1,0:T(8,128)(2,1)S(1)}, u32[]{:S(2)}, u32[]{:S(2)}) collective-permute-start(bf16[384,768]{1,0:T(8,128)(2,1)S(1)} %fusion.244), channel_id=1, source_target_pairs={{0,4},{4,8},{8,12},{12,16},{16,20},{20,24},{24,28},{1,5},{5,9},{9,... | collective-permute-start | bytes 1769480 | tf_op jit(solution)/shard_map/while/body/eval_jaxpr/ppermute | solution.py:20
  1134.7 82.6 %reduce-scatter.38.cloned.1.call-start = ((), (), s32[]{:S(2)}) async-start(), calls=%async_computation.26 | async-start | bytes 1474560
  1145.8 78.8 %reduce-scatter.28.cloned.1.call-start = ((), (), s32[]{:S(2)}) async-start(), calls=%async_computation.21 | async-start | bytes 1474560
  1150.3 104.6 %reduce-scatter.30.cloned.1.call-start = ((), (), s32[]{:S(2)}) async-start(), calls=%async_computation.22 | async-start | bytes 1474560
  1152.6 132.4 %reduce-scatter.32.cloned.1.call-start = ((), (), s32[]{:S(2)}) async-start(), calls=%async_computation.23 | async-start | bytes 1474560
  1154.9 160.1 %reduce-scatter.34.cloned.1.call-start = ((), (), s32[]{:S(2)}) async-start(), calls=%async_computation.24 | async-start | bytes 1474560
  1157.4 187.8 %reduce-scatter.22.cloned.1.call-start = ((), (), s32[]{:S(2)}) async-start(), calls=%async_computation.18 | async-start | bytes 1474560 | tf_op jit(solution)/shard_map/reduce_scatter | solution.py:372
  1159.3 274.1 %reduce-scatter.24.cloned.1.call-start = ((), (), s32[]{:S(2)}) async-start(), calls=%async_computation.19 | async-start | bytes 5898240 | tf_op jit(solution)/shard_map/reduce_scatter | solution.py:384
  1165.6 355.8 %reduce-scatter.26.cloned.1.call-start = ((), (), s32[]{:S(2)}) async-start(), calls=%async_computation.20 | async-start | bytes 5898240 | tf_op jit(solution)/shard_map/reduce_scatter | solution.py:390
  (174 other events, 4743.6 us)
Sparse Core Ops, SparseCore 0:
  9.6 32.0 all-gather.10
  43.3 29.5 all-gather.12
  74.4 29.5 all-gather.20
  105.4 29.5 all-gather.16
  136.5 29.5 all-gather.18
  167.5 29.5 all-gather.14
  198.6 29.5 all-gather.22
  229.8 86.6 all-gather.24
  318.1 87.8 all-gather.26
  1134.8 28.5 reduce-scatter.35
  1165.7 28.8 reduce-scatter.37
  1196.7 27.8 reduce-scatter.27
  1226.9 27.9 reduce-scatter.29
  1257.1 27.8 reduce-scatter.31
  1287.2 27.8 reduce-scatter.33
  1317.3 27.8 reduce-scatter.21
  1347.3 86.0 reduce-scatter.23
  1435.6 85.7 reduce-scatter.25
where the time goes:
time: 1750 us; the launch traced here: 1740 us
  waiting for transfers between devices  483 us (28%)
  matrix products  474 us (27%)
  local copies, waits for them, and re-layouts  297 us (17%)
  blocking collectives  240 us (14%)
  other arithmetic  92.1 us (5%)
  starting transfers between devices  91.2 us (5%)
  loops' own time  41.5 us (2%)
  between operations  18.4 us (1%)
    dot_general x69, matrix products, right_product(): lax.dot_general(left, right, (((1,), (1,)), ((), ())), preferred_element_...  262 us
    psum x1, blocking collectives, per_device(): lax.psum((shards[0], shards[1], shards[2], shards[3], shards[4], shards[5...  200 us
    ppermute x32, waiting for transfers between devices, passed_along(): lax.ppermute(value, axis, [(source, source + steps) for source in range(l...  157 us
    dot_general x45, matrix products, matmul(): return jnp.dot(left, right, preferred_element_type=jnp.float32)  147 us
    unnamed x24, waiting for transfers between devices  99 us
    ppermute x32, starting transfers between devices, passed_along(): lax.ppermute(value, axis, [(source, source + steps) for source in range(l...  90.2 us
    reduce_scatter x1, waiting for transfers between devices, per_device(): lax.psum_scatter(local_grads[15].astype(jnp.bfloat16), 'wa', scatter_dime...  88.2 us
    reduce_scatter x1, waiting for transfers between devices, per_device(): lax.psum_scatter(local_grads[17].astype(jnp.bfloat16), 'wa', scatter_dime...  88 us
  transfers between devices with their start and end apart: 50, of which 28 were waited for; matrix products, arithmetic and copies ran while one was open for 20% of the time, Pallas kernels for 0%

commit v1 on v0

--- a/solution.py
+++ b/solution.py
@@ -1,6 +1,8 @@
 import jax
 import jax.numpy as jnp
 from jax import lax
+from jax.experimental import pallas as pl
+from jax.experimental.pallas import tpu as pltpu
 from jax.sharding import PartitionSpec as P
 
 HD = 64
@@ -67,7 +69,7 @@
     )
 
 
-def per_device(
+def windowed_device(
     tokens,
     cotangent,
     segment_ids,
@@ -453,6 +455,511 @@
     )
 
 
+CHIPS = 4
+KEY_BLOCK = 256
+NEGATIVE = -1e30
+
+
+def lanes_product(left, right):
+    return lax.dot_general(
+        left, right, (((1,), (1,)), ((), ())), preferred_element_type=jnp.float32
+    )
+
+
+def swapped(value, step):
+    count = lax.axis_size("ctx")
+    return lax.ppermute(value, "ctx", [(i, i ^ step) for i in range(count)])
+
+
+def chip_pieces(value):
+    half = value.shape[0] // 2
+    along_x = swapped(value, 2)
+    along_y = swapped(value, 4)
+    across = jnp.concatenate([swapped(along_x[:half], 4), swapped(along_y[half:], 2)], axis=0)
+    return value, along_x, along_y, across
+
+
+def project_kernel(place, t0, t1, t2, t3, weight, bias, entity, q_ref, kv_ref):
+    tok = t0.shape[0]
+    wide = 4 * 3 * HD
+    for m, piece in enumerate((t0, t1, t2, t3)):
+        chip = jnp.bitwise_xor(place[0], m)
+        total = jnp.dot(piece[...], weight[...], preferred_element_type=jnp.float32) + bias[...]
+        is_entity = entity[chip] == 1.0
+        for h in range(3):
+            at = 4 * HD * h
+            word = total[:, at : at + 2 * HD]
+            other = total[:, at + 2 * HD : at + 4 * HD]
+            q = jnp.where(is_entity, other, word).astype(jnp.bfloat16)
+            q_ref[chip, :, 2 * HD * h : 2 * HD * (h + 1)] = q * jnp.bfloat16(HD**-0.5)
+        kv_ref[chip] = total[:, wide:].astype(jnp.bfloat16)
+
+
+def key_sources(place, own, other, entity, lanes):
+    for j in range(CHIPS):
+        for source, core in ((own, place[1]), (other, 1 - place[1])):
+            row = pl.multiple_of((2 * j + core) * own.shape[1], 128)
+            for h in range(3):
+                kv = source[j, :, 2 * HD * h : 2 * HD * (h + 1)]
+                flag = entity[pl.ds(row, own.shape[1]), :] == 1.0
+                low = lax.broadcasted_iota(jnp.int32, kv.shape, 1) < HD
+                turned = pltpu.roll(kv.astype(jnp.float32), HD, 1)
+                both = jnp.where(low, kv.astype(jnp.float32), turned)
+                keys = jnp.where(low == flag, 0.0, both)
+                yield row, h, kv, keys.astype(jnp.bfloat16)
+
+
+def attend_kernel(
+    place, first, last, q_ref, own, other, seg_col, seg_row, entity, out, turned_out, lse, keys, turned_values
+):
+    tok = q_ref.shape[1]
+    for row, h, kv, key in key_sources(place, own, other, entity, tok):
+        keys[h, pl.ds(row, tok), :] = key
+        turned_values[h, :, pl.ds(row, tok)] = kv.astype(jnp.float32).T[HD:].astype(jnp.bfloat16)
+
+    def queries(j, unused):
+        seg = seg_row[j]
+        for h in range(3):
+            q = q_ref[j, :, 2 * HD * h : 2 * HD * (h + 1)]
+
+            def step(t, carry):
+                top, total, acc = carry
+                at = pl.multiple_of(t * KEY_BLOCK, KEY_BLOCK)
+                scores = lanes_product(keys[h, pl.ds(at, KEY_BLOCK), :], q)
+                scores = jnp.where(seg_col[pl.ds(at, KEY_BLOCK), :] == seg, scores, NEGATIVE)
+                peak = jnp.maximum(top, jnp.max(scores, axis=0, keepdims=True))
+                fade = jnp.exp(top - peak)
+                expo = jnp.exp(scores - peak)
+                total = total * fade + jnp.sum(expo, axis=0, keepdims=True)
+                acc = acc * fade + jnp.dot(
+                    turned_values[h, :, pl.ds(at, KEY_BLOCK)],
+                    expo.astype(jnp.bfloat16),
+                    preferred_element_type=jnp.float32,
+                )
+                return peak, total, acc
+
+            start = (
+                jnp.full((1, tok), NEGATIVE, jnp.float32),
+                jnp.zeros((1, tok), jnp.float32),
+                jnp.zeros((HD, tok), jnp.float32),
+            )
+            top, total, acc = lax.fori_loop(first[j], last[j], step, start)
+            turned_out[j, HD * h : HD * (h + 1), :] = acc / total
+            lse[j, h] = top + jnp.log(total)
+        out[j] = turned_out[j].T.astype(jnp.bfloat16)
+        return 0
+
+    lax.fori_loop(0, CHIPS, queries, 0)
+
+
+def attend_back_kernel(
+    place,
+    first,
+    last,
+    q_ref,
+    own,
+    other,
+    seg_col,
+    seg_row,
+    entity,
+    entity_own,
+    turned_out,
+    lse,
+    grad,
+    dq_ref,
+    dkv_own,
+    dkv_other,
+    keys,
+    turned_keys,
+    values,
+    grad_keys,
+    grad_values,
+):
+    tok = q_ref.shape[1]
+    for row, h, kv, key in key_sources(place, own, other, entity, tok):
+        keys[h, pl.ds(row, tok), :] = key
+        turned_keys[h, :, pl.ds(row, tok)] = key.astype(jnp.float32).T.astype(jnp.bfloat16)
+        values[h, pl.ds(row, tok), :] = kv
+    grad_keys[...] = jnp.zeros_like(grad_keys)
+    grad_values[...] = jnp.zeros_like(grad_values)
+
+    def queries(j, unused):
+        seg = seg_row[j]
+        turned_grad = grad[j].astype(jnp.float32).T
+        slot = jnp.bitwise_xor(place[0], j)
+        is_entity = entity_own[j] == 1.0
+        for h in range(3):
+            q = q_ref[j, :, 2 * HD * h : 2 * HD * (h + 1)]
+            rows = slice(HD * h, HD * (h + 1))
+            delta = jnp.sum(turned_grad[rows] * turned_out[j, rows, :], axis=0, keepdims=True)
+            shift = lse[j, h]
+            own_grad = grad[j, :, rows]
+            padded = jnp.concatenate([jnp.zeros_like(own_grad), own_grad], axis=1)
+
+            def step(t, acc):
+                at = pl.multiple_of(t * KEY_BLOCK, KEY_BLOCK)
+                ds = pl.ds(at, KEY_BLOCK)
+                scores = lanes_product(keys[h, ds, :], q)
+                probs = jnp.where(seg_col[ds, :] == seg, jnp.exp(scores - shift), 0.0)
+                grad_probs = lanes_product(values[h, ds, :], padded)
+                grad_scores = (probs * (grad_probs - delta)).astype(jnp.bfloat16)
+                grad_values[h, ds, :] += jnp.dot(
+                    probs.astype(jnp.bfloat16), padded, preferred_element_type=jnp.float32
+                )
+                grad_keys[h, ds, :] += jnp.dot(grad_scores, q, preferred_element_type=jnp.float32)
+                return acc + jnp.dot(
+                    turned_keys[h, :, ds], grad_scores, preferred_element_type=jnp.float32
+                )
+
+            acc = lax.fori_loop(
+                first[j], last[j], step, jnp.zeros((2 * HD, tok), jnp.float32)
+            )
+            dq = acc.T * (HD**-0.5)
+            dq_ref[slot, :, 4 * HD * h : 4 * HD * h + 2 * HD] = jnp.where(
+                is_entity, 0.0, dq
+            ).astype(jnp.bfloat16)
+            dq_ref[slot, :, 4 * HD * h + 2 * HD : 4 * HD * (h + 1)] = jnp.where(
+                is_entity, dq, 0.0
+            ).astype(jnp.bfloat16)
+        return 0
+
+    lax.fori_loop(0, CHIPS, queries, 0)
+    for j in range(CHIPS):
+        slot = jnp.bitwise_xor(place[0], j)
+        for target, core in ((dkv_own, place[1]), (dkv_other, 1 - place[1])):
+            ds = pl.ds(pl.multiple_of((2 * j + core) * tok, 128), tok)
+            flag = entity[ds, :] == 1.0
+            for h in range(3):
+                both = grad_keys[h, ds, :]
+                low = lax.broadcasted_iota(jnp.int32, both.shape, 1) < HD
+                picked = jnp.where(flag, pltpu.roll(both, HD, 1), both)
+                target[slot, :, 2 * HD * h : 2 * HD * (h + 1)] = jnp.where(
+                    low, picked, grad_values[h, ds, :]
+                ).astype(jnp.bfloat16)
+
+
+def smem():
+    return pl.BlockSpec(memory_space=pltpu.SMEM)
+
+
+def vmem():
+    return pl.BlockSpec(memory_space=pltpu.VMEM)
+
+
+def whole_call(kernel, scalars, arrays, outs, scratch=(), flops=0, nbytes=0, exps=0):
+    return pl.pallas_call(
+        kernel,
+        out_shape=outs,
+        in_specs=[smem() for _ in scalars] + [vmem() for _ in arrays],
+        out_specs=jax.tree.map(lambda _: vmem(), outs),
+        scratch_shapes=list(scratch),
+        compiler_params=pltpu.CompilerParams(vmem_limit_bytes=56 << 20),
+        cost_estimate=pl.CostEstimate(flops=flops, bytes_accessed=nbytes, transcendentals=exps),
+    )(*scalars, *arrays)
+
+
+def shaped(shape, dtype):
+    return jax.ShapeDtypeStruct(shape, dtype)
+
+
+def grouped_device(
+    tokens,
+    cotangent,
+    segment_ids,
+    token_types,
+    query_wordword,
+    query_wordentity,
+    query_entityword,
+    query_entityentity,
+    bias_wordword,
+    bias_wordentity,
+    bias_entityword,
+    bias_entityentity,
+    key_weight,
+    value_weight,
+    value_bias,
+    output_weight,
+    output_bias,
+    first_gain,
+    first_bias,
+    inner_weight,
+    inner_bias,
+    outer_weight,
+    outer_bias,
+    second_gain,
+    second_bias,
+):
+    bf16, f32 = jnp.bfloat16, jnp.float32
+    place = lax.axis_index("ctx")
+    chip, core = place // 2, place % 2
+    wa = lax.axis_index("wa")
+    parts = lax.axis_size("wa")
+    inputs = tokens[0]
+    tok, dmod = inputs.shape
+    rows = key_weight.shape[0]
+    half = rows // 2
+    group = dmod // CHIPS
+    hidden_all = inner_weight.shape[1]
+    ff_slot = hidden_all // (2 * CHIPS)
+    where = jnp.stack([chip, core]).astype(jnp.int32)
+
+    tags = lax.all_gather(segment_ids[0] * 2 + token_types[0], "ctx", axis=0, tiled=True)
+    length = tags.shape[0]
+    seg, types = tags // 2, tags % 2
+    vectors = (
+        bias_wordword,
+        bias_wordentity,
+        bias_entityword,
+        bias_entityentity,
+        value_bias,
+        output_bias,
+        first_gain,
+        first_bias,
+        outer_bias,
+        second_gain,
+        second_bias,
+    )
+    packed = jnp.concatenate([v for v in vectors] + [inner_bias]).reshape(-1, rows)
+    packed = jnp.pad(packed, ((0, 16 - packed.shape[0]), (0, 256 - rows)))
+    packed = lax.all_gather(packed, "wa", axis=0, tiled=False)[:, :, :rows]
+    head_bias = lax.dynamic_index_in_dim(packed, chip, 0, keepdims=False)[:5].astype(f32)
+    full = jnp.transpose(packed, (1, 0, 2)).astype(f32)
+    shift_output, gain_one, shift_one, shift_outer, gain_two, shift_two = (
+        full[k].reshape(1, dmod) for k in range(5, 11)
+    )
+    shift_inner = packed[:, 11:15].astype(f32).reshape(1, hidden_all)
+
+    six = (query_wordword, query_wordentity, query_entityword, query_entityentity, key_weight, value_weight)
+    mine = [lax.dynamic_slice(w, (half * core, group * chip), (half, group)).reshape(half, 3, HD) for w in six]
+    mine = jnp.concatenate(
+        [jnp.stack(mine[:4], axis=2).reshape(half, 4 * group), jnp.stack(mine[4:], axis=2).reshape(half, 2 * group)],
+        axis=1,
+    )
+    mine = lax.all_gather(mine, "wa", axis=0, tiled=False)
+    theirs = swapped(mine, 1)
+    weight = jnp.where(
+        core == 0, jnp.stack([mine, theirs], axis=1), jnp.stack([theirs, mine], axis=1)
+    ).reshape(dmod, 6 * group)
+    bias = jnp.concatenate(
+        [
+            jnp.stack([b.reshape(3, HD) for b in head_bias[:4]], axis=1).reshape(1, 4 * group),
+            jnp.stack([jnp.zeros((3, HD), f32), head_bias[4].reshape(3, HD)], axis=1).reshape(1, 2 * group),
+        ],
+        axis=1,
+    )
+
+    pieces = chip_pieces(inputs)
+
+    slot = jnp.concatenate(
+        [
+            lax.dynamic_slice(inner_weight, (0, ff_slot * place), (rows, ff_slot)),
+            lax.dynamic_slice(outer_weight, (half * place, 0), (half, ff_slot)),
+            lax.dynamic_slice(outer_weight, (half * place, ff_slot), (half, ff_slot)),
+            lax.dynamic_slice(output_weight, (rows // CHIPS * chip, ff_slot * core), (rows // CHIPS, ff_slot)),
+        ],
+        axis=0,
+    )
+    slot_rows = slot.shape[0]
+    slots = jnp.stack(chip_pieces(lax.all_gather(slot, "wa", axis=0, tiled=False)))
+    order = jnp.bitwise_xor(chip, jnp.arange(CHIPS))
+    slots_other = swapped(slots, 1)
+    slots = jnp.where(core == 0, jnp.stack([slots, slots_other], 1), jnp.stack([slots_other, slots], 1))
+    slots = jnp.take(slots, order, axis=0)
+    full_inner = jnp.transpose(slots[:, :, :, :rows], (2, 3, 0, 1, 4)).reshape(dmod, hidden_all)
+    full_outer = slots[:, :, :, rows : 2 * rows].reshape(CHIPS, 2, parts, 2, half, ff_slot)
+    full_outer = jnp.transpose(full_outer, (2, 0, 1, 4, 3, 5)).reshape(hidden_all, dmod)
+    full_output = jnp.transpose(slots[:, :, :, 2 * rows :], (2, 0, 3, 1, 4)).reshape(dmod, dmod)
+
+    grouped = types.reshape(CHIPS, 2, tok)
+    entity_own = lax.dynamic_index_in_dim(grouped, core, 1, keepdims=False).astype(f32)[:, :, None]
+    q, kv = whole_call(
+        project_kernel,
+        [where],
+        [*pieces, weight, bias, entity_own],
+        [shaped((CHIPS, tok, 2 * group), bf16), shaped((CHIPS, tok, 2 * group), bf16)],
+        flops=2 * CHIPS * tok * dmod * 6 * group,
+        nbytes=8 << 20,
+    )
+    kv_other = swapped(kv, 1)
+
+    seg_col = seg[:, None]
+    ent_col = types.astype(f32)[:, None]
+    seg_shards = seg.reshape(CHIPS, 2, tok)
+    seg_row = lax.dynamic_index_in_dim(seg_shards, core, 1, keepdims=False)
+    starts = jnp.sum(seg[None, :] < seg_row[:, :1], axis=1)
+    ends = jnp.sum(seg[None, :] <= seg_row[:, -1:], axis=1)
+    first = (starts // KEY_BLOCK).astype(jnp.int32)
+    last = ((ends + KEY_BLOCK - 1) // KEY_BLOCK).astype(jnp.int32)
+    seg_row = seg_row[:, None, :]
+    context, turned, lse = whole_call(
+        attend_kernel,
+        [where, first, last],
+        [q, kv, kv_other, seg_col, seg_row, ent_col],
+        [
+            shaped((CHIPS, tok, group), bf16),
+            shaped((CHIPS, group, tok), f32),
+            shaped((CHIPS, 3, 1, tok), f32),
+        ],
+        [pltpu.VMEM((3, length, 2 * HD), bf16), pltpu.VMEM((3, HD, length), bf16)],
+        flops=4 * CHIPS * tok * length * group,
+        nbytes=8 << 20,
+        exps=CHIPS * tok * length * 3 // 2,
+    )
+    same_core = [[2 * i + k for i in range(CHIPS)] for k in range(2)]
+
+    def exchanged(value):
+        return lax.all_to_all(
+            value, "ctx", split_axis=0, concat_axis=0, tiled=True, axis_index_groups=same_core
+        )
+
+    context = jnp.transpose(exchanged(context), (1, 0, 2)).reshape(tok, dmod)
+
+    branch = matmul(context, full_output) + shift_output
+    first_norm, pull_one = jax.vjp(layer_norm, inputs.astype(f32) + branch, gain_one[0], shift_one[0])
+    first_low = first_norm.astype(bf16)
+    inner = matmul(first_low, full_inner) + shift_inner
+    activated, pull_gelu = jax.vjp(gelu_exact, inner)
+    hidden = activated.astype(bf16)
+    ffn = matmul(hidden, full_outer) + shift_outer
+    result, pull_two = jax.vjp(layer_norm, first_norm + ffn, gain_two[0], shift_two[0])
+    grad_sum_two, grad_gain_two, grad_shift_two = pull_two(cotangent[0].astype(f32))
+    grad_ffn = grad_sum_two.astype(bf16)
+    grad_outer = left_product(hidden, grad_ffn)
+    grad_inner = pull_gelu(right_product(grad_ffn, full_outer))[0].astype(bf16)
+    grad_inner_full = left_product(first_low, grad_inner)
+    grad_first = grad_sum_two + right_product(grad_inner, full_inner)
+    grad_sum_one, grad_gain_one, grad_shift_one = pull_one(grad_first)
+    grad_branch = grad_sum_one.astype(bf16)
+    grad_output = left_product(context, grad_branch)
+    grad_context = right_product(grad_branch, full_output).astype(bf16)
+    grad_context = jnp.transpose(grad_context.reshape(tok, CHIPS, group), (1, 0, 2))
+    grad_context = exchanged(grad_context)
+
+    grads = jnp.concatenate(
+        [
+            jnp.transpose(
+                grad_inner_full.astype(bf16).reshape(parts, rows, CHIPS, 2, ff_slot), (2, 3, 0, 1, 4)
+            ),
+            jnp.transpose(
+                grad_outer.astype(bf16).reshape(parts, CHIPS, 2, half, 2, ff_slot), (1, 2, 0, 4, 3, 5)
+            ).reshape(CHIPS, 2, parts, rows, ff_slot),
+            jnp.transpose(
+                grad_output.astype(bf16).reshape(parts, CHIPS, rows // CHIPS, 2, ff_slot), (1, 3, 0, 2, 4)
+            ),
+        ],
+        axis=3,
+    )
+    grads = jnp.take(grads, order, axis=0)
+    kept = lax.dynamic_index_in_dim(grads, core, 1, keepdims=False)
+    sent = lax.dynamic_index_in_dim(grads, 1 - core, 1, keepdims=False)
+    kept = kept.astype(f32) + swapped(sent, 1).astype(f32)
+
+    def chips_summed(value):
+        middle = value.shape[1] // 2
+        low = value.astype(bf16)
+        from_x = swapped(low[3, :middle], 2).astype(f32)
+        from_y = swapped(low[3, middle:], 4).astype(f32)
+        to_x = jnp.concatenate([value[1, :middle], value[1, middle:] + from_y], axis=0)
+        to_y = jnp.concatenate([value[2, :middle] + from_x, value[2, middle:]], axis=0)
+        return value[0] + swapped(to_x.astype(bf16), 2).astype(f32) + swapped(to_y.astype(bf16), 4).astype(f32)
+
+    summed = chips_summed(kept).astype(bf16)
+    summed = lax.psum_scatter(summed, "wa", scatter_dimension=0, tiled=True)[0]
+
+    def plane_gathered(value):
+        stacked = jnp.stack(chip_pieces(value))
+        others = swapped(stacked, 1)
+        both = jnp.where(core == 0, jnp.stack([stacked, others], 1), jnp.stack([others, stacked], 1))
+        return jnp.take(both, order, axis=0)
+
+    shared = plane_gathered(summed).astype(f32)
+    out_inner = jnp.transpose(shared[:, :, :rows], (2, 0, 1, 3)).reshape(rows, hidden_all)
+    out_outer = jnp.transpose(
+        shared[:, :, rows : 2 * rows].reshape(CHIPS, 2, 2, half, ff_slot), (0, 1, 3, 2, 4)
+    ).reshape(outer_weight.shape)
+    out_output = jnp.transpose(shared[:, :, 2 * rows :], (0, 2, 1, 3)).reshape(rows, dmod)
+
+    dq, dkv, dkv_other = whole_call(
+        attend_back_kernel,
+        [where, first, last],
+        [q, kv, kv_other, seg_col, seg_row, ent_col, entity_own, turned, lse, grad_context],
+        [
+            shaped((CHIPS, tok, 4 * group), bf16),
+            shaped((CHIPS, tok, 2 * group), bf16),
+            shaped((CHIPS, tok, 2 * group), bf16),
+        ],
+        [
+            pltpu.VMEM((3, length, 2 * HD), bf16),
+            pltpu.VMEM((3, 2 * HD, length), bf16),
+            pltpu.VMEM((3, length, 2 * HD), bf16),
+            pltpu.VMEM((3, length, 2 * HD), f32),
+            pltpu.VMEM((3, length, 2 * HD), f32),
+        ],
+        flops=10 * CHIPS * tok * length * group,
+        nbytes=16 << 20,
+        exps=CHIPS * tok * length * 3 // 2,
+    )
+    dkv = (dkv.astype(f32) + swapped(dkv_other, 1).astype(f32)).astype(bf16)
+    dq = dq.reshape(CHIPS * tok, 4 * group)
+    dkv = dkv.reshape(CHIPS * tok, 2 * group)
+    partial = right_product(dq, weight[:, : 4 * group]) + right_product(dkv, weight[:, 4 * group :])
+    input_grads = grad_sum_one + chips_summed(partial.reshape(CHIPS, tok, dmod))
+
+    all_tokens = jnp.concatenate(pieces, axis=0)
+    head_grads = jnp.concatenate([left_product(all_tokens, dq), left_product(all_tokens, dkv)], axis=1)
+    head_grads = head_grads.reshape(parts, 2, half, 6 * group)
+    kept = lax.dynamic_index_in_dim(head_grads, core, 1, keepdims=False)
+    sent = lax.dynamic_index_in_dim(head_grads, 1 - core, 1, keepdims=False).astype(bf16)
+    kept = (kept + swapped(sent, 1).astype(f32)).astype(bf16)
+    kept = lax.psum_scatter(kept, "wa", scatter_dimension=0, tiled=True)[0]
+    shared = plane_gathered(kept).astype(f32)
+    shared = jnp.transpose(shared, (1, 2, 0, 3)).reshape(rows, CHIPS, 6 * group)
+    for_q = shared[:, :, : 4 * group].reshape(rows, CHIPS, 3, 4, HD)
+    for_kv = shared[:, :, 4 * group :].reshape(rows, CHIPS, 3, 2, HD)
+    out_q = [for_q[:, :, :, k].reshape(rows, dmod) for k in range(4)]
+    out_kv = [for_kv[:, :, :, k].reshape(rows, dmod) for k in range(2)]
+
+    head_sums = jnp.concatenate([column_sums(dq), column_sums(dkv)])
+    head_sums = jnp.where(jnp.arange(CHIPS)[:, None] == chip, head_sums[None], 0.0)
+    head_sums = lax.psum(head_sums, ("ctx", "wa"))
+    head_sums = lax.dynamic_index_in_dim(head_sums, wa, 0, keepdims=False)
+    sum_q = head_sums[: 4 * group].reshape(3, 4, HD)
+    sum_kv = head_sums[4 * group :].reshape(3, 2, HD)
+    small = jnp.stack(
+        [
+            column_sums(grad_branch),
+            grad_gain_one,
+            grad_shift_one,
+            column_sums(grad_ffn),
+            grad_gain_two,
+            grad_shift_two,
+        ]
+    )
+    small = jnp.concatenate([small, column_sums(grad_inner).reshape(parts, dmod)])
+    small = lax.psum(small, ("ctx", "wa"))
+    mine_small = lax.dynamic_slice(small, (0, wa * rows), (6, rows))
+    out_inner_bias = lax.dynamic_index_in_dim(small[6:], wa, 0, keepdims=False)
+
+    return (
+        result.astype(bf16)[None],
+        input_grads[None],
+        *out_q,
+        *(sum_q[:, k].reshape(rows) for k in range(4)),
+        *out_kv,
+        sum_kv[:, 1].reshape(rows),
+        out_output,
+        mine_small[0],
+        mine_small[1],
+        mine_small[2],
+        out_inner,
+        out_inner_bias,
+        out_outer,
+        mine_small[3],
+        mine_small[4],
+        mine_small[5],
+    )
+
+
 def solution(mesh):
     in_specs = (
         P("wa", "ctx", None),
@@ -506,6 +1013,7 @@
         P("wa"),
         P("wa"),
     )
+    body = grouped_device if mesh.shape["ctx"] == 2 * CHIPS else windowed_device
     return jax.shard_map(
-        per_device, mesh=mesh, in_specs=in_specs, out_specs=out_specs, check_vma=False
-    )
+        body, mesh=mesh, in_specs=in_specs, out_specs=out_specs, check_vma=False
+    )

time: 1750 us -> 736 us (0.42)
  matrix products: 474 us -> 46.8 us
  waiting for transfers between devices: 483 us -> 134 us
  blocking collectives: 240 us -> 92.3 us
  Pallas kernels: 0 us -> 109 us
  local copies, waits for them, and re-layouts: 297 us -> 197 us
  starting transfers between devices: 91.2 us -> 36.6 us
  loops' own time: 41.5 us -> 0 us
    dot_general x69 -> x5, matrix products: 262 us -> 14 us  [right_product(): lax.dot_general(left, right, (((1,), (1,)), ((), ())), preferred_element_...]
    reduce_scatter x3 -> x2, waiting for transfers between devices: 205 us -> 0.01 us  [the longest x1 0.01 us: grouped_device(): kept = lax.psum_scatter(kept, 'wa', scatter_dimension=0, tiled=True)[0]]
    psum x1, blocking collectives: 200 us -> 41 us  [grouped_device(): head_sums = lax.psum(head_sums, ('ctx', 'wa'))]
    dot_general x45 -> x3, matrix products: 147 us -> 19.7 us  [matmul(): return jnp.dot(left, right, preferred_element_type=jnp.float32)]
    pallas_call x0 -> x3, Pallas kernels: none -> 109 us  [whole_call(): pl.pallas_call(kernel, out_shape=outs, in_specs=[smem() for _ in scalars]...]
    unnamed x24 -> x3, waiting for transfers between devices: 99 us -> 0.05 us
    dynamic_slice x68 -> x11, local copies, waits for them, and re-layouts: 103 us -> 8.36 us  [the longest x6 5.92 us: grouped_device(): lax.dynamic_slice(w, (half * core, group * chip), (half, group))]
    ppermute x32, starting transfers between devices: 90.2 us -> 32.8 us  [swapped(): return lax.ppermute(value, 'ctx', [(i, i ^ step) for i in range(count)])]
  transfers between devices with their start and end apart: 50 -> 36, of which waited for: 28 -> 16; matrix products, arithmetic and copies ran while one was open for 20% -> 24% of each run, Pallas kernels for 0% -> 15%
where the time goes in v1:
time: 736 us; the launch traced here: 722 us
  local copies, waits for them, and re-layouts  197 us (27%)
  waiting for transfers between devices  134 us (18%)
  Pallas kernels  109 us (15%)
  blocking collectives  92.3 us (13%)
  other arithmetic  91.6 us (12%)
  matrix products  46.8 us (6%)
  starting transfers between devices  36.6 us (5%)
  between operations  15.3 us (2%)
    pallas_call x3, Pallas kernels, whole_call(): pl.pallas_call(kernel, out_shape=outs, in_specs=[smem() for _ in scalars]...  109 us
    ppermute x32, waiting for transfers between devices, swapped(): return lax.ppermute(value, 'ctx', [(i, i ^ step) for i in range(count)])  101 us
    psum x1, blocking collectives, grouped_device(): head_sums = lax.psum(head_sums, ('ctx', 'wa'))  41 us
    all_gather x1, waiting for transfers between devices, grouped_device(): lax.all_gather(slot, 'wa', axis=0, tiled=False)  33.3 us
    ppermute x32, starting transfers between devices, swapped(): return lax.ppermute(value, 'ctx', [(i, i ^ step) for i in range(count)])  32.8 us
    unnamed x161, local copies, waits for them, and re-layouts  29.2 us
    dot_general x3, matrix products, matmul(): return jnp.dot(left, right, preferred_element_type=jnp.float32)  19.7 us
    gather x4, local copies, waits for them, and re-layouts, grouped_device(): slots = jnp.take(slots, order, axis=0)  18.5 us
  transfers between devices with their start and end apart: 36, of which 16 were waited for; matrix products, arithmetic and copies ran while one was open for 24% of the time, Pallas kernels for 15%

profile of v1, /device:TPU:9, one launch (start us, length us, event | category | flops | bytes accessed | tf_op | source)
XLA Modules:
  0.0 721.8 jit_solution(18435460815625240186)
XLA Ops:
  10.1 33.3 %all-gather.6.cloned.1.call-done = bf16[1728,384]{1,0:T(8,128)(2,1)} async-done(((bf16[432,384]{1,0:T(8,128)(2,1)}), bf16[1728,384]{1,0:T(8,128)(2,1)}) %all-gather.6.cloned.1.call-update) | async-done | bytes 1327120 | tf_op jit(solution)/shard_map/all_gather | solution.py:763
  45.8 27.6 %collective-permute-done.7 = bf16[4,432,384]{2,1,0:T(8,128)(2,1)S(1)} collective-permute-done((bf16[4,432,384]{2,1,0:T(8,128)(2,1)}, bf16[4,432,384]{2,1,0:T(8,128)(2,1)S(1)}, u32[]{:S(2)}, u32[]{:S(2)}) %collective-permute-start.7) | collective-permute-done | bytes 1327136 | tf_op jit(solution)/shard_map/ppermute | solution.py:471
  76.1 12.1 %collective-permute-done.9 = bf16[2,432,384]{2,1,0:T(8,128)(2,1)S(1)} collective-permute-done((bf16[2,432,384]{2,1,0:T(8,128)(2,1)S(1)}, bf16[2,432,384]{2,1,0:T(8,128)(2,1)S(1)}, u32[]{:S(2)}, u32[]{:S(2)}) %collective-permute-start.9) | collective-permute-done | bytes 663584 | tf_op jit(solution)/shard_map/ppermute | solution.py:471
  105.5 17.2 %all-gather.1 = bf16[384,1152]{1,0:T(8,128)(2,1)S(1)} all-gather(bf16[96,1152]{1,0:T(8,128)(2,1)S(1)} %copy.174), channel_id=3, replica_groups=mesh['ctx'=8,'wa'=4] {'wa'}, dimensions={0}, use_global_device_ids=true | all-gather | bytes 1105920 | tf_op jit(solution)/shard_map/all_gather | solution.py:738
  124.9 10.5 %all-gather.2 = bf16[64,256]{1,0:T(8,128)(2,1)S(1)} all-gather(bf16[16,256]{1,0:T(8,128)(2,1)S(1)} %pad.5), channel_id=4, replica_groups=mesh['ctx'=8,'wa'=4] {'wa'}, dimensions={0}, use_global_device_ids=true | all-gather | bytes 40960 | tf_op jit(solution)/shard_map/all_gather | solution.py:724
  136.1 11.5 %all-gather = s32[1,3072]{1,0:T(1,128)S(1)} all-gather(s32[1,384]{1,0:T(1,128)S(1)} %multiply_add_fusion.3), channel_id=2, replica_groups=mesh['ctx'=8,'wa'=4] {'ctx'}, dimensions={1}, use_global_device_ids=true | all-gather | bytes 13824 | tf_op jit(solution)/shard_map/all_gather | solution.py:706
  160.3 6.8 shard_map.416
  176.1 48.0 %shard_map.417 = (bf16[4,384,192]{2,1,0:T(8,128)(2,1)}, f32[4,192,384]{2,1,0:T(8,128)}, f32[4,3,1,384]{3,2,1,0:T(1,128)}) custom-call(s32[2]{0:T(128)} %pad_add_fusion.place, s32[4]{0:T(128)} %get-tuple-element.223.first, s32[4]{0:T(128)} %get-tuple-element.222.last, bf16[4,384,384]{2,1,0:T(8,128)(2,1)} %get-tuple-element.32.q_ref, ...), custom_call_target="tpu_custom_call" | custom-call | flops 3623878656 | bytes 8388608 | tf_op jit(solution)/shard_map/pallas_call | solution.py:650
  230.1 8.4 %maximum_select_fusion = bf16[4,2,4,432,384]{4,3,2,1,0:T(8,128)(2,1)S(1)} fusion(bf16[4,1,4,432,384]{4,3,2,1,0:T(8,128)(2,1)} %bitcast.27, bf16[4,1,4,432,384]{4,3,2,1,0:T(8,128)(2,1)} %get-tuple-element.184, pred[]{:T(512)S(6)} %eq.19), kind=kLoop, calls=%fused_computation.6 | loop fusion | flops 15925248 | bytes 21233664 | tf_op jit(solution)/shard_map/jit(_where)/select_n | solution.py:766
  250.1 6.8 gather_fusion.2
  257.0 10.2 %maximum_select_fusion.1 = bf16[4,2,4,432,384]{4,3,2,1,0:T(8,128)(2,1)} fusion(bf16[4,2,4,176,384]{4,3,2,1,0:T(8,128)(2,1)} %gather_fusion.3, bf16[4,2,4,256,384]{4,3,2,1,0:T(8,128)(2,1)} %gather_fusion.2, pred[4]{0:T(512)(128)(4,1)S(1)} %get-tuple-element.224), kind=kLoop, calls=%fused_computation.7 | loop fusion | flops 26542080 | bytes 21233668 | tf_op jit(solution)/shard_map/jit(_take)/select_n | solution.py:767
  267.1 8.7 %fusion.50 = (bf16[4,2,4,192,384]{4,3,2,1,0:T(8,128)(2,1)}, bf16[4,192,4,2,384]{4,1,0,3,2:T(8,128)(2,1)}) fusion(bf16[4,2,4,432,384]{4,3,2,1,0:T(8,128)(2,1)} %maximum_select_fusion.1), kind=kLoop, calls=%fused_computation.213 | loop fusion | bytes 18874368 | tf_op jit(solution)/shard_map/slice | solution.py:769
  275.8 9.3 %copy.181 = bf16[4,192,4,2,384]{4,3,2,1,0:T(2,128)(2,1)} copy(bf16[4,192,4,2,384]{4,1,0,3,2:T(8,128)(2,1)} %get-tuple-element.177) | data formatting | bytes 9437184 | tf_op jit(solution)/shard_map/transpose | solution.py:768
  285.1 11.4 %reshape.301 = bf16[768,3072]{1,0:T(8,128)(2,1)} reshape(bf16[4,192,4,2,384]{4,3,2,1,0:T(2,128)(2,1)} %copy.181) | data formatting | bytes 9437184 | tf_op jit(solution)/shard_map/reshape | solution.py:768
  302.0 9.3 %copy.182 = bf16[4,4,2,96,2,384]{5,4,3,2,1,0:T(2,128)(2,1)} copy(bf16[4,4,2,96,2,384]{5,3,4,0,2,1:T(8,128)(2,1)} %bitcast.227) | data formatting | bytes 9437184 | tf_op jit(solution)/shard_map/transpose | solution.py:770
  315.0 14.0 %multiply_convert_fusion = (bf16[384,3072]{1,0:T(8,128)(2,1)S(1)}, f32[384,3072]{1,0:T(8,128)S(1)}, f32[384,3072]{1,0:T(8,128)}) fusion(f32[3072]{0:T(1024)S(1)} %reshape.328, bf16[768,3072]{1,0:T(8,128)(2,1)S(1)} %bitcast.243, f32[384,768]{1,0:T(8,128)S(1)} %get-tuple-element.217, f32[768]{0:T(1024)S(1)} %add.250, f32[768]{0:T(1024)S(1)} %mul.186, ...), kind=kOutput, calls=%fused_computation.22 | convolution fusion | flops 1891270656 | bytes 17716224 | tf_op jit(solution)/shard_map/dot_general | solution.py:36
  339.8 5.8 convert_reduce_fusion
  358.1 10.3 %reshape.316 = bf16[4,4,2,96,2,384]{5,4,3,2,1,0:T(2,128)(2,1)} reshape(bf16[3072,768]{1,0:T(8,128)(2,1)} %convolution_convert_fusion) | data formatting | bytes 9437184 | tf_op jit(solution)/shard_map/reshape | solution.py:844
  376.4 5.6 gather_fusion.5
  382.0 11.7 %reshape.315 = bf16[4,192,4,2,384]{4,3,2,1,0:T(2,128)(2,1)} reshape(bf16[768,3072]{1,0:T(8,128)(2,1)} %convolution_convert_fusion.1) | data formatting | bytes 9437184 | tf_op jit(solution)/shard_map/reshape | solution.py:841
  393.7 5.6 copy.221
  399.3 5.8 pad_maximum_fusion
  405.1 7.0 gather_fusion.4
  412.0 6.4 maximum_select_fusion.2
  425.2 12.1 %all_to_all.10 = bf16[4,384,192]{1,2,0:T(8,128)(2,1)S(1)} all-to-all(bf16[4,384,192]{1,2,0:T(8,128)(2,1)S(1)} %bitcast.263), channel_id=1, replica_groups={{0,8,16,24},{4,12,20,28},{1,9,17,25},{5,13,21,29},{2,10,18,26},{6,14,22..., dimensions={0} | all-to-all | bytes 1179648 | tf_op jit(solution)/shard_map/all_to_all | solution.py:811
  438.4 53.7 %shard_map.418 = (bf16[4,384,768]{2,1,0:T(8,128)(2,1)}, bf16[4,384,384]{2,1,0:T(8,128)(2,1)}, bf16[4,384,384]{2,1,0:T(8,128)(2,1)}) custom-call(s32[2]{0:T(128)} %pad_add_fusion.place, s32[4]{0:T(128)} %get-tuple-element.223.first, s32[4]{0:T(128)} %get-tuple-element.222.last, bf16[4,384,384]{2,1,0:T(8,128)(2,1)} %get-tuple-element.32.q_ref, ...), custom_call_target="tpu_custom_call" | custom-call | flops 9059696640 | bytes 16777216 | tf_op jit(solution)/shard_map/pallas_call | solution.py:650
  500.2 5.6 copy.188
  508.3 11.1 %fusion.46 = (bf16[4,4,432,384]{3,2,1,0:T(8,128)(2,1)}, f32[4,4,432,384]{3,2,1,0:T(8,128)}) fusion(bf16[4,4,432,384]{3,2,1,0:T(8,128)(2,1)} %collective-permute-done.22, bf16[4,2,4,432,384]{4,3,2,1,0:T(8,128)(2,1)} %copy-done.2, s32[]{:T(128)S(6)} %select_n.157), kind=kLoop, calls=%fused_computation.210 | loop fusion | flops 10616832 | bytes 26542084 | tf_op jit(solution)/shard_map/convert.12
  526.1 12.9 %collective-permute-done.23 = bf16[2,432,384]{2,1,0:T(8,128)(2,1)} collective-permute-done((bf16[2,432,384]{2,1,0:T(8,128)(2,1)}, bf16[2,432,384]{2,1,0:T(8,128)(2,1)}, u32[]{:S(2)}, u32[]{:S(2)}) %collective-permute-start.23) | collective-permute-done | bytes 663584 | tf_op jit(solution)/shard_map/ppermute | solution.py:471
  548.4 24.0 %collective-permute-done.26 = bf16[4,432,384]{2,1,0:T(8,128)(2,1)} collective-permute-done((bf16[4,432,384]{2,1,0:T(8,128)(2,1)}, bf16[4,432,384]{2,1,0:T(8,128)(2,1)}, u32[]{:S(2)}, u32[]{:S(2)}) %collective-permute-start.26) | collective-permute-done | bytes 1327136 | tf_op jit(solution)/shard_map/ppermute | solution.py:471
  586.4 41.0 %all-reduce.2 = (f32[4,1152]{1,0:T(4,128)S(1)}, f32[10,768]{1,0:T(8,128)S(1)}) all-reduce(f32[4,1152]{1,0:T(4,128)S(1)} %broadcast_select_fusion, f32[10,768]{1,0:T(8,128)S(1)} %concatenate.72), channel_id=1, replica_groups=mesh['ctx'=8,'wa'=4] {'ctx','wa'}, use_global_device_ids=true, to_apply=%region_13.15 | all-reduce | flops 12288 | bytes 98304 | tf_op jit(solution)/shard_map/psum | solution.py:924
  638.1 9.5 %collective-permute-done.19 = bf16[48,1152]{1,0:T(8,128)(2,1)S(1)} collective-permute-done((bf16[48,1152]{1,0:T(8,128)(2,1)S(1)}, bf16[48,1152]{1,0:T(8,128)(2,1)S(1)}, u32[]{:S(2)}, u32[]{:S(2)}) %collective-permute-start.19) | collective-permute-done | bytes 110624 | tf_op jit(solution)/shard_map/ppermute | solution.py:471
  (405 shorter events, 233.3 us)
Async XLA Ops:
  7.2 36.3 %all-gather.6.cloned.1.call-start = ((), (), s32[]{:S(2)}) async-start(), calls=%async_computation.6 | async-start | bytes 1658880 | tf_op jit(solution)/shard_map/all_gather | solution.py:763
  43.5 30.0 %collective-permute-start.7 = (bf16[4,432,384]{2,1,0:T(8,128)(2,1)}, bf16[4,432,384]{2,1,0:T(8,128)(2,1)S(1)}, u32[]{:S(2)}, u32[]{:S(2)}) collective-permute-start(bf16[4,432,384]{2,1,0:T(8,128)(2,1)} %bitcast.267), channel_id=1, source_target_pairs={{0,16},{4,20},{8,24},{12,28},{16,0},{20,4},{24,8},{28,12},{1,17},{... | collective-permute-start | bytes 3981320 | tf_op jit(solution)/shard_map/ppermute | solution.py:471
  44.7 30.1 %collective-permute-start.6 = (bf16[4,432,384]{2,1,0:T(8,128)(2,1)}, bf16[4,432,384]{2,1,0:T(8,128)(2,1)S(1)}, u32[]{:S(2)}, u32[]{:S(2)}) collective-permute-start(bf16[4,432,384]{2,1,0:T(8,128)(2,1)} %bitcast.268), channel_id=1, source_target_pairs={{0,8},{4,12},{8,0},{12,4},{16,24},{20,28},{24,16},{28,20},{1,9},{5... | collective-permute-start | bytes 3981320 | tf_op jit(solution)/shard_map/ppermute | solution.py:471
  73.5 14.7 %collective-permute-start.9 = (bf16[2,432,384]{2,1,0:T(8,128)(2,1)S(1)}, bf16[2,432,384]{2,1,0:T(8,128)(2,1)S(1)}, u32[]{:S(2)}, u32[]{:S(2)}) collective-permute-start(bf16[2,432,384]{2,1,0:T(8,128)(2,1)S(1)} %slice.296), channel_id=1, source_target_pairs={{0,8},{4,12},{8,0},{12,4},{16,24},{20,28},{24,16},{28,20},{1,9},{5... | collective-permute-start | bytes 1990664 | tf_op jit(solution)/shard_map/ppermute | solution.py:471
  74.8 14.4 %collective-permute-start.8 = (bf16[2,432,384]{2,1,0:T(8,128)(2,1)S(1)}, bf16[2,432,384]{2,1,0:T(8,128)(2,1)S(1)}, u32[]{:S(2)}, u32[]{:S(2)}) collective-permute-start(bf16[2,432,384]{2,1,0:T(8,128)(2,1)S(1)} %slice.295), channel_id=1, source_target_pairs={{0,16},{4,20},{8,24},{12,28},{16,0},{20,4},{24,8},{28,12},{1,17},{... | collective-permute-start | bytes 1990664 | tf_op jit(solution)/shard_map/ppermute | solution.py:471
  93.9 136.2 %collective-permute-start.10 = (bf16[4,4,432,384]{3,2,1,0:T(8,128)(2,1)}, bf16[4,4,432,384]{3,2,1,0:T(8,128)(2,1)}, u32[]{:S(2)}, u32[]{:S(2)}) collective-permute-start(bf16[4,4,432,384]{3,2,1,0:T(8,128)(2,1)} %get-tuple-element.185), channel_id=1, source_target_pairs={{0,4},{4,0},{8,12},{12,8},{16,20},{20,16},{24,28},{28,24},{1,5},{5... | collective-permute-start | bytes 15925256 | tf_op jit(solution)/shard_map/ppermute | solution.py:471
  97.0 53.5 %collective-permute-start = (bf16[384,768]{1,0:T(8,128)(2,1)}, bf16[384,768]{1,0:T(8,128)(2,1)S(1)}, u32[]{:S(2)}, u32[]{:S(2)}) collective-permute-start(bf16[384,768]{1,0:T(8,128)(2,1)} %bitcast.t0), channel_id=1, source_target_pairs={{0,8},{4,12},{8,0},{12,4},{16,24},{20,28},{24,16},{28,20},{1,9},{5... | collective-permute-start | bytes 1769480 | tf_op jit(solution)/shard_map/ppermute | solution.py:471
  97.7 52.4 %collective-permute-start.1 = (bf16[384,768]{1,0:T(8,128)(2,1)}, bf16[384,768]{1,0:T(8,128)(2,1)S(1)}, u32[]{:S(2)}, u32[]{:S(2)}) collective-permute-start(bf16[384,768]{1,0:T(8,128)(2,1)} %bitcast.t0), channel_id=1, source_target_pairs={{0,16},{4,20},{8,24},{12,28},{16,0},{20,4},{24,8},{28,12},{1,17},{... | collective-permute-start | bytes 1769480 | tf_op jit(solution)/shard_map/ppermute | solution.py:471
  122.6 29.2 %collective-permute-start.4 = (bf16[4,96,1152]{2,1,0:T(8,128)(2,1)S(1)}, bf16[4,96,1152]{2,1,0:T(8,128)(2,1)S(1)}, u32[]{:S(2)}, u32[]{:S(2)}) collective-permute-start(bf16[4,96,1152]{2,1,0:T(8,128)(2,1)S(1)} %bitcast.247), channel_id=1, source_target_pairs={{0,4},{4,0},{8,12},{12,8},{16,20},{20,16},{24,28},{28,24},{1,5},{5... | collective-permute-start | bytes 2654216 | tf_op jit(solution)/shard_map/ppermute | solution.py:471
  150.2 8.5 %collective-permute-start.3 = (bf16[192,768]{1,0:T(8,128)(2,1)S(1)}, bf16[192,768]{1,0:T(8,128)(2,1)S(1)}, u32[]{:S(2)}, u32[]{:S(2)}) collective-permute-start(bf16[192,768]{1,0:T(8,128)(2,1)S(1)} %slice.292), channel_id=1, source_target_pairs={{0,8},{4,12},{8,0},{12,4},{16,24},{20,28},{24,16},{28,20},{1,9},{5... | collective-permute-start | bytes 884744 | tf_op jit(solution)/shard_map/ppermute | solution.py:471
  150.5 8.2 %collective-permute-start.2 = (bf16[192,768]{1,0:T(8,128)(2,1)S(1)}, bf16[192,768]{1,0:T(8,128)(2,1)S(1)}, u32[]{:S(2)}, u32[]{:S(2)}) collective-permute-start(bf16[192,768]{1,0:T(8,128)(2,1)S(1)} %slice.291), channel_id=1, source_target_pairs={{0,16},{4,20},{8,24},{12,28},{16,0},{20,4},{24,8},{28,12},{1,17},{... | collective-permute-start | bytes 884744 | tf_op jit(solution)/shard_map/ppermute | solution.py:471
  167.1 8.0 %collective-permute-start.5 = (bf16[4,384,384]{2,1,0:T(8,128)(2,1)}, bf16[4,384,384]{2,1,0:T(8,128)(2,1)S(1)}, u32[]{:S(2)}, u32[]{:S(2)}) collective-permute-start(bf16[4,384,384]{2,1,0:T(8,128)(2,1)} %get-tuple-element.33.own), channel_id=1, source_target_pairs={{0,4},{4,0},{8,12},{12,8},{16,20},{20,16},{24,28},{28,24},{1,5},{5... | collective-permute-start | bytes 3538952 | tf_op jit(solution)/shard_map/ppermute | solution.py:471
  226.4 73.1 %all-to-all-start = ((bf16[4,384,192]{1,2,0:T(8,128)(2,1)}), bf16[4,384,192]{1,2,0:T(8,128)(2,1)S(1)}, u32[]{:S(2)}, u32[]{:S(2)}) async-start(bf16[4,384,192]{1,2,0:T(8,128)(2,1)} %copy.179), calls=%async_computation | async-start | bytes 1179648 | tf_op jit(solution)/shard_map/all_to_all | solution.py:811
  229.9 397.6 %reduce-scatter.3.cloned.1.call-start = ((), (), s32[]{:S(2)}) async-start(), calls=%async_computation.4 | async-start | bytes 1105920 | tf_op jit(solution)/shard_map/reduce_scatter | solution.py:914
  424.2 84.1 %collective-permute-start.22 = (bf16[4,4,432,384]{3,2,1,0:T(8,128)(2,1)}, bf16[4,4,432,384]{3,2,1,0:T(8,128)(2,1)}, u32[]{:S(2)}, u32[]{:S(2)}) collective-permute-start(bf16[4,4,432,384]{3,2,1,0:T(8,128)(2,1)} %dynamic-slice_bitcast_fusion), channel_id=1, source_target_pairs={{0,4},{4,0},{8,12},{12,8},{16,20},{20,16},{24,28},{28,24},{1,5},{5... | collective-permute-start | bytes 15925256 | tf_op jit(solution)/shard_map/ppermute | solution.py:471
  508.3 15.5 %collective-permute-start.16 = (bf16[4,96,1152]{2,1,0:T(8,128)(2,1)}, bf16[4,96,1152]{2,1,0:T(8,128)(2,1)}, u32[]{:S(2)}, u32[]{:S(2)}) collective-permute-start(bf16[4,96,1152]{2,1,0:T(8,128)(2,1)} %fusion.27), channel_id=1, source_target_pairs={{0,4},{4,0},{8,12},{12,8},{16,20},{20,16},{24,28},{28,24},{1,5},{5... | collective-permute-start | bytes 2654216 | tf_op jit(solution)/shard_map/ppermute | solution.py:471
  522.8 16.3 %collective-permute-start.23 = (bf16[2,432,384]{2,1,0:T(8,128)(2,1)}, bf16[2,432,384]{2,1,0:T(8,128)(2,1)}, u32[]{:S(2)}, u32[]{:S(2)}) collective-permute-start(bf16[2,432,384]{2,1,0:T(8,128)(2,1)} %get-tuple-element.183), channel_id=1, source_target_pairs={{0,16},{4,20},{8,24},{12,28},{16,0},{20,4},{24,8},{28,12},{1,17},{... | collective-permute-start | bytes 1990664 | tf_op jit(solution)/shard_map/ppermute | solution.py:471
  523.4 16.0 %collective-permute-start.25 = (bf16[2,432,384]{2,1,0:T(8,128)(2,1)}, bf16[2,432,384]{2,1,0:T(8,128)(2,1)}, u32[]{:S(2)}, u32[]{:S(2)}) collective-permute-start(bf16[2,432,384]{2,1,0:T(8,128)(2,1)} %get-tuple-element.182), channel_id=1, source_target_pairs={{0,8},{4,12},{8,0},{12,4},{16,24},{20,28},{24,16},{28,20},{1,9},{5... | collective-permute-start | bytes 1990664 | tf_op jit(solution)/shard_map/ppermute | solution.py:471
  526.1 124.8 %reduce-scatter.5.cloned.1.call-start = ((), (), s32[]{:S(2)}) async-start(), calls=%async_computation.5 | async-start | bytes 1658880 | tf_op jit(solution)/shard_map/reduce_scatter | solution.py:867
  543.2 29.3 %collective-permute-start.26 = (bf16[4,432,384]{2,1,0:T(8,128)(2,1)}, bf16[4,432,384]{2,1,0:T(8,128)(2,1)}, u32[]{:S(2)}, u32[]{:S(2)}) collective-permute-start(bf16[4,432,384]{2,1,0:T(8,128)(2,1)} %pad_maximum_fusion.5), channel_id=1, source_target_pairs={{0,16},{4,20},{8,24},{12,28},{16,0},{20,4},{24,8},{28,12},{1,17},{... | collective-permute-start | bytes 3981320 | tf_op jit(solution)/shard_map/ppermute | solution.py:471
  545.3 29.0 %collective-permute-start.24 = (bf16[4,432,384]{2,1,0:T(8,128)(2,1)}, bf16[4,432,384]{2,1,0:T(8,128)(2,1)}, u32[]{:S(2)}, u32[]{:S(2)}) collective-permute-start(bf16[4,432,384]{2,1,0:T(8,128)(2,1)} %pad_maximum_fusion.4), channel_id=1, source_target_pairs={{0,8},{4,12},{8,0},{12,4},{16,24},{20,28},{24,16},{28,20},{1,9},{5... | collective-permute-start | bytes 3981320 | tf_op jit(solution)/shard_map/ppermute | solution.py:471
  585.3 44.5 %collective-permute-start.12 = (bf16[192,768]{1,0:T(8,128)(2,1)S(1)}, bf16[192,768]{1,0:T(8,128)(2,1)S(1)}, u32[]{:S(2)}, u32[]{:S(2)}) collective-permute-start(bf16[192,768]{1,0:T(8,128)(2,1)S(1)} %get-tuple-element.195), channel_id=1, source_target_pairs={{0,16},{4,20},{8,24},{12,28},{16,0},{20,4},{24,8},{28,12},{1,17},{... | collective-permute-start | bytes 884744 | tf_op jit(solution)/shard_map/ppermute | solution.py:471
  586.0 43.8 %collective-permute-start.14 = (bf16[192,768]{1,0:T(8,128)(2,1)S(1)}, bf16[192,768]{1,0:T(8,128)(2,1)S(1)}, u32[]{:S(2)}, u32[]{:S(2)}) collective-permute-start(bf16[192,768]{1,0:T(8,128)(2,1)S(1)} %get-tuple-element.194), channel_id=1, source_target_pairs={{0,8},{4,12},{8,0},{12,4},{16,24},{20,28},{24,16},{28,20},{1,9},{5... | collective-permute-start | bytes 884744 | tf_op jit(solution)/shard_map/ppermute | solution.py:471
  627.5 5.4 collective-permute-start.18
  632.0 31.9 %collective-permute-start.15 = (bf16[384,768]{1,0:T(8,128)(2,1)}, bf16[384,768]{1,0:T(8,128)(2,1)}, u32[]{:S(2)}, u32[]{:S(2)}) collective-permute-start(bf16[384,768]{1,0:T(8,128)(2,1)} %pad_maximum_fusion.10), channel_id=1, source_target_pairs={{0,16},{4,20},{8,24},{12,28},{16,0},{20,4},{24,8},{28,12},{1,17},{... | collective-permute-start | bytes 1769480 | tf_op jit(solution)/shard_map/ppermute | solution.py:471
  634.2 13.4 %collective-permute-start.19 = (bf16[48,1152]{1,0:T(8,128)(2,1)S(1)}, bf16[48,1152]{1,0:T(8,128)(2,1)S(1)}, u32[]{:S(2)}, u32[]{:S(2)}) collective-permute-start(bf16[48,1152]{1,0:T(8,128)(2,1)S(1)} %slice.316), channel_id=1, source_target_pairs={{0,16},{4,20},{8,24},{12,28},{16,0},{20,4},{24,8},{28,12},{1,17},{... | collective-permute-start | bytes 331784 | tf_op jit(solution)/shard_map/ppermute | solution.py:471
  636.1 27.8 %collective-permute-start.13 = (bf16[384,768]{1,0:T(8,128)(2,1)}, bf16[384,768]{1,0:T(8,128)(2,1)}, u32[]{:S(2)}, u32[]{:S(2)}) collective-permute-start(bf16[384,768]{1,0:T(8,128)(2,1)} %pad_maximum_fusion.9), channel_id=1, source_target_pairs={{0,8},{4,12},{8,0},{12,4},{16,24},{20,28},{24,16},{28,20},{1,9},{5... | collective-permute-start | bytes 1769480 | tf_op jit(solution)/shard_map/ppermute | solution.py:471
  647.8 24.8 %collective-permute-start.21 = (bf16[4,96,1152]{2,1,0:T(8,128)(2,1)S(1)}, bf16[4,96,1152]{2,1,0:T(8,128)(2,1)}, u32[]{:S(2)}, u32[]{:S(2)}) collective-permute-start(bf16[4,96,1152]{2,1,0:T(8,128)(2,1)S(1)} %get-tuple-element.204), channel_id=1, source_target_pairs={{0,4},{4,0},{8,12},{12,8},{16,20},{20,16},{24,28},{28,24},{1,5},{5... | collective-permute-start | bytes 2654216 | tf_op jit(solution)/shard_map/ppermute | solution.py:471
  650.8 9.9 %collective-permute-start.28 = (bf16[432,384]{1,0:T(8,128)(2,1)}, bf16[432,384]{1,0:T(8,128)(2,1)S(1)}, u32[]{:S(2)}, u32[]{:S(2)}) collective-permute-start(bf16[432,384]{1,0:T(8,128)(2,1)} %bitcast.279), channel_id=1, source_target_pairs={{0,16},{4,20},{8,24},{12,28},{16,0},{20,4},{24,8},{28,12},{1,17},{... | collective-permute-start | bytes 995336 | tf_op jit(solution)/shard_map/ppermute | solution.py:471
  652.4 9.7 %collective-permute-start.27 = (bf16[432,384]{1,0:T(8,128)(2,1)}, bf16[432,384]{1,0:T(8,128)(2,1)}, u32[]{:S(2)}, u32[]{:S(2)}) collective-permute-start(bf16[432,384]{1,0:T(8,128)(2,1)} %bitcast.280), channel_id=1, source_target_pairs={{0,8},{4,12},{8,0},{12,4},{16,24},{20,28},{24,16},{28,20},{1,9},{5... | collective-permute-start | bytes 995336 | tf_op jit(solution)/shard_map/ppermute | solution.py:471
  660.7 6.1 collective-permute-start.30
  670.7 21.3 %collective-permute-start.31 = (bf16[4,432,384]{2,1,0:T(8,128)(2,1)}, bf16[4,432,384]{2,1,0:T(8,128)(2,1)}, u32[]{:S(2)}, u32[]{:S(2)}) collective-permute-start(bf16[4,432,384]{2,1,0:T(8,128)(2,1)} %get-tuple-element.199), channel_id=1, source_target_pairs={{0,4},{4,0},{8,12},{12,8},{16,20},{20,16},{24,28},{28,24},{1,5},{5... | collective-permute-start | bytes 3981320 | tf_op jit(solution)/shard_map/ppermute | solution.py:471
  (73 other events, 1382.0 us)
Sparse Core Ops, SparseCore 0:
  10.2 33.1 all-gather.5
  526.2 21.1 reduce-scatter.2
  578.4 29.8 reduce-scatter.4

commit v2 on v0

--- a/solution.py
+++ b/solution.py
@@ -1,6 +1,8 @@
 import jax
 import jax.numpy as jnp
 from jax import lax
+from jax.experimental import pallas as pl
+from jax.experimental.pallas import tpu as pltpu
 from jax.sharding import PartitionSpec as P
 
 HD = 64
@@ -67,7 +69,7 @@
     )
 
 
-def per_device(
+def windowed_device(
     tokens,
     cotangent,
     segment_ids,
@@ -453,6 +455,840 @@
     )
 
 
+CHIPS = 4
+KEY_BLOCK = 256
+NEGATIVE = -1e30
+TAG_ROWS = 16
+TILE = 128
+
+
+def lanes_product(left, right):
+    return lax.dot_general(
+        left, right, (((1,), (1,)), ((), ())), preferred_element_type=jnp.float32
+    )
+
+
+def rows_product(left, right):
+    return lax.dot_general(
+        left, right, (((0,), (0,)), ((), ())), preferred_element_type=jnp.float32
+    )
+
+
+def plain_product(left, right):
+    return jnp.dot(left, right, preferred_element_type=jnp.float32)
+
+
+def swapped(value, step):
+    count = lax.axis_size("ctx")
+    return lax.ppermute(value, "ctx", [(i, i ^ step) for i in range(count)])
+
+
+def turned(value, step):
+    count = lax.axis_size("wa")
+    return lax.ppermute(value, "wa", [(i, (i + step) % count) for i in range(count)])
+
+
+def as_column(row):
+    return jnp.broadcast_to(row, (TILE, row.shape[1])).T
+
+
+def segment_of(tag):
+    return jnp.floor(tag * 0.5)
+
+
+def project_kernel(place, t0, t1, t2, t3a, t3b, mine, theirs, weight, tokens, q_ref, kv_ref):
+    parts, rows = mine.shape[0], mine.shape[1] - TAG_ROWS
+    tok = q_ref.shape[1]
+    chip, core, wa = place[0], place[1], place[2]
+    cut = t3a.shape[0]
+    tokens[0] = t0[...]
+    tokens[1] = t1[...]
+    tokens[2] = t2[...]
+    tokens[3, :cut] = t3a[...]
+    tokens[3, cut:] = t3b[...]
+    for z in range(parts):
+        k = lax.rem(wa - z + parts, parts)
+        for source, side in ((mine, core), (theirs, 1 - core)):
+            weight[pl.ds(pl.multiple_of(2 * rows * z + rows * side, 32), rows), :] = source[k, :rows]
+    k = lax.rem(wa - chip + parts, parts)
+    bias = mine[k, rows : rows + TAG_ROWS].astype(jnp.float32)[:1]
+    wide = 2 * HD
+
+    def piece(m, unused):
+        to = jnp.bitwise_xor(chip, m)
+        tags = tokens[m, tok : tok + TAG_ROWS].astype(jnp.float32)[:1, :tok]
+        flag = as_column(tags - 2.0 * segment_of(tags)) == 1.0
+        text = tokens[m, :tok]
+        for h in range(3):
+            at = 2 * wide * h
+            both = plain_product(text, weight[:, at : at + 2 * wide]) + bias[:, at : at + 2 * wide]
+            q = jnp.where(flag, both[:, wide:], both[:, :wide]).astype(jnp.bfloat16)
+            q_ref[to, :, wide * h : wide * (h + 1)] = q * jnp.bfloat16(HD**-0.5)
+        kv = plain_product(text, weight[:, 6 * wide :]) + bias[:, 6 * wide :]
+        kv_ref[to, :tok] = kv.astype(jnp.bfloat16)
+        kv_ref[to, tok:] = jnp.broadcast_to(tags, (TAG_ROWS, tok)).astype(jnp.bfloat16)
+        return 0
+
+    lax.fori_loop(0, CHIPS, piece, 0)
+
+
+def masked_keys(kv, flag):
+    wide = kv.astype(jnp.float32)
+    low = lax.broadcasted_iota(jnp.int32, kv.shape, 1) < HD
+    both = jnp.where(low, wide, pltpu.roll(wide, HD, 1))
+    return jnp.where(low == flag, 0.0, both)
+
+
+def attend_kernel(place, q_ref, own, other, out, turned_out, lse, bounds, keys, values, seg_col, seg_row, acc):
+    tok = q_ref.shape[1]
+    core = place[1]
+
+    def prepare(j, unused):
+        for source, side in ((own, core), (other, 1 - core)):
+            shard = 2 * j + side
+            at = pl.ds(pl.multiple_of(shard * tok, TILE), tok)
+            tags = source[j, tok : tok + TAG_ROWS].astype(jnp.float32)[:1]
+            seg_row[shard] = jnp.broadcast_to(segment_of(tags), (8, tok))
+            column = as_column(tags)
+            segment = segment_of(column)
+            seg_col[at, :] = segment
+            flag = column - 2.0 * segment == 1.0
+            for h in range(3):
+                kv = source[j, :tok, 2 * HD * h : 2 * HD * (h + 1)]
+                keys[h, at, :] = masked_keys(kv, flag).astype(jnp.bfloat16)
+                values[h, :, at] = kv.astype(jnp.float32).T[HD:].astype(jnp.bfloat16)
+        return 0
+
+    lax.fori_loop(0, CHIPS, prepare, 0)
+
+    def queries(j, unused):
+        seg = seg_row[2 * j + core][:1]
+        everyone = seg_row[...][:, 0, :]
+        before = jnp.sum((everyone < jnp.min(seg)).astype(jnp.float32)).astype(jnp.int32)
+        through = jnp.sum((everyone <= jnp.max(seg)).astype(jnp.float32)).astype(jnp.int32)
+        first = before // KEY_BLOCK
+        last = (through + KEY_BLOCK - 1) // KEY_BLOCK
+        bounds[0, j] = first
+        bounds[1, j] = last
+        acc[...] = jnp.zeros_like(acc)
+
+        def step(t, carry):
+            at = pl.ds(pl.multiple_of(t * KEY_BLOCK, KEY_BLOCK), KEY_BLOCK)
+            column = seg_col[at, :]
+            same = jnp.concatenate([column] * (tok // TILE), axis=1) == seg
+            after = []
+            for h in range(3):
+                top, total = carry[2 * h], carry[2 * h + 1]
+                scores = lanes_product(keys[h, at, :], q_ref[j, :, 2 * HD * h : 2 * HD * (h + 1)])
+                scores = jnp.where(same, scores, NEGATIVE)
+                peak = jnp.maximum(top, jnp.max(scores, axis=0, keepdims=True))
+                fade = jnp.exp(top - peak)
+                expo = jnp.exp(scores - peak)
+                total = total * fade + jnp.sum(expo, axis=0, keepdims=True)
+                acc[h] = acc[h] * fade + plain_product(values[h, :, at], expo.astype(jnp.bfloat16))
+                after += [peak, total]
+            return tuple(after)
+
+        start = (jnp.full((1, tok), NEGATIVE, jnp.float32), jnp.zeros((1, tok), jnp.float32)) * 3
+        done = lax.fori_loop(first, last, step, start)
+        for h in range(3):
+            turned_out[j, HD * h : HD * (h + 1), :] = acc[h] / done[2 * h + 1]
+            lse[j, h] = done[2 * h] + jnp.log(done[2 * h + 1])
+        out[j] = turned_out[j].T.astype(jnp.bfloat16)
+        return 0
+
+    lax.fori_loop(0, CHIPS, queries, 0)
+
+
+def attend_back_kernel(
+    place,
+    bounds,
+    q_ref,
+    own,
+    other,
+    turned_out,
+    lse,
+    grad,
+    dq_ref,
+    dkv_own,
+    dkv_other,
+    keys,
+    turned_keys,
+    values,
+    grad_keys,
+    grad_values,
+    seg_col,
+    seg_row,
+    acc,
+):
+    tok = q_ref.shape[1]
+    chip, core = place[0], place[1]
+    wide = 2 * HD
+
+    def prepare(j, unused):
+        for source, side in ((own, core), (other, 1 - core)):
+            shard = 2 * j + side
+            at = pl.ds(pl.multiple_of(shard * tok, TILE), tok)
+            tags = source[j, tok : tok + TAG_ROWS].astype(jnp.float32)[:1]
+            seg_row[shard] = jnp.broadcast_to(tags, (8, tok))
+            column = as_column(tags)
+            segment = segment_of(column)
+            seg_col[at, :] = segment
+            flag = column - 2.0 * segment == 1.0
+            for h in range(3):
+                kv = source[j, :tok, wide * h : wide * (h + 1)]
+                key = masked_keys(kv, flag)
+                keys[h, at, :] = key.astype(jnp.bfloat16)
+                turned_keys[h, :, at] = key.T.astype(jnp.bfloat16)
+                values[h, at, :] = kv
+                grad_keys[h, at, :] = jnp.zeros((tok, wide), jnp.float32)
+                grad_values[h, at, :] = jnp.zeros((tok, wide), jnp.float32)
+        return 0
+
+    lax.fori_loop(0, CHIPS, prepare, 0)
+
+    def queries(j, unused):
+        tags = seg_row[2 * j + core][:1]
+        seg = segment_of(tags)
+        slot = jnp.bitwise_xor(chip, j)
+        flag = as_column(tags - 2.0 * seg) == 1.0
+        turned_grad = grad[j].astype(jnp.float32).T
+        deltas, shifts, padded = [], [], []
+        for h in range(3):
+            rows = slice(HD * h, HD * (h + 1))
+            deltas.append(jnp.sum(turned_grad[rows] * turned_out[j, rows, :], axis=0, keepdims=True))
+            shifts.append(lse[j, h])
+            head = grad[j, :, rows]
+            padded.append(jnp.concatenate([jnp.zeros_like(head), head], axis=1))
+        acc[...] = jnp.zeros_like(acc)
+
+        def step(t, carry):
+            at = pl.ds(pl.multiple_of(t * KEY_BLOCK, KEY_BLOCK), KEY_BLOCK)
+            column = seg_col[at, :]
+            same = jnp.concatenate([column] * (tok // TILE), axis=1) == seg
+            for h in range(3):
+                q = q_ref[j, :, wide * h : wide * (h + 1)]
+                scores = lanes_product(keys[h, at, :], q)
+                probs = jnp.where(same, jnp.exp(scores - shifts[h]), 0.0)
+                grad_probs = lanes_product(values[h, at, :], padded[h])
+                grad_scores = (probs * (grad_probs - deltas[h])).astype(jnp.bfloat16)
+                grad_values[h, at, :] += plain_product(probs.astype(jnp.bfloat16), padded[h])
+                grad_keys[h, at, :] += plain_product(grad_scores, q)
+                acc[h] += plain_product(turned_keys[h, :, at], grad_scores)
+            return carry
+
+        lax.fori_loop(bounds[0, j], bounds[1, j], step, 0)
+        for h in range(3):
+            dq = acc[h].T * (HD**-0.5)
+            at = 2 * wide * h
+            dq_ref[slot, :, at : at + wide] = jnp.where(flag, 0.0, dq).astype(jnp.bfloat16)
+            dq_ref[slot, :, at + wide : at + 2 * wide] = jnp.where(flag, dq, 0.0).astype(jnp.bfloat16)
+        return 0
+
+    lax.fori_loop(0, CHIPS, queries, 0)
+
+    def finish(j, unused):
+        slot = jnp.bitwise_xor(chip, j)
+        for target, side in ((dkv_own, core), (dkv_other, 1 - core)):
+            shard = 2 * j + side
+            at = pl.ds(pl.multiple_of(shard * tok, TILE), tok)
+            tags = seg_row[shard][:1]
+            flag = as_column(tags - 2.0 * segment_of(tags)) == 1.0
+            for h in range(3):
+                both = grad_keys[h, at, :]
+                low = lax.broadcasted_iota(jnp.int32, both.shape, 1) < HD
+                picked = jnp.where(flag, pltpu.roll(both, HD, 1), both)
+                target[slot, :, wide * h : wide * (h + 1)] = jnp.where(
+                    low, picked, grad_values[h, at, :]
+                ).astype(jnp.bfloat16)
+        return 0
+
+    lax.fori_loop(0, CHIPS, finish, 0)
+
+
+def normed(total, gain, shift):
+    center = total - jnp.mean(total, axis=-1, keepdims=True)
+    spread = jnp.mean(center * center, axis=-1, keepdims=True)
+    inverse = lax.rsqrt(spread + EPSILON)
+    unit = center * inverse
+    return unit * gain + shift, unit, inverse
+
+
+def normed_back(grad, unit, inverse, gain):
+    scaled = grad * gain
+    mean = jnp.mean(scaled, axis=-1, keepdims=True)
+    along = jnp.mean(scaled * unit, axis=-1, keepdims=True)
+    return inverse * (scaled - mean - unit * along)
+
+
+def summed_rows(value):
+    return jnp.sum(value, axis=0, keepdims=True)
+
+
+def dense_kernel(
+    place,
+    context,
+    text,
+    cotangent,
+    vectors,
+    inner_bias,
+    near_own,
+    near_other,
+    far_own,
+    far_other,
+    result,
+    grad_sum,
+    grad_context,
+    kept,
+    sent_far,
+    sent_near,
+    inner_w,
+    outer_w,
+    output_w,
+    hidden,
+    slope,
+    inner_g,
+    outer_g,
+    output_g,
+    small,
+    sums,
+    in_sems,
+    out_sems,
+):
+    bf16, f32 = jnp.bfloat16, jnp.float32
+    chip, core, wa = place[0], place[1], place[2]
+    tok, dmod = result.shape
+    ff = hidden.shape[1]
+    group = dmod // CHIPS
+    parts = CHIPS
+    rows = dmod // parts
+    half = rows // 2
+    quarter = rows // CHIPS
+    slot_w = ff // (2 * CHIPS)
+
+    def fetch(m, unused):
+        g = jnp.bitwise_xor(chip, m)
+        for source, side, base in (
+            (near_own, core, 0),
+            (near_other, 1 - core, 0),
+            (far_own, core, 2),
+            (far_other, 1 - core, 2),
+        ):
+            s = 2 * g + side
+            for u in range(2):
+                z = lax.rem(wa - base - u + parts, parts)
+                pltpu.make_async_copy(
+                    source.at[m, u, pl.ds(2 * rows, quarter), :],
+                    output_w.at[
+                        pl.ds(pl.multiple_of(rows * z + quarter * g, 16), quarter),
+                        pl.ds(pl.multiple_of(slot_w * side, TILE), slot_w),
+                    ],
+                    in_sems.at[0],
+                ).start()
+                pltpu.make_async_copy(
+                    source.at[m, u, pl.ds(0, rows), :],
+                    inner_w.at[
+                        pl.ds(pl.multiple_of(rows * z, 16), rows),
+                        pl.ds(pl.multiple_of(slot_w * s, TILE), slot_w),
+                    ],
+                    in_sems.at[1],
+                ).start()
+                for v in range(2):
+                    pltpu.make_async_copy(
+                        source.at[m, u, pl.ds(rows + half * v, half), :],
+                        outer_w.at[
+                            pl.ds(pl.multiple_of(dmod * z + half * s, 16), half),
+                            pl.ds(slot_w * v, slot_w),
+                        ],
+                        in_sems.at[2],
+                    ).start()
+        return 0
+
+    lax.fori_loop(0, CHIPS, fetch, 0)
+    names = ("outb", "g1", "s1", "outerb", "g2", "s2")
+    vec = {name: vectors[k : k + 1, :] for k, name in enumerate(names)}
+
+    pltpu.make_async_copy(output_w, output_w, in_sems.at[0]).wait()
+    branch = vec["outb"]
+    for g in range(CHIPS):
+        branch = branch + plain_product(context[g], output_w[group * g : group * (g + 1), :])
+    first, unit_one, inverse_one = normed(text[:tok, :].astype(f32) + branch, vec["g1"], vec["s1"])
+    low = first.astype(bf16)
+
+    pltpu.make_async_copy(inner_w, inner_w, in_sems.at[1]).wait()
+    pltpu.make_async_copy(outer_w, outer_w, in_sems.at[2]).wait()
+
+    def forward(s, ffn):
+        at = pl.ds(pl.multiple_of(slot_w * s, TILE), slot_w)
+        inner = plain_product(low, inner_w[:, at]) + inner_bias[:, at]
+        cdf = 0.5 + 0.5 * lax.erf(inner * (0.5**0.5))
+        active = (inner * cdf).astype(bf16)
+        hidden[:, at] = active
+        slope[:, at] = cdf + inner * (jnp.exp(-0.5 * inner * inner) * (0.5 / jnp.pi) ** 0.5)
+        return ffn + plain_product(active, outer_w[at, :])
+
+    ffn = lax.fori_loop(0, 2 * CHIPS, forward, jnp.broadcast_to(vec["outerb"], (tok, dmod)))
+    second, unit_two, inverse_two = normed(first + ffn, vec["g2"], vec["s2"])
+    result[...] = second.astype(bf16)
+    grad_out = cotangent[...].astype(f32)
+    grad_two = normed_back(grad_out, unit_two, inverse_two, vec["g2"])
+    low_two = grad_two.astype(bf16)
+
+    sums[...] = jnp.zeros_like(sums)
+
+    def put(row, value):
+        for v in range(2):
+            for z in range(parts):
+                sums[z, row + v : row + v + 1, :] = value[:, slot_w * v : slot_w * (v + 1)]
+
+    put(6, summed_rows(low_two.astype(f32)))
+    put(8, summed_rows(grad_out * unit_two))
+    put(10, summed_rows(grad_out))
+    low_turned = low.astype(f32).T.astype(bf16)
+
+    def backward(s, grad_first):
+        at = pl.ds(pl.multiple_of(slot_w * s, TILE), slot_w)
+        grad_hidden = lanes_product(low_two, outer_w[at, :])
+        grad_inner = (grad_hidden * slope[:, at]).astype(bf16)
+        outer_g[at, :] = rows_product(hidden[:, at], low_two).astype(bf16)
+        inner_g[:, at] = plain_product(low_turned, grad_inner).astype(bf16)
+        sums[s // 2, pl.ds(12 + lax.rem(s, 2), 1), :] = summed_rows(grad_inner.astype(f32))
+        return grad_first + lanes_product(grad_inner, inner_w[:, at])
+
+    grad_first = lax.fori_loop(0, 2 * CHIPS, backward, grad_two)
+
+    def targets():
+        for m in range(CHIPS):
+            far = sent_far if m == CHIPS - 1 else sent_near.at[m]
+            for target, side, sem in ((kept.at[m], core, 0), (far, 1 - core, 1 + (m < CHIPS - 1))):
+                yield target, jnp.bitwise_xor(chip, m), side, sem
+
+    inner_view = inner_g.reshape(parts, rows, ff)
+    outer_view = outer_g.reshape(parts, dmod, dmod)
+    output_view = output_g.reshape(parts, rows, dmod)
+    for target, g, side, sem in targets():
+        s = 2 * g + side
+        pltpu.make_async_copy(
+            inner_view.at[:, :, pl.ds(pl.multiple_of(slot_w * s, TILE), slot_w)],
+            target.at[:, pl.ds(0, rows), :],
+            out_sems.at[sem],
+        ).start()
+        for v in range(2):
+            pltpu.make_async_copy(
+                outer_view.at[:, pl.ds(pl.multiple_of(half * s, 16), half), pl.ds(slot_w * v, slot_w)],
+                target.at[:, pl.ds(rows + half * v, half), :],
+                out_sems.at[sem],
+            ).start()
+
+    put(2, summed_rows(grad_first * unit_one))
+    put(4, summed_rows(grad_first))
+    grad_one = normed_back(grad_first, unit_one, inverse_one, vec["g1"])
+    grad_sum[...] = grad_one
+    low_one = grad_one.astype(bf16)
+    put(0, summed_rows(low_one.astype(f32)))
+    small[0] = jnp.zeros_like(small[0])
+    small[1] = sums[...].astype(bf16)
+    for g in range(CHIPS):
+        at = slice(group * g, group * (g + 1))
+        output_g[at, :] = rows_product(context[g], low_one).astype(bf16)
+        grad_context[g] = lanes_product(low_one, output_w[at, :]).astype(bf16)
+    for target, g, side, sem in targets():
+        pltpu.make_async_copy(
+            output_view.at[
+                :,
+                pl.ds(pl.multiple_of(quarter * g, 16), quarter),
+                pl.ds(pl.multiple_of(slot_w * side, TILE), slot_w),
+            ],
+            target.at[:, pl.ds(2 * rows, quarter), :],
+            out_sems.at[sem],
+        ).start()
+        filled = jnp.where(2 * g + side == 0, 1, 0)
+        pltpu.make_async_copy(
+            small.at[filled], target.at[:, pl.ds(2 * rows + quarter, TAG_ROWS), :], out_sems.at[sem]
+        ).start()
+    for sem, target in enumerate((kept, sent_far, sent_near)):
+        pltpu.make_async_copy(target, target, out_sems.at[sem]).wait()
+
+
+def project_back_kernel(place, tokens, dq, dkv_own, dkv_other, weight, partial, kept, sent, acc, dkv):
+    tok = dq.shape[1]
+    core = place[1]
+    wide = dq.shape[2]
+    parts, rows = kept.shape[0], kept.shape[1] - TAG_ROWS
+    acc[...] = jnp.zeros_like(acc)
+
+    def piece(m, carry):
+        text = tokens[m, :tok]
+        both = dkv_own[m].astype(jnp.float32) + dkv_other[m].astype(jnp.float32)
+        dkv[...] = both.astype(jnp.bfloat16)
+        partial[m] = (
+            lanes_product(dq[m], weight[:, :wide]) + lanes_product(dkv[...], weight[:, wide:])
+        ).astype(jnp.bfloat16)
+        text_turned = text.astype(jnp.float32).T.astype(jnp.bfloat16)
+        acc[:, :wide] += plain_product(text_turned, dq[m])
+        acc[:, wide:] += plain_product(text_turned, dkv[...])
+        return (
+            carry[0] + summed_rows(dq[m].astype(jnp.float32)),
+            carry[1] + summed_rows(dkv[...].astype(jnp.float32)),
+        )
+
+    start = (jnp.zeros((1, wide), jnp.float32), jnp.zeros((1, wide // 2), jnp.float32))
+    sums = jnp.concatenate(lax.fori_loop(0, CHIPS, piece, start), axis=1)
+    sums = jnp.broadcast_to(sums, (TAG_ROWS, sums.shape[1]))
+    for z in range(parts):
+        for target, side in ((kept, core), (sent, 1 - core)):
+            at = pl.ds(pl.multiple_of(2 * rows * z + rows * side, 32), rows)
+            target[z, :rows] = acc[at, :].astype(jnp.bfloat16)
+            target[z, rows:] = jnp.where(side == 0, sums, 0.0).astype(jnp.bfloat16)
+
+
+def picked_piece(place, own, other, g, side, rows):
+    m = jnp.bitwise_xor(place[0], g)
+    here = own[m, rows, :].astype(jnp.float32)
+    there = other[m, rows, :].astype(jnp.float32)
+    return jnp.where(place[1] == side, here, there)
+
+
+def unpack_dense_kernel(place, own, other, inner, outer, output, small):
+    rows = inner.shape[0]
+    half, quarter = rows // 2, rows // CHIPS
+    slot_w = own.shape[2]
+    for g in range(CHIPS):
+        for side in range(2):
+            s = 2 * g + side
+            at = slice(slot_w * s, slot_w * (s + 1))
+            inner[:, at] = picked_piece(place, own, other, g, side, slice(0, rows))
+            for v in range(2):
+                outer[half * s : half * (s + 1), slot_w * v : slot_w * (v + 1)] = picked_piece(
+                    place, own, other, g, side, slice(rows + half * v, rows + half * (v + 1))
+                )
+            output[quarter * g : quarter * (g + 1), slot_w * side : slot_w * (side + 1)] = picked_piece(
+                place, own, other, g, side, slice(2 * rows, 2 * rows + quarter)
+            )
+    small[...] = picked_piece(place, own, other, 0, 0, slice(2 * rows + quarter, own.shape[1]))
+
+
+def unpack_heads_kernel(place, own, other, ww, we, ew, ee, key, value, sums):
+    rows = own.shape[1] - TAG_ROWS
+    wide = 4 * 3 * HD
+    for side in range(2):
+        at = slice(rows * side, rows * (side + 1))
+        pieces = [picked_piece(place, own, other, g, side, slice(0, rows)) for g in range(CHIPS)]
+        for k, target in enumerate((ww, we, ew, ee)):
+            target[at, :] = jnp.concatenate(
+                [p[:, HD * (4 * h + k) : HD * (4 * h + k + 1)] for p in pieces for h in range(3)], axis=1
+            )
+        for k, target in enumerate((key, value)):
+            target[at, :] = jnp.concatenate(
+                [
+                    p[:, wide + HD * (2 * h + k) : wide + HD * (2 * h + k + 1)]
+                    for p in pieces
+                    for h in range(3)
+                ],
+                axis=1,
+            )
+    sums[...] = picked_piece(place, own, other, place[2], 0, slice(rows, rows + TAG_ROWS))
+
+
+def smem():
+    return pl.BlockSpec(memory_space=pltpu.SMEM)
+
+
+def vmem():
+    return pl.BlockSpec(memory_space=pltpu.VMEM)
+
+
+def hbm():
+    return pl.BlockSpec(memory_space=pl.ANY)
+
+
+def whole_call(kernel, operands, outs, scratch=(), flops=0, nbytes=0, exps=0):
+    return pl.pallas_call(
+        kernel,
+        out_shape=[jax.ShapeDtypeStruct(shape, dtype) for shape, dtype, _ in outs],
+        in_specs=[spec() for _, spec in operands],
+        out_specs=[spec() for _, _, spec in outs],
+        scratch_shapes=list(scratch),
+        compiler_params=pltpu.CompilerParams(vmem_limit_bytes=58 << 20),
+        cost_estimate=pl.CostEstimate(flops=flops, bytes_accessed=nbytes, transcendentals=exps),
+    )(*(value for value, _ in operands))
+
+
+def grouped_device(
+    tokens,
+    cotangent,
+    segment_ids,
+    token_types,
+    query_wordword,
+    query_wordentity,
+    query_entityword,
+    query_entityentity,
+    bias_wordword,
+    bias_wordentity,
+    bias_entityword,
+    bias_entityentity,
+    key_weight,
+    value_weight,
+    value_bias,
+    output_weight,
+    output_bias,
+    first_gain,
+    first_bias,
+    inner_weight,
+    inner_bias,
+    outer_weight,
+    outer_bias,
+    second_gain,
+    second_bias,
+):
+    bf16, f32 = jnp.bfloat16, jnp.float32
+    index = lax.axis_index("ctx")
+    chip, core = index // 2, index % 2
+    wa = lax.axis_index("wa")
+    parts = lax.axis_size("wa")
+    place = jnp.stack([chip, core, wa]).astype(jnp.int32)
+    inputs = tokens[0]
+    tok, dmod = inputs.shape
+    length = 2 * CHIPS * tok
+    rows = key_weight.shape[0]
+    half, quarter = rows // 2, rows // CHIPS
+    group = dmod // CHIPS
+    ff = inner_weight.shape[1]
+    slot_w = ff // (2 * CHIPS)
+
+    tags = (segment_ids[0] * 2 + token_types[0]).astype(bf16)
+    tag_rows = jnp.pad(tags[None], ((0, TAG_ROWS - 1), (0, dmod - tok)))
+    text = jnp.concatenate([inputs, tag_rows], axis=0)
+    cut = tok // 2
+    text_x, text_y = swapped(text, 2), swapped(text, 4)
+    text_far = swapped(text_x[:cut], 4), swapped(text_y[cut:], 2)
+
+    six = (query_wordword, query_wordentity, query_entityword, query_entityentity, key_weight, value_weight)
+    cols = [lax.dynamic_slice(w, (half * core, group * chip), (half, group)).reshape(half, 3, HD) for w in six]
+    queries = [b.reshape(1, 3, HD) for b in (bias_wordword, bias_wordentity, bias_entityword, bias_entityentity)]
+    lone = value_bias.reshape(1, 3, HD)
+    by_head = [
+        (jnp.stack(cols[:4], axis=2), jnp.stack(cols[4:], axis=2)),
+        (jnp.stack(queries, axis=2), jnp.stack([jnp.zeros_like(lone), lone], axis=2)),
+    ]
+    mine = [jnp.concatenate([a.reshape(a.shape[0], -1), b.reshape(b.shape[0], -1)], axis=1) for a, b in by_head]
+    six_vectors = jnp.concatenate([output_bias, first_gain, first_bias, outer_bias, second_gain, second_bias])
+    mine += [six_vectors[None], jnp.pad(inner_bias, (0, 6 * group - inner_bias.shape[0]))[None]]
+    mine.append(jnp.zeros((TAG_ROWS - 3, 6 * group), bf16))
+    mine = jnp.concatenate(mine, axis=0)
+    mine = jnp.stack([mine] + [turned(mine, k) for k in range(1, parts)])
+    theirs = swapped(mine, 1)
+    order = (wa - jnp.arange(parts)) % parts
+    vectors = jnp.take(mine[:, half + 1], order, axis=0).reshape(parts, 6, rows)
+    vectors = jnp.pad(jnp.transpose(vectors, (1, 0, 2)).reshape(6, dmod), ((0, 2), (0, 0))).astype(f32)
+    full_inner_bias = jnp.take(mine[:, half + 2, : ff // parts], order, axis=0).reshape(1, ff).astype(f32)
+
+    slot = jnp.concatenate(
+        [
+            lax.dynamic_slice(inner_weight, (0, slot_w * index), (rows, slot_w)),
+            lax.dynamic_slice(outer_weight, (half * index, 0), (half, slot_w)),
+            lax.dynamic_slice(outer_weight, (half * index, slot_w), (half, slot_w)),
+            lax.dynamic_slice(output_weight, (quarter * chip, slot_w * core), (quarter, slot_w)),
+        ],
+        axis=0,
+    )
+    slots = [slot] + [turned(slot, k) for k in range(1, parts)]
+
+    def chip_stacked(value):
+        middle = value.shape[0] // 2
+        along_x, along_y = swapped(value, 2), swapped(value, 4)
+        across = jnp.concatenate([swapped(along_x[:middle], 4), swapped(along_y[middle:], 2)], axis=0)
+        stacked = jnp.stack([value, along_x, along_y, across])
+        return stacked, swapped(stacked, 1)
+
+    near_slots = chip_stacked(jnp.stack(slots[:2]))
+    far_slots = chip_stacked(jnp.stack(slots[2:]))
+
+    weight, all_text, q, kv = whole_call(
+        project_kernel,
+        [(place, smem)] + [(a, vmem) for a in (text, text_x, text_y, *text_far, mine, theirs)],
+        [
+            ((dmod, 6 * group), bf16, vmem),
+            ((CHIPS, tok + TAG_ROWS, dmod), bf16, vmem),
+            ((CHIPS, tok, 2 * group), bf16, vmem),
+            ((CHIPS, tok + TAG_ROWS, 2 * group), bf16, vmem),
+        ],
+        flops=2 * CHIPS * tok * dmod * 6 * group,
+        nbytes=12 << 20,
+    )
+    kv_other = swapped(kv, 1)
+
+    context, turned_out, lse, bounds = whole_call(
+        attend_kernel,
+        [(place, smem), (q, vmem), (kv, vmem), (kv_other, vmem)],
+        [
+            ((CHIPS, tok, group), bf16, vmem),
+            ((CHIPS, group, tok), f32, vmem),
+            ((CHIPS, 3, 1, tok), f32, vmem),
+            ((2, CHIPS), jnp.int32, smem),
+        ],
+        [
+            pltpu.VMEM((3, length, 2 * HD), bf16),
+            pltpu.VMEM((3, HD, length), bf16),
+            pltpu.VMEM((length, TILE), f32),
+            pltpu.VMEM((2 * CHIPS, 8, tok), f32),
+            pltpu.VMEM((3, HD, tok), f32),
+        ],
+        flops=4 * CHIPS * tok * length * group // 2,
+        nbytes=8 << 20,
+        exps=CHIPS * tok * length * 3 // 2,
+    )
+    same_core = [[2 * i + k for i in range(CHIPS)] for k in range(2)]
+
+    def exchanged(value):
+        return lax.all_to_all(
+            value, "ctx", split_axis=0, concat_axis=0, tiled=True, axis_index_groups=same_core
+        )
+
+    slot_rows = 2 * rows + quarter + TAG_ROWS
+    result, grad_sum, grad_context, kept, sent_far, sent_near = whole_call(
+        dense_kernel,
+        [(place, smem)]
+        + [(a, vmem) for a in (exchanged(context), text, cotangent[0], vectors, full_inner_bias)]
+        + [(a, hbm) for a in (*near_slots, *far_slots)],
+        [
+            ((tok, dmod), bf16, vmem),
+            ((tok, dmod), f32, vmem),
+            ((CHIPS, tok, group), bf16, vmem),
+            ((CHIPS, parts, slot_rows, slot_w), bf16, hbm),
+            ((parts, slot_rows, slot_w), bf16, hbm),
+            ((CHIPS - 1, parts, slot_rows, slot_w), bf16, hbm),
+        ],
+        [
+            pltpu.VMEM((dmod, ff), bf16),
+            pltpu.VMEM((ff, dmod), bf16),
+            pltpu.VMEM((dmod, dmod), bf16),
+            pltpu.VMEM((tok, ff), bf16),
+            pltpu.VMEM((tok, ff), f32),
+            pltpu.VMEM((dmod, ff), bf16),
+            pltpu.VMEM((ff, dmod), bf16),
+            pltpu.VMEM((dmod, dmod), bf16),
+            pltpu.VMEM((2, parts, TAG_ROWS, slot_w), bf16),
+            pltpu.VMEM((parts, TAG_ROWS, slot_w), f32),
+            pltpu.SemaphoreType.DMA((3,)),
+            pltpu.SemaphoreType.DMA((3,)),
+        ],
+        flops=6 * tok * dmod * (dmod + 2 * ff),
+        nbytes=26 << 20,
+        exps=2 * tok * ff,
+    )
+    grad_context = exchanged(grad_context)
+
+    dq, dkv, dkv_sent = whole_call(
+        attend_back_kernel,
+        [(place, smem), (bounds, smem)]
+        + [(a, vmem) for a in (q, kv, kv_other, turned_out, lse, grad_context)],
+        [
+            ((CHIPS, tok, 4 * group), bf16, vmem),
+            ((CHIPS, tok, 2 * group), bf16, vmem),
+            ((CHIPS, tok, 2 * group), bf16, vmem),
+        ],
+        [
+            pltpu.VMEM((3, length, 2 * HD), bf16),
+            pltpu.VMEM((3, 2 * HD, length), bf16),
+            pltpu.VMEM((3, length, 2 * HD), bf16),
+            pltpu.VMEM((3, length, 2 * HD), f32),
+            pltpu.VMEM((3, length, 2 * HD), f32),
+            pltpu.VMEM((length, TILE), f32),
+            pltpu.VMEM((2 * CHIPS, 8, tok), f32),
+            pltpu.VMEM((3, 2 * HD, tok), f32),
+        ],
+        flops=10 * CHIPS * tok * length * group // 2,
+        nbytes=16 << 20,
+        exps=CHIPS * tok * length * 3 // 2,
+    )
+    partial, head_kept, head_sent = whole_call(
+        project_back_kernel,
+        [(place, smem)] + [(a, vmem) for a in (all_text, dq, dkv, swapped(dkv_sent, 1), weight)],
+        [
+            ((CHIPS, tok, dmod), bf16, vmem),
+            ((parts, half + TAG_ROWS, 6 * group), bf16, vmem),
+            ((parts, half + TAG_ROWS, 6 * group), bf16, vmem),
+        ],
+        [pltpu.VMEM((dmod, 6 * group), f32), pltpu.VMEM((tok, 2 * group), bf16)],
+        flops=4 * CHIPS * tok * dmod * 6 * group,
+        nbytes=16 << 20,
+    )
+
+    def added(*values):
+        total = values[0].astype(f32)
+        for v in values[1:]:
+            total = total + v.astype(f32)
+        return total
+
+    def chips_summed(far, near, to):
+        middle = far.shape[0] // 2
+        from_x, from_y = swapped(far[:middle], 2), swapped(far[middle:], 4)
+        x0, x1 = near(1, slice(0, middle)), near(1, slice(middle, None))
+        y0, y1 = near(2, slice(0, middle)), near(2, slice(middle, None))
+        x0 = swapped(added(*x0).astype(bf16), 2)
+        y1 = swapped(added(*y1).astype(bf16), 4)
+        x1 = swapped(added(*x1, from_y).astype(bf16), 2)
+        y0 = swapped(added(*y0, from_x).astype(bf16), 4)
+        low = added(*near(0, slice(0, middle)), x0, y0).astype(to)
+        high = added(*near(0, slice(middle, None)), x1, y1).astype(to)
+        return low, high
+
+    def parts_summed(value):
+        total = [lax.dynamic_index_in_dim(value, wa, 0, keepdims=False)]
+        for k in range(1, parts):
+            total.append(turned(lax.dynamic_index_in_dim(value, (wa + k) % parts, 0, keepdims=False), k))
+        return added(*total).astype(bf16)
+
+    far = added(kept[CHIPS - 1], swapped(sent_far, 1)).astype(bf16)
+    received = swapped(sent_near, 1)
+    low, high = chips_summed(far, lambda m, at: (kept[m, at], received[m, at]), bf16)
+    summed = parts_summed(jnp.concatenate([low, high], axis=0))
+    out_inner, out_outer, out_output, small = whole_call(
+        unpack_dense_kernel,
+        [(place, smem)] + [(a, vmem) for a in chip_stacked(summed)],
+        [
+            ((rows, ff), f32, vmem),
+            (outer_weight.shape, f32, vmem),
+            ((rows, dmod), f32, vmem),
+            ((TAG_ROWS, slot_w), f32, vmem),
+        ],
+        nbytes=8 << 20,
+    )
+
+    summed = parts_summed(added(head_kept, swapped(head_sent, 1)).astype(bf16))
+    *out_heads, sums = whole_call(
+        unpack_heads_kernel,
+        [(place, smem)] + [(a, vmem) for a in chip_stacked(summed)],
+        [((rows, dmod), f32, vmem) for _ in range(6)] + [((TAG_ROWS, 6 * group), f32, vmem)],
+        nbytes=8 << 20,
+    )
+    low, high = chips_summed(partial[CHIPS - 1], lambda m, at: (partial[m, at],), f32)
+    input_grads = grad_sum + jnp.concatenate([low, high], axis=0)
+
+    sum_q = sums[0, : 4 * group].reshape(3, 4, HD)
+    sum_v = sums[0, 4 * group :].reshape(3, 2, HD)[:, 1].reshape(rows)
+    own_small = lax.dynamic_slice(small[:12].reshape(6, dmod), (0, wa * rows), (6, rows))
+    return (
+        result[None],
+        input_grads[None],
+        *out_heads[:4],
+        *(sum_q[:, k].reshape(rows) for k in range(4)),
+        *out_heads[4:],
+        sum_v,
+        out_output,
+        own_small[0],
+        own_small[1],
+        own_small[2],
+        out_inner,
+        small[12:14].reshape(ff // parts),
+        out_outer,
+        own_small[3],
+        own_small[4],
+        own_small[5],
+    )
+
+
 def solution(mesh):
     in_specs = (
         P("wa", "ctx", None),
@@ -506,6 +1342,7 @@
         P("wa"),
         P("wa"),
     )
+    body = grouped_device if mesh.shape["ctx"] == 2 * CHIPS else windowed_device
     return jax.shard_map(
-        per_device, mesh=mesh, in_specs=in_specs, out_specs=out_specs, check_vma=False
-    )
+        body, mesh=mesh, in_specs=in_specs, out_specs=out_specs, check_vma=False
+    )

time: 1750 us -> 413 us (0.24)
  matrix products: 474 us -> 0 us
  waiting for transfers between devices: 483 us -> 138 us
  local copies, waits for them, and re-layouts: 297 us -> 33.6 us
  blocking collectives: 240 us -> 10.8 us
  Pallas kernels: 0 us -> 129 us
  other arithmetic: 92.1 us -> 27.6 us
  loops' own time: 41.5 us -> 0 us
    dot_general x159 -> x0, matrix products: 474 us -> none  [the longest x69 262 us: right_product(): lax.dot_general(left, right, (((1,), (1,)), ((), ())), preferred_element_...]
    reduce_scatter x3 -> x0, waiting for transfers between devices: 205 us -> none  [the longest x1 88.2 us: per_device(): lax.psum_scatter(local_grads[15].astype(jnp.bfloat16), 'wa', scatter_dime...]
    psum x1 -> x0, blocking collectives: 200 us -> none  [per_device(): lax.psum((shards[0], shards[1], shards[2], shards[3], shards[4], shards[5...]
    pallas_call x0 -> x7, Pallas kernels: none -> 129 us  [whole_call(): pl.pallas_call(kernel, out_shape=[jax.ShapeDtypeStruct(shape, dtype) for...]
    unnamed x24 -> x0, waiting for transfers between devices: 99 us -> none
    dynamic_slice x68 -> x9, local copies, waits for them, and re-layouts: 103 us -> 7.74 us  [the longest x6 5.92 us: grouped_device(): lax.dynamic_slice(w, (half * core, group * chip), (half, group))]
    convert_element_type x64 -> x11, other arithmetic: 58.7 us -> 13.1 us  [the longest x1 3.16 us: chips_summed(): y1 = swapped(added(*y1).astype(bf16), 4)]
    another operation x6 -> x0, loops' own time: 41.5 us -> none  [the longest x1 32.3 us: per_device(): lax.map(lambda index: head_backward(index), jnp.arange(heads))]
  transfers between devices with their start and end apart: 50 -> 55, of which waited for: 28 -> 22; matrix products, arithmetic and copies ran while one was open for 20% -> 13% of each run, Pallas kernels for 0% -> 21%
where the time goes in v2:
time: 413 us; the launch traced here: 414 us
  waiting for transfers between devices  138 us (33%)
  Pallas kernels  129 us (31%)
  starting transfers between devices  74.5 us (18%)
  local copies, waits for them, and re-layouts  33.6 us (8%)
  other arithmetic  27.6 us (7%)
  blocking collectives  10.8 us (3%)
    pallas_call x7, Pallas kernels, whole_call(): pl.pallas_call(kernel, out_shape=[jax.ShapeDtypeStruct(shape, dtype) for...  129 us
    ppermute x42, waiting for transfers between devices, swapped(): return lax.ppermute(value, 'ctx', [(i, i ^ step) for i in range(count)])  73.9 us
    ppermute x12, waiting for transfers between devices, turned(): lax.ppermute(value, 'wa', [(i, (i + step) % count) for i in range(count)])  59.7 us
    ppermute x42, starting transfers between devices, swapped(): return lax.ppermute(value, 'ctx', [(i, i ^ step) for i in range(count)])  43.1 us
    ppermute x12, starting transfers between devices, turned(): lax.ppermute(value, 'wa', [(i, (i + step) % count) for i in range(count)])  27.7 us
    all_to_all x1, blocking collectives, exchanged(): lax.all_to_all(value, 'ctx', split_axis=0, concat_axis=0, tiled=True, axi...  10.8 us
    another operation x10, other arithmetic, chip_stacked(): stacked = jnp.stack([value, along_x, along_y, across])  8.55 us
  transfers between devices with their start and end apart: 55, of which 22 were waited for; matrix products, arithmetic and copies ran while one was open for 13% of the time, Pallas kernels for 21%

profile of v2, /device:TPU:9, one launch (start us, length us, event | category | flops | bytes accessed | tf_op | source)
XLA Modules:
  0.0 414.4 jit_solution(5015973225889674423)
XLA Ops:
  13.8 13.2 %collective-permute-done.15 = bf16[432,384]{1,0:T(8,128)(2,1)S(1)} collective-permute-done((bf16[432,384]{1,0:T(8,128)(2,1)S(1)}, bf16[432,384]{1,0:T(8,128)(2,1)S(1)}, u32[]{:S(2)}, u32[]{:S(2)}) %collective-permute-start.15) | collective-permute-done | bytes 331808 | tf_op jit(solution)/shard_map/ppermute | solution.py:488
  26.9 6.2 %collective-permute-done.16 = bf16[432,384]{1,0:T(8,128)(2,1)S(1)} collective-permute-done((bf16[432,384]{1,0:T(8,128)(2,1)S(1)}, bf16[432,384]{1,0:T(8,128)(2,1)S(1)}, u32[]{:S(2)}, u32[]{:S(2)}) %collective-permute-start.16) | collective-permute-done | bytes 331808 | tf_op jit(solution)/shard_map/ppermute | solution.py:488
  41.3 8.1 %collective-permute-done.17 = bf16[2,432,384]{2,1,0:T(8,128)(2,1)S(1)} collective-permute-done((bf16[2,432,384]{2,1,0:T(8,128)(2,1)}, bf16[2,432,384]{2,1,0:T(8,128)(2,1)S(1)}, u32[]{:S(2)}, u32[]{:S(2)}) %collective-permute-start.17) | collective-permute-done | bytes 663584 | tf_op jit(solution)/shard_map/ppermute | solution.py:483
  51.3 14.7 %collective-permute-done.5 = bf16[112,1152]{1,0:T(8,128)(2,1)S(1)} collective-permute-done((bf16[112,1152]{1,0:T(8,128)(2,1)S(1)}, bf16[112,1152]{1,0:T(8,128)(2,1)S(1)}, u32[]{:S(2)}, u32[]{:S(2)}) %collective-permute-start.5) | collective-permute-done | bytes 258080 | tf_op jit(solution)/shard_map/ppermute | solution.py:488
  77.0 14.5 %collective-permute-done.12 = bf16[1,432,384]{2,1,0:T(8,128)(2,1)S(1)} collective-permute-done((bf16[1,432,384]{2,1,0:T(8,128)(2,1)S(1)}, bf16[1,432,384]{2,1,0:T(8,128)(2,1)S(1)}, u32[]{:S(2)}, u32[]{:S(2)}) %collective-permute-start.12) | collective-permute-done | bytes 331808 | tf_op jit(solution)/shard_map/ppermute | solution.py:483
  94.7 3.2 pad_maximum_fusion.near_own
  103.2 6.6 %collective-permute-done.2.t3a = bf16[192,768]{1,0:T(8,128)(2,1)S(1)} collective-permute-done((bf16[192,768]{1,0:T(8,128)(2,1)S(1)}, bf16[192,768]{1,0:T(8,128)(2,1)S(1)}, u32[]{:S(2)}, u32[]{:S(2)}) %collective-permute-start.2) | collective-permute-done | bytes 294944 | tf_op jit(solution)/shard_map/ppermute | solution.py:483
  110.6 8.2 %shard_map.416 = (bf16[768,1152]{1,0:T(8,128)(2,1)}, bf16[4,400,768]{2,1,0:T(8,128)(2,1)}, bf16[4,384,384]{2,1,0:T(8,128)(2,1)}, bf16[4,400,384]{2,1,0:T(8,128)(2,1)}) custom-call(s32[3]{0:T(128)} %pad_add_fusion.place, bf16[400,768]{1,0:T(8,128)(2,1)} %copy-done.7, bf16[400,768]{1,0:T(8,128)(2,1)} %copy-done.10, bf16[400,768]{1,0:T(8,128)(2,1)} %copy-done.9, ...), custom_call_target="tpu_custom_call" | custom-call | flops 2717908992 | bytes 12582912 | tf_op jit(solution)/shard_map/pallas_call | solution.py:1006
  123.7 28.0 %shard_map.417 = (bf16[4,384,192]{2,1,0:T(8,128)(2,1)}, f32[4,192,384]{2,1,0:T(8,128)}, f32[4,3,1,384]{3,2,1,0:T(1,128)}, s32[2,4]{1,0:T(2,128)}) custom-call(s32[3]{0:T(128)} %pad_add_fusion.place, bf16[4,384,384]{2,1,0:T(8,128)(2,1)} %get-tuple-element.54.q_ref, bf16[4,400,384]{2,1,0:T(8,128)(2,1)} %get-tuple-element.55.own, bf16[4,400,384]{2,1,0:T(8,128)(2,1)} %copy-done.21), custom_call_target="tpu_custom_call" | custom-call | flops 1811939328 | bytes 8388608 | tf_op jit(solution)/shard_map/pallas_call | solution.py:1006
  153.9 3.7 all-to-all-start
  160.5 4.4 %all-to-all-done = bf16[4,384,192]{1,2,0:T(8,128)(2,1)S(1)} async-done(((bf16[4,384,192]{1,2,0:T(8,128)(2,1)}), bf16[4,384,192]{1,2,0:T(8,128)(2,1)S(1)}, u32[]{:S(2)}, u32[]{:S(2)}) %all-to-all-start) | async-done | bytes 589856 | tf_op jit(solution)/shard_map/all_to_all | solution.py:1144
  166.1 35.1 %shard_map.418 = (bf16[384,768]{1,0:T(8,128)(2,1)}, f32[384,768]{1,0:T(8,128)}, bf16[4,384,192]{2,1,0:T(8,128)(2,1)}, bf16[4,4,448,384]{3,2,1,0:T(8,128)(2,1)}, ...) custom-call(s32[3]{0:T(128)} %pad_add_fusion.place, bf16[4,384,192]{2,1,0:T(8,128)(2,1)} %copy.76.context, ...), custom_call_target="tpu_custom_call" | custom-call | flops 12230590464 | bytes 27262976 | tf_op jit(solution)/shard_map/pallas_call | solution.py:1006
  204.9 10.8 %all_to_all.10 = bf16[4,384,192]{1,2,0:T(8,128)(2,1)S(1)} all-to-all(bf16[4,384,192]{1,2,0:T(8,128)(2,1)S(1)} %copy.77), channel_id=1, replica_groups={{0,8,16,24},{4,12,20,28},{1,9,17,25},{5,13,21,29},{2,10,18,26},{6,14,22..., dimensions={0} | all-to-all | bytes 1179648 | tf_op jit(solution)/shard_map/all_to_all | solution.py:1144
  219.7 34.5 %shard_map.419 = (bf16[4,384,768]{2,1,0:T(8,128)(2,1)}, bf16[4,384,384]{2,1,0:T(8,128)(2,1)}, bf16[4,384,384]{2,1,0:T(8,128)(2,1)}) custom-call(s32[3]{0:T(128)} %pad_add_fusion.place, s32[2,4]{1,0:T(2,128)} %get-tuple-element.60.bounds, bf16[4,384,384]{2,1,0:T(8,128)(2,1)} %get-tuple-element.54.q_ref, bf16[4,400,384]{2,1,0:T(8,128)(2,1)} %get-tuple-element.55.own, ...), custom_call_target="tpu_custom_call" | custom-call | flops 4529848320 | bytes 16777216 | tf_op jit(solution)/shard_map/pallas_call | solution.py:1006
  254.3 2.8 collective-permute-start.22
  260.9 3.2 fusion.10
  266.1 14.2 %shard_map.420 = (bf16[4,384,768]{2,1,0:T(8,128)(2,1)}, bf16[4,112,1152]{2,1,0:T(8,128)(2,1)}, bf16[4,112,1152]{2,1,0:T(8,128)(2,1)}) custom-call(s32[3]{0:T(128)} %pad_add_fusion.place, bf16[4,400,768]{2,1,0:T(8,128)(2,1)} %get-tuple-element.59.tokens, bf16[4,384,768]{2,1,0:T(8,128)(2,1)} %get-tuple-element.64.dq, ...), custom_call_target="tpu_custom_call" | custom-call | flops 5435817984 | bytes 16777216 | tf_op jit(solution)/shard_map/pallas_call | solution.py:1006
  281.6 7.4 %collective-permute-done.44 = bf16[2,448,384]{2,1,0:T(8,128)(2,1)} collective-permute-done((bf16[2,448,384]{2,1,0:T(8,128)(2,1)}, bf16[2,448,384]{2,1,0:T(8,128)(2,1)}, u32[]{:S(2)}, u32[]{:S(2)}) %collective-permute-start.44) | collective-permute-done | bytes 688160 | tf_op jit(solution)/shard_map/ppermute | solution.py:483
  289.0 2.7 fusion.3
  293.1 9.4 %collective-permute-start.30 = (bf16[112,1152]{1,0:T(8,128)(2,1)S(1)}, bf16[112,1152]{1,0:T(8,128)(2,1)S(1)}, u32[]{:S(2)}, u32[]{:S(2)}) collective-permute-start(bf16[112,1152]{1,0:T(8,128)(2,1)S(1)} %get-tuple-element.106), channel_id=1, source_target_pairs={{0,1},{1,2},{2,3},{3,0},{4,5},{5,6},{6,7},{7,4},{8,9},{9,10},{10,1... | collective-permute-start | bytes 774152 | tf_op jit(solution)/shard_map/ppermute | solution.py:488
  309.7 9.4 %collective-permute-start.46 = (bf16[448,384]{1,0:T(8,128)(2,1)S(1)}, bf16[448,384]{1,0:T(8,128)(2,1)S(1)}, u32[]{:S(2)}, u32[]{:S(2)}) collective-permute-start(bf16[448,384]{1,0:T(8,128)(2,1)S(1)} %get-tuple-element.99), channel_id=1, source_target_pairs={{0,1},{1,2},{2,3},{3,0},{4,5},{5,6},{6,7},{7,4},{8,9},{9,10},{10,1... | collective-permute-start | bytes 1032200 | tf_op jit(solution)/shard_map/ppermute | solution.py:488
  320.6 3.6 collective-permute-done.31
  324.2 17.3 %collective-permute-done.32 = bf16[112,1152]{1,0:T(8,128)(2,1)S(1)} collective-permute-done((bf16[112,1152]{1,0:T(8,128)(2,1)S(1)}, bf16[112,1152]{1,0:T(8,128)(2,1)S(1)}, u32[]{:S(2)}, u32[]{:S(2)}) %collective-permute-start.32) | collective-permute-done | bytes 258080 | tf_op jit(solution)/shard_map/ppermute | solution.py:488
  342.9 5.9 %collective-permute-done.33 = bf16[112,1152]{1,0:T(8,128)(2,1)S(1)} collective-permute-done((bf16[112,1152]{1,0:T(8,128)(2,1)S(1)}, bf16[112,1152]{1,0:T(8,128)(2,1)S(1)}, u32[]{:S(2)}, u32[]{:S(2)}) %collective-permute-start.33) | collective-permute-done | bytes 258080 | tf_op jit(solution)/shard_map/ppermute | solution.py:483
  353.1 3.2 collective-permute-done.48
  358.9 5.9 %collective-permute-done.36 = bf16[56,1152]{1,0:T(8,128)(2,1)S(1)} collective-permute-done((bf16[56,1152]{1,0:T(8,128)(2,1)S(1)}, bf16[56,1152]{1,0:T(8,128)(2,1)S(1)}, u32[]{:S(2)}, u32[]{:S(2)}) %collective-permute-start.36) | collective-permute-done | bytes 129056 | tf_op jit(solution)/shard_map/ppermute | solution.py:483
  365.7 6.4 %collective-permute-done.49 = bf16[448,384]{1,0:T(8,128)(2,1)S(1)} collective-permute-done((bf16[448,384]{1,0:T(8,128)(2,1)S(1)}, bf16[448,384]{1,0:T(8,128)(2,1)S(1)}, u32[]{:S(2)}, u32[]{:S(2)}) %collective-permute-start.49) | collective-permute-done | bytes 344096 | tf_op jit(solution)/shard_map/ppermute | solution.py:483
  373.9 6.2 %collective-permute-done.51 = bf16[224,384]{1,0:T(8,128)(2,1)S(1)} collective-permute-done((bf16[224,384]{1,0:T(8,128)(2,1)S(1)}, bf16[224,384]{1,0:T(8,128)(2,1)S(1)}, u32[]{:S(2)}, u32[]{:S(2)}) %collective-permute-start.51) | collective-permute-done | bytes 172064 | tf_op jit(solution)/shard_map/ppermute | solution.py:483
  380.3 5.5 %collective-permute-start.37 = (bf16[4,112,1152]{2,1,0:T(8,128)(2,1)S(1)}, bf16[4,112,1152]{2,1,0:T(8,128)(2,1)}, u32[]{:S(2)}, u32[]{:S(2)}) collective-permute-start(bf16[4,112,1152]{2,1,0:T(8,128)(2,1)S(1)} %pad_maximum_fusion.4.own), channel_id=1, source_target_pairs={{0,4},{4,0},{8,12},{12,8},{16,20},{20,16},{24,28},{28,24},{1,5},{5... | collective-permute-start | bytes 3096584 | tf_op jit(solution)/shard_map/ppermute | solution.py:483
  387.7 8.2 %collective-permute-done.27 = bf16[192,768]{1,0:T(8,128)(2,1)} collective-permute-done((bf16[192,768]{1,0:T(8,128)(2,1)}, bf16[192,768]{1,0:T(8,128)(2,1)}, u32[]{:S(2)}, u32[]{:S(2)}) %collective-permute-start.27) | collective-permute-done | bytes 294944 | tf_op jit(solution)/shard_map/ppermute | solution.py:483
  398.3 4.0 shard_map.421
  407.2 4.5 %shard_map.422 = (f32[192,3072]{1,0:T(8,128)}, f32[768,768]{1,0:T(8,128)}, f32[192,768]{1,0:T(8,128)}, f32[16,384]{1,0:T(8,128)}) custom-call(s32[3]{0:T(128)} %pad_add_fusion.place, bf16[4,448,384]{2,1,0:T(8,128)(2,1)} %copy-done.2, bf16[4,448,384]{2,1,0:T(8,128)(2,1)} %collective-permute-done.53.other), custom_call_target="tpu_custom_call" | custom-call | bytes 8388608 | tf_op jit(solution)/shard_map/pallas_call | solution.py:1006
  (259 shorter events, 102.1 us)
Async XLA Ops:
  2.9 24.0 %collective-permute-start.15 = (bf16[432,384]{1,0:T(8,128)(2,1)S(1)}, bf16[432,384]{1,0:T(8,128)(2,1)S(1)}, u32[]{:S(2)}, u32[]{:S(2)}) collective-permute-start(bf16[432,384]{1,0:T(8,128)(2,1)S(1)} %get-tuple-element.114), channel_id=1, source_target_pairs={{0,2},{1,3},{2,0},{3,1},{4,6},{5,7},{6,4},{7,5},{8,10},{9,11},{10,... | collective-permute-start | bytes 995336 | tf_op jit(solution)/shard_map/ppermute | solution.py:488
  5.2 27.9 %collective-permute-start.16 = (bf16[432,384]{1,0:T(8,128)(2,1)S(1)}, bf16[432,384]{1,0:T(8,128)(2,1)S(1)}, u32[]{:S(2)}, u32[]{:S(2)}) collective-permute-start(bf16[432,384]{1,0:T(8,128)(2,1)S(1)} %get-tuple-element.114), channel_id=1, source_target_pairs={{0,3},{1,0},{2,1},{3,2},{4,7},{5,4},{6,5},{7,6},{8,11},{9,8},{10,9... | collective-permute-start | bytes 995336 | tf_op jit(solution)/shard_map/ppermute | solution.py:488
  5.4 31.6 %collective-permute-start.9 = (bf16[432,384]{1,0:T(8,128)(2,1)S(1)}, bf16[432,384]{1,0:T(8,128)(2,1)}, u32[]{:S(2)}, u32[]{:S(2)}) collective-permute-start(bf16[432,384]{1,0:T(8,128)(2,1)S(1)} %get-tuple-element.114), channel_id=1, source_target_pairs={{0,1},{1,2},{2,3},{3,0},{4,5},{5,6},{6,7},{7,4},{8,9},{9,10},{10,1... | collective-permute-start | bytes 995336 | tf_op jit(solution)/shard_map/ppermute | solution.py:488
  39.0 30.2 %collective-permute-start.10 = (bf16[2,432,384]{2,1,0:T(8,128)(2,1)}, bf16[2,432,384]{2,1,0:T(8,128)(2,1)}, u32[]{:S(2)}, u32[]{:S(2)}) collective-permute-start(bf16[2,432,384]{2,1,0:T(8,128)(2,1)} %get-tuple-element.112), channel_id=1, source_target_pairs={{0,8},{4,12},{8,0},{12,4},{16,24},{20,28},{24,16},{28,20},{1,9},{5... | collective-permute-start | bytes 1990664 | tf_op jit(solution)/shard_map/ppermute | solution.py:483
  39.2 31.2 %collective-permute-start.11 = (bf16[2,432,384]{2,1,0:T(8,128)(2,1)}, bf16[2,432,384]{2,1,0:T(8,128)(2,1)}, u32[]{:S(2)}, u32[]{:S(2)}) collective-permute-start(bf16[2,432,384]{2,1,0:T(8,128)(2,1)} %get-tuple-element.112), channel_id=1, source_target_pairs={{0,16},{4,20},{8,24},{12,28},{16,0},{20,4},{24,8},{28,12},{1,17},{... | collective-permute-start | bytes 1990664 | tf_op jit(solution)/shard_map/ppermute | solution.py:483
  49.5 16.5 %collective-permute-start.5 = (bf16[112,1152]{1,0:T(8,128)(2,1)S(1)}, bf16[112,1152]{1,0:T(8,128)(2,1)S(1)}, u32[]{:S(2)}, u32[]{:S(2)}) collective-permute-start(bf16[112,1152]{1,0:T(8,128)(2,1)S(1)} %concatenate.40), channel_id=1, source_target_pairs={{0,2},{1,3},{2,0},{3,1},{4,6},{5,7},{6,4},{7,5},{8,10},{9,11},{10,... | collective-permute-start | bytes 774152 | tf_op jit(solution)/shard_map/ppermute | solution.py:488
  49.9 16.9 %collective-permute-start.6 = (bf16[112,1152]{1,0:T(8,128)(2,1)S(1)}, bf16[112,1152]{1,0:T(8,128)(2,1)S(1)}, u32[]{:S(2)}, u32[]{:S(2)}) collective-permute-start(bf16[112,1152]{1,0:T(8,128)(2,1)S(1)} %concatenate.40), channel_id=1, source_target_pairs={{0,3},{1,0},{2,1},{3,2},{4,7},{5,4},{6,5},{7,6},{8,11},{9,8},{10,9... | collective-permute-start | bytes 774152 | tf_op jit(solution)/shard_map/ppermute | solution.py:488
  50.0 23.3 %collective-permute-start.19 = (bf16[1,432,384]{2,1,0:T(8,128)(2,1)S(1)}, bf16[1,432,384]{2,1,0:T(8,128)(2,1)S(1)}, u32[]{:S(2)}, u32[]{:S(2)}) collective-permute-start(bf16[1,432,384]{2,1,0:T(8,128)(2,1)S(1)} %slice.221), channel_id=1, source_target_pairs={{0,16},{4,20},{8,24},{12,28},{16,0},{20,4},{24,8},{28,12},{1,17},{... | collective-permute-start | bytes 995336 | tf_op jit(solution)/shard_map/ppermute | solution.py:483
  66.7 33.0 %collective-permute-start.1 = (bf16[400,768]{1,0:T(8,128)(2,1)S(1)}, bf16[400,768]{1,0:T(8,128)(2,1)S(1)}, u32[]{:S(2)}, u32[]{:S(2)}) collective-permute-start(bf16[400,768]{1,0:T(8,128)(2,1)S(1)} %fusion.14.t0.text), channel_id=1, source_target_pairs={{0,16},{4,20},{8,24},{12,28},{16,0},{20,4},{24,8},{28,12},{1,17},{... | collective-permute-start | bytes 1843208 | tf_op jit(solution)/shard_map/ppermute | solution.py:483
  69.2 31.4 %collective-permute-start = (bf16[400,768]{1,0:T(8,128)(2,1)S(1)}, bf16[400,768]{1,0:T(8,128)(2,1)S(1)}, u32[]{:S(2)}, u32[]{:S(2)}) collective-permute-start(bf16[400,768]{1,0:T(8,128)(2,1)S(1)} %fusion.14.t0.text), channel_id=1, source_target_pairs={{0,8},{4,12},{8,0},{12,4},{16,24},{20,28},{24,16},{28,20},{1,9},{5... | collective-permute-start | bytes 1843208 | tf_op jit(solution)/shard_map/ppermute | solution.py:483
  70.4 39.4 %collective-permute-start.7 = (bf16[4,112,1152]{2,1,0:T(8,128)(2,1)}, bf16[4,112,1152]{2,1,0:T(8,128)(2,1)}, u32[]{:S(2)}, u32[]{:S(2)}) collective-permute-start(bf16[4,112,1152]{2,1,0:T(8,128)(2,1)} %pad_maximum_fusion.3.mine), channel_id=1, source_target_pairs={{0,4},{4,0},{8,12},{12,8},{16,20},{20,16},{24,28},{28,24},{1,5},{5... | collective-permute-start | bytes 3096584 | tf_op jit(solution)/shard_map/ppermute | solution.py:483
  73.3 18.1 %collective-permute-start.12 = (bf16[1,432,384]{2,1,0:T(8,128)(2,1)S(1)}, bf16[1,432,384]{2,1,0:T(8,128)(2,1)S(1)}, u32[]{:S(2)}, u32[]{:S(2)}) collective-permute-start(bf16[1,432,384]{2,1,0:T(8,128)(2,1)S(1)} %slice.219), channel_id=1, source_target_pairs={{0,16},{4,20},{8,24},{12,28},{16,0},{20,4},{24,8},{28,12},{1,17},{... | collective-permute-start | bytes 995336 | tf_op jit(solution)/shard_map/ppermute | solution.py:483
  74.3 20.3 %collective-permute-start.13 = (bf16[1,432,384]{2,1,0:T(8,128)(2,1)S(1)}, bf16[1,432,384]{2,1,0:T(8,128)(2,1)S(1)}, u32[]{:S(2)}, u32[]{:S(2)}) collective-permute-start(bf16[1,432,384]{2,1,0:T(8,128)(2,1)S(1)} %slice.220), channel_id=1, source_target_pairs={{0,8},{4,12},{8,0},{12,4},{16,24},{20,28},{24,16},{28,20},{1,9},{5... | collective-permute-start | bytes 995336 | tf_op jit(solution)/shard_map/ppermute | solution.py:483
  91.5 74.6 %collective-permute-start.21 = (bf16[4,2,432,384]{3,2,1,0:T(8,128)(2,1)}, bf16[4,2,432,384]{3,2,1,0:T(8,128)(2,1)}, u32[]{:S(2)}, u32[]{:S(2)}) collective-permute-start(bf16[4,2,432,384]{3,2,1,0:T(8,128)(2,1)} %pad_maximum_fusion.1.far_own), channel_id=1, source_target_pairs={{0,4},{4,0},{8,12},{12,8},{16,20},{20,16},{24,28},{28,24},{1,5},{5... | collective-permute-start | bytes 7962632 | tf_op jit(solution)/shard_map/ppermute | solution.py:483
  97.9 68.2 %collective-permute-start.14 = (bf16[4,2,432,384]{3,2,1,0:T(8,128)(2,1)}, bf16[4,2,432,384]{3,2,1,0:T(8,128)(2,1)}, u32[]{:S(2)}, u32[]{:S(2)}) collective-permute-start(bf16[4,2,432,384]{3,2,1,0:T(8,128)(2,1)} %pad_maximum_fusion.near_own), channel_id=1, source_target_pairs={{0,4},{4,0},{8,12},{12,8},{16,20},{20,16},{24,28},{28,24},{1,5},{5... | collective-permute-start | bytes 7962632 | tf_op jit(solution)/shard_map/ppermute | solution.py:483
  201.2 56.2 %collective-permute-start.38 = (bf16[3,4,448,384]{3,2,1,0:T(8,128)(2,1)}, bf16[3,4,448,384]{3,2,1,0:T(8,128)(2,1)}, u32[]{:S(2)}, u32[]{:S(2)}) collective-permute-start(bf16[3,4,448,384]{3,2,1,0:T(8,128)(2,1)} %get-tuple-element.79), channel_id=1, source_target_pairs={{0,4},{4,0},{8,12},{12,8},{16,20},{20,16},{24,28},{28,24},{1,5},{5... | collective-permute-start | bytes 12386312 | tf_op jit(solution)/shard_map/ppermute | solution.py:483
  218.7 38.6 %collective-permute-start.43 = (bf16[2,448,384]{2,1,0:T(8,128)(2,1)S(1)}, bf16[2,448,384]{2,1,0:T(8,128)(2,1)S(1)}, u32[]{:S(2)}, u32[]{:S(2)}) collective-permute-start(bf16[2,448,384]{2,1,0:T(8,128)(2,1)S(1)} %get-tuple-element.102), channel_id=1, source_target_pairs={{0,16},{4,20},{8,24},{12,28},{16,0},{20,4},{24,8},{28,12},{1,17},{... | collective-permute-start | bytes 2064392 | tf_op jit(solution)/shard_map/ppermute | solution.py:483
  257.0 24.6 %collective-permute-start.41 = (bf16[2,448,384]{2,1,0:T(8,128)(2,1)S(1)}, bf16[2,448,384]{2,1,0:T(8,128)(2,1)S(1)}, u32[]{:S(2)}, u32[]{:S(2)}) collective-permute-start(bf16[2,448,384]{2,1,0:T(8,128)(2,1)S(1)} %get-tuple-element.103), channel_id=1, source_target_pairs={{0,8},{4,12},{8,0},{12,4},{16,24},{20,28},{24,16},{28,20},{1,9},{5... | collective-permute-start | bytes 2064392 | tf_op jit(solution)/shard_map/ppermute | solution.py:483
  259.7 29.2 %collective-permute-start.44 = (bf16[2,448,384]{2,1,0:T(8,128)(2,1)}, bf16[2,448,384]{2,1,0:T(8,128)(2,1)}, u32[]{:S(2)}, u32[]{:S(2)}) collective-permute-start(bf16[2,448,384]{2,1,0:T(8,128)(2,1)} %fusion.1), channel_id=1, source_target_pairs={{0,8},{4,12},{8,0},{12,4},{16,24},{20,28},{24,16},{28,20},{1,9},{5... | collective-permute-start | bytes 2064392 | tf_op jit(solution)/shard_map/ppermute | solution.py:483
  264.1 24.9 %collective-permute-start.45 = (bf16[2,448,384]{2,1,0:T(8,128)(2,1)}, bf16[2,448,384]{2,1,0:T(8,128)(2,1)}, u32[]{:S(2)}, u32[]{:S(2)}) collective-permute-start(bf16[2,448,384]{2,1,0:T(8,128)(2,1)} %get-tuple-element.91), channel_id=1, source_target_pairs={{0,16},{4,20},{8,24},{12,28},{16,0},{20,4},{24,8},{28,12},{1,17},{... | collective-permute-start | bytes 2064392 | tf_op jit(solution)/shard_map/ppermute | solution.py:483
  281.2 23.8 %collective-permute-start.39 = (bf16[2,448,384]{2,1,0:T(8,128)(2,1)}, bf16[2,448,384]{2,1,0:T(8,128)(2,1)S(1)}, u32[]{:S(2)}, u32[]{:S(2)}) collective-permute-start(bf16[2,448,384]{2,1,0:T(8,128)(2,1)} %get-tuple-element.92), channel_id=1, source_target_pairs={{0,8},{4,12},{8,0},{12,4},{16,24},{20,28},{24,16},{28,20},{1,9},{5... | collective-permute-start | bytes 2064392 | tf_op jit(solution)/shard_map/ppermute | solution.py:483
  293.1 26.0 %collective-permute-start.30 = (bf16[112,1152]{1,0:T(8,128)(2,1)S(1)}, bf16[112,1152]{1,0:T(8,128)(2,1)S(1)}, u32[]{:S(2)}, u32[]{:S(2)}) collective-permute-start(bf16[112,1152]{1,0:T(8,128)(2,1)S(1)} %get-tuple-element.106), channel_id=1, source_target_pairs={{0,1},{1,2},{2,3},{3,0},{4,5},{5,6},{6,7},{7,4},{8,9},{9,10},{10,1... | collective-permute-start | bytes 774152 | tf_op jit(solution)/shard_map/ppermute | solution.py:488
  302.5 21.7 %collective-permute-start.31 = (bf16[112,1152]{1,0:T(8,128)(2,1)S(1)}, bf16[112,1152]{1,0:T(8,128)(2,1)S(1)}, u32[]{:S(2)}, u32[]{:S(2)}) collective-permute-start(bf16[112,1152]{1,0:T(8,128)(2,1)S(1)} %get-tuple-element.108), channel_id=1, source_target_pairs={{0,2},{1,3},{2,0},{3,1},{4,6},{5,7},{6,4},{7,5},{8,10},{9,11},{10,... | collective-permute-start | bytes 774152 | tf_op jit(solution)/shard_map/ppermute | solution.py:488
  303.6 37.9 %collective-permute-start.32 = (bf16[112,1152]{1,0:T(8,128)(2,1)S(1)}, bf16[112,1152]{1,0:T(8,128)(2,1)S(1)}, u32[]{:S(2)}, u32[]{:S(2)}) collective-permute-start(bf16[112,1152]{1,0:T(8,128)(2,1)S(1)} %get-tuple-element.107), channel_id=1, source_target_pairs={{0,3},{1,0},{2,1},{3,2},{4,7},{5,4},{6,5},{7,6},{8,11},{9,8},{10,9... | collective-permute-start | bytes 774152 | tf_op jit(solution)/shard_map/ppermute | solution.py:488
  309.7 40.7 %collective-permute-start.46 = (bf16[448,384]{1,0:T(8,128)(2,1)S(1)}, bf16[448,384]{1,0:T(8,128)(2,1)S(1)}, u32[]{:S(2)}, u32[]{:S(2)}) collective-permute-start(bf16[448,384]{1,0:T(8,128)(2,1)S(1)} %get-tuple-element.99), channel_id=1, source_target_pairs={{0,1},{1,2},{2,3},{3,0},{4,5},{5,6},{6,7},{7,4},{8,9},{9,10},{10,1... | collective-permute-start | bytes 1032200 | tf_op jit(solution)/shard_map/ppermute | solution.py:488
  319.1 33.6 %collective-permute-start.47 = (bf16[448,384]{1,0:T(8,128)(2,1)S(1)}, bf16[448,384]{1,0:T(8,128)(2,1)S(1)}, u32[]{:S(2)}, u32[]{:S(2)}) collective-permute-start(bf16[448,384]{1,0:T(8,128)(2,1)S(1)} %get-tuple-element.100), channel_id=1, source_target_pairs={{0,2},{1,3},{2,0},{3,1},{4,6},{5,7},{6,4},{7,5},{8,10},{9,11},{10,... | collective-permute-start | bytes 1032200 | tf_op jit(solution)/shard_map/ppermute | solution.py:488
  319.2 37.1 %collective-permute-start.48 = (bf16[448,384]{1,0:T(8,128)(2,1)S(1)}, bf16[448,384]{1,0:T(8,128)(2,1)S(1)}, u32[]{:S(2)}, u32[]{:S(2)}) collective-permute-start(bf16[448,384]{1,0:T(8,128)(2,1)S(1)} %get-tuple-element.101), channel_id=1, source_target_pairs={{0,3},{1,0},{2,1},{3,2},{4,7},{5,4},{6,5},{7,6},{8,11},{9,8},{10,9... | collective-permute-start | bytes 1032200 | tf_op jit(solution)/shard_map/ppermute | solution.py:488
  349.6 36.5 %collective-permute-start.23 = (bf16[192,768]{1,0:T(8,128)(2,1)S(1)}, bf16[192,768]{1,0:T(8,128)(2,1)S(1)}, u32[]{:S(2)}, u32[]{:S(2)}) collective-permute-start(bf16[192,768]{1,0:T(8,128)(2,1)S(1)} %get-tuple-element.95), channel_id=1, source_target_pairs={{0,8},{4,12},{8,0},{12,4},{16,24},{20,28},{24,16},{28,20},{1,9},{5... | collective-permute-start | bytes 884744 | tf_op jit(solution)/shard_map/ppermute | solution.py:483
  357.8 28.4 %collective-permute-start.26 = (bf16[192,768]{1,0:T(8,128)(2,1)S(1)}, bf16[192,768]{1,0:T(8,128)(2,1)S(1)}, u32[]{:S(2)}, u32[]{:S(2)}) collective-permute-start(bf16[192,768]{1,0:T(8,128)(2,1)S(1)} %get-tuple-element.97), channel_id=1, source_target_pairs={{0,16},{4,20},{8,24},{12,28},{16,0},{20,4},{24,8},{28,12},{1,17},{... | collective-permute-start | bytes 884744 | tf_op jit(solution)/shard_map/ppermute | solution.py:483
  364.8 21.4 %collective-permute-start.25 = (bf16[192,768]{1,0:T(8,128)(2,1)S(1)}, bf16[192,768]{1,0:T(8,128)(2,1)S(1)}, u32[]{:S(2)}, u32[]{:S(2)}) collective-permute-start(bf16[192,768]{1,0:T(8,128)(2,1)S(1)} %fusion.17), channel_id=1, source_target_pairs={{0,16},{4,20},{8,24},{12,28},{16,0},{20,4},{24,8},{28,12},{1,17},{... | collective-permute-start | bytes 884744 | tf_op jit(solution)/shard_map/ppermute | solution.py:483
  380.3 17.9 %collective-permute-start.37 = (bf16[4,112,1152]{2,1,0:T(8,128)(2,1)S(1)}, bf16[4,112,1152]{2,1,0:T(8,128)(2,1)}, u32[]{:S(2)}, u32[]{:S(2)}) collective-permute-start(bf16[4,112,1152]{2,1,0:T(8,128)(2,1)S(1)} %pad_maximum_fusion.4.own), channel_id=1, source_target_pairs={{0,4},{4,0},{8,12},{12,8},{16,20},{20,16},{24,28},{28,24},{1,5},{5... | collective-permute-start | bytes 3096584 | tf_op jit(solution)/shard_map/ppermute | solution.py:483
  386.1 21.1 %collective-permute-start.53 = (bf16[4,448,384]{2,1,0:T(8,128)(2,1)S(1)}, bf16[4,448,384]{2,1,0:T(8,128)(2,1)}, u32[]{:S(2)}, u32[]{:S(2)}) collective-permute-start(bf16[4,448,384]{2,1,0:T(8,128)(2,1)S(1)} %pad_maximum_fusion.2.own), channel_id=1, source_target_pairs={{0,4},{4,0},{8,12},{12,8},{16,20},{20,16},{24,28},{28,24},{1,5},{5... | collective-permute-start | bytes 4128776 | tf_op jit(solution)/shard_map/ppermute | solution.py:483
  (52 other events, 467.6 us)

commit v3 on v2

--- a/solution.py
+++ b/solution.py
@@ -460,6 +460,7 @@
 NEGATIVE = -1e30
 TAG_ROWS = 16
 TILE = 128
+FLOPS_PER_MICRO = 1_100_000_000
 
 
 def lanes_product(left, right):
@@ -488,12 +489,79 @@
     return lax.ppermute(value, "wa", [(i, (i + step) % count) for i in range(count)])
 
 
+def ring_far(one, three):
+    middle = one.shape[0] // 2
+    return jnp.concatenate([turned(one[:middle], 1), turned(three[middle:], 3)], axis=0)
+
+
 def as_column(row):
     return jnp.broadcast_to(row, (TILE, row.shape[1])).T
 
 
 def segment_of(tag):
     return jnp.floor(tag * 0.5)
+
+
+def prepare_kernel(
+    place, ww, we, ew, ee, key, value, *others
+):
+    *lines, inner, outer, output, mine, slot, sem = others
+    rows = key.shape[0]
+    half, quarter = rows // 2, rows // CHIPS
+    slot_w = slot.shape[1]
+    chip, core = place[0], place[1]
+    index = 2 * chip + core
+    copies = [
+        (inner.at[:, pl.ds(pl.multiple_of(slot_w * index, TILE), slot_w)], slot.at[pl.ds(0, rows), :])
+    ]
+    for v in range(2):
+        copies.append(
+            (
+                outer.at[pl.ds(pl.multiple_of(half * index, 16), half), pl.ds(slot_w * v, slot_w)],
+                slot.at[pl.ds(rows + half * v, half), :],
+            )
+        )
+    copies.append(
+        (
+            output.at[
+                pl.ds(pl.multiple_of(quarter * chip, 16), quarter),
+                pl.ds(pl.multiple_of(slot_w * core, TILE), slot_w),
+            ],
+            slot.at[pl.ds(2 * rows, quarter), :],
+        )
+    )
+    copies = [pltpu.make_async_copy(a, b, sem.at[k]) for k, (a, b) in enumerate(copies)]
+    for copy in copies:
+        copy.start()
+    at = pl.ds(pl.multiple_of(half * core, 16), half)
+    for g in range(CHIPS):
+
+        @pl.when(chip == g)
+        def _():
+            def heads(sources):
+                return jnp.concatenate(
+                    [
+                        w[at, HD * (3 * g + h) : HD * (3 * g + h + 1)].astype(jnp.float32)
+                        for h in range(3)
+                        for w in sources
+                    ],
+                    axis=1,
+                ).astype(jnp.bfloat16)
+
+            mine[:half, : 4 * 3 * HD] = heads((ww, we, ew, ee))
+            mine[:half, 4 * 3 * HD :] = heads((key, value))
+
+    lines = [line[...].astype(jnp.float32).reshape(1, line.shape[0]) for line in lines]
+    bias = [lines[k][:, HD * h : HD * (h + 1)] for h in range(3) for k in range(4)]
+    for h in range(3):
+        bias += [jnp.zeros((1, HD), jnp.float32), lines[4][:, HD * h : HD * (h + 1)]]
+    six = jnp.concatenate(lines[5:11], axis=1)
+    last = jnp.concatenate([lines[11], jnp.zeros((1, 2 * rows), jnp.float32)], axis=1)
+    which = lax.broadcasted_iota(jnp.int32, (TAG_ROWS, 6 * rows), 0)
+    below = jnp.where(which == 0, jnp.concatenate(bias, axis=1), jnp.where(which == 1, six, last))
+    mine[half:] = jnp.where(which < 3, below, 0.0).astype(jnp.bfloat16)
+    for copy in copies:
+        copy.wait()
 
 
 def project_kernel(place, t0, t1, t2, t3a, t3b, mine, theirs, weight, tokens, q_ref, kv_ref):
@@ -577,16 +645,19 @@
             column = seg_col[at, :]
             same = jnp.concatenate([column] * (tok // TILE), axis=1) == seg
             after = []
+            queries = [q_ref[j, :, 2 * HD * h : 2 * HD * (h + 1)] for h in range(3)]
+            scores = [
+                jnp.where(same, lanes_product(keys[h, at, :], queries[h]), NEGATIVE) for h in range(3)
+            ]
+            peaks = [
+                jnp.maximum(carry[2 * h], jnp.max(scores[h], axis=0, keepdims=True)) for h in range(3)
+            ]
+            expo = [jnp.exp(scores[h] - peaks[h]) for h in range(3)]
             for h in range(3):
-                top, total = carry[2 * h], carry[2 * h + 1]
-                scores = lanes_product(keys[h, at, :], q_ref[j, :, 2 * HD * h : 2 * HD * (h + 1)])
-                scores = jnp.where(same, scores, NEGATIVE)
-                peak = jnp.maximum(top, jnp.max(scores, axis=0, keepdims=True))
-                fade = jnp.exp(top - peak)
-                expo = jnp.exp(scores - peak)
-                total = total * fade + jnp.sum(expo, axis=0, keepdims=True)
-                acc[h] = acc[h] * fade + plain_product(values[h, :, at], expo.astype(jnp.bfloat16))
-                after += [peak, total]
+                fade = jnp.exp(carry[2 * h] - peaks[h])
+                total = carry[2 * h + 1] * fade + jnp.sum(expo[h], axis=0, keepdims=True)
+                acc[h] = acc[h] * fade + plain_product(values[h, :, at], expo[h].astype(jnp.bfloat16))
+                after += [peaks[h], total]
             return tuple(after)
 
         start = (jnp.full((1, tok), NEGATIVE, jnp.float32), jnp.zeros((1, tok), jnp.float32)) * 3
@@ -594,7 +665,7 @@
         for h in range(3):
             turned_out[j, HD * h : HD * (h + 1), :] = acc[h] / done[2 * h + 1]
             lse[j, h] = done[2 * h] + jnp.log(done[2 * h + 1])
-        out[j] = turned_out[j].T.astype(jnp.bfloat16)
+        out[jnp.bitwise_xor(place[0], j)] = turned_out[j].T.astype(jnp.bfloat16)
         return 0
 
     lax.fori_loop(0, CHIPS, queries, 0)
@@ -608,7 +679,10 @@
     other,
     turned_out,
     lse,
-    grad,
+    grad0,
+    grad1,
+    grad2,
+    grad3,
     dq_ref,
     dkv_own,
     dkv_other,
@@ -620,10 +694,13 @@
     seg_col,
     seg_row,
     acc,
+    grad,
 ):
     tok = q_ref.shape[1]
     chip, core = place[0], place[1]
     wide = 2 * HD
+    for m, piece in enumerate((grad0, grad1, grad2, grad3)):
+        grad[jnp.bitwise_xor(chip, m)] = piece[...]
 
     def prepare(j, unused):
         for source, side in ((own, core), (other, 1 - core)):
@@ -727,11 +804,17 @@
 
 def dense_kernel(
     place,
-    context,
+    context0,
+    context1,
+    context2,
+    context3,
     text,
     cotangent,
     vectors,
     inner_bias,
+    inner_shard,
+    outer_shard,
+    output_shard,
     near_own,
     near_other,
     far_own,
@@ -766,19 +849,35 @@
     quarter = rows // CHIPS
     slot_w = ff // (2 * CHIPS)
 
+    context = (context0, context1, context2, context3)
+
+    def head_rows(m):
+        return pl.ds(pl.multiple_of(group * jnp.bitwise_xor(chip, m), 64), group)
+
+    pltpu.make_async_copy(
+        output_shard, output_w.at[pl.ds(pl.multiple_of(rows * wa, 16), rows), :], in_sems.at[0]
+    ).start()
+    pltpu.make_async_copy(
+        inner_shard, inner_w.at[pl.ds(pl.multiple_of(rows * wa, 16), rows), :], in_sems.at[1]
+    ).start()
+    pltpu.make_async_copy(
+        outer_shard, outer_w.at[pl.ds(pl.multiple_of(dmod * wa, 16), dmod), :], in_sems.at[2]
+    ).start()
+
     def fetch(m, unused):
         g = jnp.bitwise_xor(chip, m)
-        for source, side, base in (
+        for source, side, far in (
             (near_own, core, 0),
             (near_other, 1 - core, 0),
-            (far_own, core, 2),
-            (far_other, 1 - core, 2),
+            (far_own, core, 1),
+            (far_other, 1 - core, 1),
         ):
             s = 2 * g + side
-            for u in range(2):
-                z = lax.rem(wa - base - u + parts, parts)
+            for u in range(2 - far):
+                z = lax.rem(wa - 1 - far - 2 * u + parts, parts)
+                piece = source.at[m] if far else source.at[m, u]
                 pltpu.make_async_copy(
-                    source.at[m, u, pl.ds(2 * rows, quarter), :],
+                    piece.at[pl.ds(2 * rows, quarter), :],
                     output_w.at[
                         pl.ds(pl.multiple_of(rows * z + quarter * g, 16), quarter),
                         pl.ds(pl.multiple_of(slot_w * side, TILE), slot_w),
@@ -786,7 +885,7 @@
                     in_sems.at[0],
                 ).start()
                 pltpu.make_async_copy(
-                    source.at[m, u, pl.ds(0, rows), :],
+                    piece.at[pl.ds(0, rows), :],
                     inner_w.at[
                         pl.ds(pl.multiple_of(rows * z, 16), rows),
                         pl.ds(pl.multiple_of(slot_w * s, TILE), slot_w),
@@ -795,7 +894,7 @@
                 ).start()
                 for v in range(2):
                     pltpu.make_async_copy(
-                        source.at[m, u, pl.ds(rows + half * v, half), :],
+                        piece.at[pl.ds(rows + half * v, half), :],
                         outer_w.at[
                             pl.ds(pl.multiple_of(dmod * z + half * s, 16), half),
                             pl.ds(slot_w * v, slot_w),
@@ -810,8 +909,8 @@
 
     pltpu.make_async_copy(output_w, output_w, in_sems.at[0]).wait()
     branch = vec["outb"]
-    for g in range(CHIPS):
-        branch = branch + plain_product(context[g], output_w[group * g : group * (g + 1), :])
+    for m in range(CHIPS):
+        branch = branch + plain_product(context[m][...], output_w[head_rows(m), :])
     first, unit_one, inverse_one = normed(text[:tok, :].astype(f32) + branch, vec["g1"], vec["s1"])
     low = first.astype(bf16)
 
@@ -888,10 +987,10 @@
     put(0, summed_rows(low_one.astype(f32)))
     small[0] = jnp.zeros_like(small[0])
     small[1] = sums[...].astype(bf16)
-    for g in range(CHIPS):
-        at = slice(group * g, group * (g + 1))
-        output_g[at, :] = rows_product(context[g], low_one).astype(bf16)
-        grad_context[g] = lanes_product(low_one, output_w[at, :]).astype(bf16)
+    for m in range(CHIPS):
+        at = head_rows(m)
+        output_g[at, :] = rows_product(context[m][...], low_one).astype(bf16)
+        grad_context[m] = lanes_product(low_one, output_w[at, :]).astype(bf16)
     for target, g, side, sem in targets():
         pltpu.make_async_copy(
             output_view.at[
@@ -910,7 +1009,7 @@
         pltpu.make_async_copy(target, target, out_sems.at[sem]).wait()
 
 
-def project_back_kernel(place, tokens, dq, dkv_own, dkv_other, weight, partial, kept, sent, acc, dkv):
+def head_grads_kernel(place, tokens, dq, dkv_own, dkv_other, dkv, kept, sent, acc):
     tok = dq.shape[1]
     core = place[1]
     wide = dq.shape[2]
@@ -920,16 +1019,13 @@
     def piece(m, carry):
         text = tokens[m, :tok]
         both = dkv_own[m].astype(jnp.float32) + dkv_other[m].astype(jnp.float32)
-        dkv[...] = both.astype(jnp.bfloat16)
-        partial[m] = (
-            lanes_product(dq[m], weight[:, :wide]) + lanes_product(dkv[...], weight[:, wide:])
-        ).astype(jnp.bfloat16)
+        dkv[m] = both.astype(jnp.bfloat16)
         text_turned = text.astype(jnp.float32).T.astype(jnp.bfloat16)
         acc[:, :wide] += plain_product(text_turned, dq[m])
-        acc[:, wide:] += plain_product(text_turned, dkv[...])
+        acc[:, wide:] += plain_product(text_turned, dkv[m])
         return (
             carry[0] + summed_rows(dq[m].astype(jnp.float32)),
-            carry[1] + summed_rows(dkv[...].astype(jnp.float32)),
+            carry[1] + summed_rows(dkv[m].astype(jnp.float32)),
         )
 
     start = (jnp.zeros((1, wide), jnp.float32), jnp.zeros((1, wide // 2), jnp.float32))
@@ -940,6 +1036,18 @@
             at = pl.ds(pl.multiple_of(2 * rows * z + rows * side, 32), rows)
             target[z, :rows] = acc[at, :].astype(jnp.bfloat16)
             target[z, rows:] = jnp.where(side == 0, sums, 0.0).astype(jnp.bfloat16)
+
+
+def token_grads_kernel(dq, dkv, weight, partial):
+    wide = dq.shape[2]
+
+    def piece(m, carry):
+        partial[m] = (
+            lanes_product(dq[m], weight[:, :wide]) + lanes_product(dkv[m], weight[:, wide:])
+        ).astype(jnp.bfloat16)
+        return carry
+
+    lax.fori_loop(0, CHIPS, piece, 0)
 
 
 def picked_piece(place, own, other, g, side, rows):
@@ -1002,7 +1110,7 @@
     return pl.BlockSpec(memory_space=pl.ANY)
 
 
-def whole_call(kernel, operands, outs, scratch=(), flops=0, nbytes=0, exps=0):
+def whole_call(kernel, operands, outs, scratch=(), micros=1):
     return pl.pallas_call(
         kernel,
         out_shape=[jax.ShapeDtypeStruct(shape, dtype) for shape, dtype, _ in outs],
@@ -1010,7 +1118,9 @@
         out_specs=[spec() for _, _, spec in outs],
         scratch_shapes=list(scratch),
         compiler_params=pltpu.CompilerParams(vmem_limit_bytes=58 << 20),
-        cost_estimate=pl.CostEstimate(flops=flops, bytes_accessed=nbytes, transcendentals=exps),
+        cost_estimate=pl.CostEstimate(
+            flops=micros * FLOPS_PER_MICRO, bytes_accessed=micros << 20, transcendentals=0
+        ),
     )(*(value for value, _ in operands))
 
 
@@ -1061,48 +1171,50 @@
     text = jnp.concatenate([inputs, tag_rows], axis=0)
     cut = tok // 2
     text_x, text_y = swapped(text, 2), swapped(text, 4)
+
+    def after(value, *earlier):
+        return lax.optimization_barrier((value, *earlier))[0]
+
+
+    lines = (
+        bias_wordword,
+        bias_wordentity,
+        bias_entityword,
+        bias_entityentity,
+        value_bias,
+        output_bias,
+        first_gain,
+        first_bias,
+        outer_bias,
+        second_gain,
+        second_bias,
+        inner_bias,
+    )
+    six = (query_wordword, query_wordentity, query_entityword, query_entityentity, key_weight, value_weight)
+    mine, slot = whole_call(
+        prepare_kernel,
+        [(place, smem)]
+        + [(a, vmem) for a in (*six, *lines)]
+        + [(a, hbm) for a in (inner_weight, outer_weight, output_weight)],
+        [((half + TAG_ROWS, 6 * group), bf16, vmem), ((2 * rows + quarter, slot_w), bf16, vmem)],
+        [pltpu.SemaphoreType.DMA((4,))],
+        micros=3,
+    )
+    one, three = turned(mine, 1), turned(mine, 3)
+    text_x, text_y, one, three = lax.optimization_barrier((text_x, text_y, one, three))
     text_far = swapped(text_x[:cut], 4), swapped(text_y[cut:], 2)
-
-    six = (query_wordword, query_wordentity, query_entityword, query_entityentity, key_weight, value_weight)
-    cols = [lax.dynamic_slice(w, (half * core, group * chip), (half, group)).reshape(half, 3, HD) for w in six]
-    queries = [b.reshape(1, 3, HD) for b in (bias_wordword, bias_wordentity, bias_entityword, bias_entityentity)]
-    lone = value_bias.reshape(1, 3, HD)
-    by_head = [
-        (jnp.stack(cols[:4], axis=2), jnp.stack(cols[4:], axis=2)),
-        (jnp.stack(queries, axis=2), jnp.stack([jnp.zeros_like(lone), lone], axis=2)),
-    ]
-    mine = [jnp.concatenate([a.reshape(a.shape[0], -1), b.reshape(b.shape[0], -1)], axis=1) for a, b in by_head]
-    six_vectors = jnp.concatenate([output_bias, first_gain, first_bias, outer_bias, second_gain, second_bias])
-    mine += [six_vectors[None], jnp.pad(inner_bias, (0, 6 * group - inner_bias.shape[0]))[None]]
-    mine.append(jnp.zeros((TAG_ROWS - 3, 6 * group), bf16))
-    mine = jnp.concatenate(mine, axis=0)
-    mine = jnp.stack([mine] + [turned(mine, k) for k in range(1, parts)])
+    two = ring_far(one, three)
+    slot = after(slot, text_x, text_y, one, three)
+    slot_one, slot_three = turned(slot, 1), turned(slot, 3)
+    *text_far, two, slot_one, slot_three = lax.optimization_barrier((*text_far, two, slot_one, slot_three))
+    near_slot = jnp.stack([slot_one, slot_three])
+    far_slot = ring_far(slot_one, slot_three)
+    mine = jnp.stack([mine, one, two, three])
     theirs = swapped(mine, 1)
     order = (wa - jnp.arange(parts)) % parts
     vectors = jnp.take(mine[:, half + 1], order, axis=0).reshape(parts, 6, rows)
     vectors = jnp.pad(jnp.transpose(vectors, (1, 0, 2)).reshape(6, dmod), ((0, 2), (0, 0))).astype(f32)
     full_inner_bias = jnp.take(mine[:, half + 2, : ff // parts], order, axis=0).reshape(1, ff).astype(f32)
-
-    slot = jnp.concatenate(
-        [
-            lax.dynamic_slice(inner_weight, (0, slot_w * index), (rows, slot_w)),
-            lax.dynamic_slice(outer_weight, (half * index, 0), (half, slot_w)),
-            lax.dynamic_slice(outer_weight, (half * index, slot_w), (half, slot_w)),
-            lax.dynamic_slice(output_weight, (quarter * chip, slot_w * core), (quarter, slot_w)),
-        ],
-        axis=0,
-    )
-    slots = [slot] + [turned(slot, k) for k in range(1, parts)]
-
-    def chip_stacked(value):
-        middle = value.shape[0] // 2
-        along_x, along_y = swapped(value, 2), swapped(value, 4)
-        across = jnp.concatenate([swapped(along_x[:middle], 4), swapped(along_y[middle:], 2)], axis=0)
-        stacked = jnp.stack([value, along_x, along_y, across])
-        return stacked, swapped(stacked, 1)
-
-    near_slots = chip_stacked(jnp.stack(slots[:2]))
-    far_slots = chip_stacked(jnp.stack(slots[2:]))
 
     weight, all_text, q, kv = whole_call(
         project_kernel,
@@ -1113,10 +1225,12 @@
             ((CHIPS, tok, 2 * group), bf16, vmem),
             ((CHIPS, tok + TAG_ROWS, 2 * group), bf16, vmem),
         ],
-        flops=2 * CHIPS * tok * dmod * 6 * group,
-        nbytes=12 << 20,
+        micros=8,
     )
     kv_other = swapped(kv, 1)
+    kv_other, far_slot = lax.optimization_barrier((kv_other, far_slot))
+    far_slots = [far_slot] + [swapped(far_slot, 2 * m) for m in range(1, CHIPS)]
+    near_slots = [near_slot] + [swapped(near_slot, 2 * m) for m in range(1, CHIPS)]
 
     context, turned_out, lse, bounds = whole_call(
         attend_kernel,
@@ -1134,23 +1248,27 @@
             pltpu.VMEM((2 * CHIPS, 8, tok), f32),
             pltpu.VMEM((3, HD, tok), f32),
         ],
-        flops=4 * CHIPS * tok * length * group // 2,
-        nbytes=8 << 20,
-        exps=CHIPS * tok * length * 3 // 2,
-    )
-    same_core = [[2 * i + k for i in range(CHIPS)] for k in range(2)]
+        micros=25,
+    )
+    barrier = lax.optimization_barrier((context, *near_slots, *far_slots))
+    context, near_slots, far_slots = barrier[0], jnp.stack(barrier[1 : 1 + CHIPS]), jnp.stack(barrier[1 + CHIPS :])
+    near_slots = near_slots, swapped(near_slots, 1)
+    far_slots = far_slots, swapped(far_slots, 1)
 
     def exchanged(value):
-        return lax.all_to_all(
-            value, "ctx", split_axis=0, concat_axis=0, tiled=True, axis_index_groups=same_core
-        )
+        return [value[0]] + [swapped(value[m], 2 * m) for m in range(1, CHIPS)]
+
+    contexts = exchanged(context)
 
     slot_rows = 2 * rows + quarter + TAG_ROWS
     result, grad_sum, grad_context, kept, sent_far, sent_near = whole_call(
         dense_kernel,
         [(place, smem)]
-        + [(a, vmem) for a in (exchanged(context), text, cotangent[0], vectors, full_inner_bias)]
-        + [(a, hbm) for a in (*near_slots, *far_slots)],
+        + [(a, vmem) for a in (*contexts, text, cotangent[0], vectors, full_inner_bias)]
+        + [
+            (a, hbm)
+            for a in (inner_weight, outer_weight, output_weight, *near_slots, *far_slots)
+        ],
         [
             ((tok, dmod), bf16, vmem),
             ((tok, dmod), f32, vmem),
@@ -1173,16 +1291,34 @@
             pltpu.SemaphoreType.DMA((3,)),
             pltpu.SemaphoreType.DMA((3,)),
         ],
-        flops=6 * tok * dmod * (dmod + 2 * ff),
-        nbytes=26 << 20,
-        exps=2 * tok * ff,
-    )
-    grad_context = exchanged(grad_context)
+        micros=35,
+    )
+    grad_pieces = exchanged(grad_context)
+
+    def added(*values):
+        total = values[0].astype(f32)
+        for v in values[1:]:
+            total = total + v.astype(f32)
+        return total
+
+    middle = parts // 2
+    upper, lower = slice(0, middle), slice(middle, None)
+    received_far = swapped(sent_far, 1)
+    received = swapped(sent_near, 1)
+    far_x = added(kept[CHIPS - 1, upper], received_far[upper]).astype(bf16)
+    far_y = added(kept[CHIPS - 1, lower], received_far[lower]).astype(bf16)
+    near_x = added(kept[1, upper], received[1, upper]).astype(bf16)
+    near_y = added(kept[2, lower], received[2, lower]).astype(bf16)
+    *grad_pieces, far_x, far_y, near_x, near_y = lax.optimization_barrier(
+        (*grad_pieces, far_x, far_y, near_x, near_y)
+    )
+    far_x, far_y = swapped(far_x, 2), swapped(far_y, 4)
+    near_x, near_y = swapped(near_x, 2), swapped(near_y, 4)
 
     dq, dkv, dkv_sent = whole_call(
         attend_back_kernel,
         [(place, smem), (bounds, smem)]
-        + [(a, vmem) for a in (q, kv, kv_other, turned_out, lse, grad_context)],
+        + [(a, vmem) for a in (q, kv, kv_other, turned_out, lse, *grad_pieces)],
         [
             ((CHIPS, tok, 4 * group), bf16, vmem),
             ((CHIPS, tok, 2 * group), bf16, vmem),
@@ -1197,74 +1333,106 @@
             pltpu.VMEM((length, TILE), f32),
             pltpu.VMEM((2 * CHIPS, 8, tok), f32),
             pltpu.VMEM((3, 2 * HD, tok), f32),
+            pltpu.VMEM((CHIPS, tok, group), bf16),
         ],
-        flops=10 * CHIPS * tok * length * group // 2,
-        nbytes=16 << 20,
-        exps=CHIPS * tok * length * 3 // 2,
-    )
-    partial, head_kept, head_sent = whole_call(
-        project_back_kernel,
-        [(place, smem)] + [(a, vmem) for a in (all_text, dq, dkv, swapped(dkv_sent, 1), weight)],
+        micros=40,
+    )
+    dq, dkv, dkv_sent, far_x, far_y, near_x, near_y = lax.optimization_barrier(
+        (dq, dkv, dkv_sent, far_x, far_y, near_x, near_y)
+    )
+    dkv_received = swapped(dkv_sent, 1)
+    last_x = added(kept[1, lower], received[1, lower], far_y).astype(bf16)
+    last_y = added(kept[2, upper], received[2, upper], far_x).astype(bf16)
+    last_x, last_y = lax.optimization_barrier((last_x, last_y))
+    last_x, last_y = swapped(last_x, 2), swapped(last_y, 4)
+    dkv, head_kept, head_sent = whole_call(
+        head_grads_kernel,
+        [(place, smem)] + [(a, vmem) for a in (all_text, dq, dkv, dkv_received)],
         [
-            ((CHIPS, tok, dmod), bf16, vmem),
+            ((CHIPS, tok, 2 * group), bf16, vmem),
             ((parts, half + TAG_ROWS, 6 * group), bf16, vmem),
             ((parts, half + TAG_ROWS, 6 * group), bf16, vmem),
         ],
-        [pltpu.VMEM((dmod, 6 * group), f32), pltpu.VMEM((tok, 2 * group), bf16)],
-        flops=4 * CHIPS * tok * dmod * 6 * group,
-        nbytes=16 << 20,
-    )
-
-    def added(*values):
-        total = values[0].astype(f32)
-        for v in values[1:]:
-            total = total + v.astype(f32)
-        return total
-
-    def chips_summed(far, near, to):
-        middle = far.shape[0] // 2
-        from_x, from_y = swapped(far[:middle], 2), swapped(far[middle:], 4)
-        x0, x1 = near(1, slice(0, middle)), near(1, slice(middle, None))
-        y0, y1 = near(2, slice(0, middle)), near(2, slice(middle, None))
-        x0 = swapped(added(*x0).astype(bf16), 2)
-        y1 = swapped(added(*y1).astype(bf16), 4)
-        x1 = swapped(added(*x1, from_y).astype(bf16), 2)
-        y0 = swapped(added(*y0, from_x).astype(bf16), 4)
-        low = added(*near(0, slice(0, middle)), x0, y0).astype(to)
-        high = added(*near(0, slice(middle, None)), x1, y1).astype(to)
-        return low, high
-
-    def parts_summed(value):
-        total = [lax.dynamic_index_in_dim(value, wa, 0, keepdims=False)]
-        for k in range(1, parts):
-            total.append(turned(lax.dynamic_index_in_dim(value, (wa + k) % parts, 0, keepdims=False), k))
-        return added(*total).astype(bf16)
-
-    far = added(kept[CHIPS - 1], swapped(sent_far, 1)).astype(bf16)
-    received = swapped(sent_near, 1)
-    low, high = chips_summed(far, lambda m, at: (kept[m, at], received[m, at]), bf16)
-    summed = parts_summed(jnp.concatenate([low, high], axis=0))
+        [pltpu.VMEM((dmod, 6 * group), f32)],
+        micros=10,
+    )
+    head_received = swapped(head_sent, 1)
+    (partial,) = whole_call(
+        token_grads_kernel,
+        [(a, vmem) for a in (dq, dkv, weight)],
+        [((CHIPS, tok, dmod), bf16, vmem)],
+        micros=8,
+    )
+    partial, head_received = lax.optimization_barrier((partial, head_received))
+
+    def parts_sent(value):
+        kept_part = lax.dynamic_index_in_dim(value, wa, 0, keepdims=False)
+        return [kept_part] + [
+            lax.dynamic_index_in_dim(value, (wa + k) % parts, 0, keepdims=False) for k in range(1, parts)
+        ]
+
+    def parts_moved(values):
+        return [turned(v, k) for k, v in enumerate(values) if k]
+
+    def chips_moved(value):
+        return [swapped(value, 2 * m) for m in range(1, CHIPS)]
+
+    low, high = slice(0, cut), slice(cut, None)
+    head_parts = parts_sent(added(head_kept, head_received).astype(bf16))
+    text_sent = [partial[3, low], partial[3, high], partial[1, low], partial[2, high]]
+    barrier = lax.optimization_barrier((*head_parts, *text_sent))
+    head_parts, text_sent = barrier[:parts], barrier[parts:]
+    head_moved = parts_moved(head_parts)
+    text_moved = [swapped(v, 2 << (k % 2)) for k, v in enumerate(text_sent)]
+    barrier = lax.optimization_barrier((*head_moved, *text_moved, last_x, last_y))
+    head_moved, text_moved, last_x, last_y = barrier[:3], barrier[3:7], barrier[7], barrier[8]
+
+    summed = jnp.concatenate(
+        [
+            added(kept[0, upper], received[0, upper], near_x, last_y),
+            added(kept[0, lower], received[0, lower], last_x, near_y),
+        ],
+        axis=0,
+    ).astype(bf16)
+    dense_parts = parts_sent(summed)
+    far_x, far_y, near_x, near_y = text_moved
+    text_x = added(partial[1, high], far_y).astype(bf16)
+    text_y = added(partial[2, low], far_x).astype(bf16)
+    head_summed = added(head_parts[0], *head_moved).astype(bf16)
+    barrier = lax.optimization_barrier((*dense_parts, text_x, text_y, head_summed))
+    dense_parts, text_x, text_y, head_summed = barrier[:parts], *barrier[parts:]
+    dense_moved = parts_moved(dense_parts)
+    text_x, text_y = swapped(text_x, 2), swapped(text_y, 4)
+    head_moved = chips_moved(head_summed)
+    barrier = lax.optimization_barrier((*dense_moved, text_x, text_y, *head_moved))
+    dense_moved, text_x, text_y, head_moved = barrier[:3], barrier[3], barrier[4], barrier[5:]
+
+    dense_summed = added(dense_parts[0], *dense_moved).astype(bf16)
+    head_all = jnp.stack([head_summed, *head_moved])
+    dense_summed, head_all = lax.optimization_barrier((dense_summed, head_all))
+    dense_moved = chips_moved(dense_summed)
+    *out_heads, sums = whole_call(
+        unpack_heads_kernel,
+        [(place, smem), (head_all, vmem), (swapped(head_all, 1), vmem)],
+        [((rows, dmod), f32, vmem) for _ in range(6)] + [((TAG_ROWS, 6 * group), f32, vmem)],
+        micros=4,
+    )
+    input_grads = grad_sum + jnp.concatenate(
+        [added(partial[0, low], near_x, text_y), added(partial[0, high], text_x, near_y)], axis=0
+    )
+    *dense_moved, input_grads = lax.optimization_barrier((*dense_moved, input_grads))
+    dense_all = jnp.stack([dense_summed, *dense_moved])
     out_inner, out_outer, out_output, small = whole_call(
         unpack_dense_kernel,
-        [(place, smem)] + [(a, vmem) for a in chip_stacked(summed)],
+        [(place, smem), (dense_all, vmem), (swapped(dense_all, 1), vmem)],
         [
             ((rows, ff), f32, vmem),
             (outer_weight.shape, f32, vmem),
             ((rows, dmod), f32, vmem),
             ((TAG_ROWS, slot_w), f32, vmem),
         ],
-        nbytes=8 << 20,
-    )
-
-    summed = parts_summed(added(head_kept, swapped(head_sent, 1)).astype(bf16))
-    *out_heads, sums = whole_call(
-        unpack_heads_kernel,
-        [(place, smem)] + [(a, vmem) for a in chip_stacked(summed)],
-        [((rows, dmod), f32, vmem) for _ in range(6)] + [((TAG_ROWS, 6 * group), f32, vmem)],
-        nbytes=8 << 20,
-    )
-    low, high = chips_summed(partial[CHIPS - 1], lambda m, at: (partial[m, at],), f32)
-    input_grads = grad_sum + jnp.concatenate([low, high], axis=0)
+        micros=4,
+    )
 
     sum_q = sums[0, : 4 * group].reshape(3, 4, HD)
     sum_v = sums[0, 4 * group :].reshape(3, 2, HD)[:, 1].reshape(rows)

time: 413 us -> 354 us (0.86)
  waiting for transfers between devices: 138 us -> 118 us
  local copies, waits for them, and re-layouts: 33.6 us -> 20.4 us
  blocking collectives: 10.8 us -> 0 us
  other arithmetic: 27.6 us -> 18.5 us
  Pallas kernels: 129 us -> 123 us
    ppermute x42 -> x44, waiting for transfers between devices: 73.9 us -> 54.4 us  [swapped(): return lax.ppermute(value, 'ctx', [(i, i ^ step) for i in range(count)])]
    all_to_all x1 -> x0, blocking collectives: 10.8 us -> none  [exchanged(): lax.all_to_all(value, 'ctx', split_axis=0, concat_axis=0, tiled=True, axi...]
    dynamic_slice x9 -> x0, local copies, waits for them, and re-layouts: 7.74 us -> none  [the longest x6 5.92 us: grouped_device(): lax.dynamic_slice(w, (half * core, group * chip), (half, group))]
    pallas_call x7 -> x9, Pallas kernels: 129 us -> 123 us  [whole_call(): pl.pallas_call(kernel, out_shape=[jax.ShapeDtypeStruct(shape, dtype) for...]
    another operation x15 -> x7, other arithmetic: 9.81 us -> 5.11 us  [the longest x10 8.55 us: chip_stacked(): stacked = jnp.stack([value, along_x, along_y, across])]
    all_to_all x1 -> x0, waiting for transfers between devices: 4.42 us -> none  [exchanged(): lax.all_to_all(value, 'ctx', split_axis=0, concat_axis=0, tiled=True, axi...]
    convert_element_type x9 -> x7, other arithmetic: 12.4 us -> 8.19 us  [the longest x1 3.16 us: grouped_device(): last_y = added(kept[2, upper], received[2, upper], far_x).astype(bf16)]
    ppermute x12 -> x14, starting transfers between devices: 27.7 us -> 31.7 us  [turned(): lax.ppermute(value, 'wa', [(i, (i + step) % count) for i in range(count)])]
  transfers between devices with their start and end apart: 55 -> 58, of which waited for: 22 -> 28; matrix products, arithmetic and copies ran while one was open for 13% -> 7% of each run, Pallas kernels for 21% -> 18%
where the time goes in v3:
time: 354 us; the launch traced here: 355 us
  Pallas kernels  123 us (35%)
  waiting for transfers between devices  118 us (33%)
  starting transfers between devices  73.6 us (21%)
  local copies, waits for them, and re-layouts  20.4 us (6%)
  other arithmetic  18.5 us (5%)
    pallas_call x9, Pallas kernels, whole_call(): pl.pallas_call(kernel, out_shape=[jax.ShapeDtypeStruct(shape, dtype) for...  123 us
    ppermute x14, waiting for transfers between devices, turned(): lax.ppermute(value, 'wa', [(i, (i + step) % count) for i in range(count)])  63.6 us
    ppermute x44, waiting for transfers between devices, swapped(): return lax.ppermute(value, 'ctx', [(i, i ^ step) for i in range(count)])  54.4 us
    ppermute x44, starting transfers between devices, swapped(): return lax.ppermute(value, 'ctx', [(i, i ^ step) for i in range(count)])  41.9 us
    ppermute x14, starting transfers between devices, turned(): lax.ppermute(value, 'wa', [(i, (i + step) % count) for i in range(count)])  31.7 us
  transfers between devices with their start and end apart: 58, of which 28 were waited for; matrix products, arithmetic and copies ran while one was open for 7% of the time, Pallas kernels for 18%

profile of v3, /device:TPU:9, one launch (start us, length us, event | category | flops | bytes accessed | tf_op | source)
XLA Modules:
  0.0 355.0 jit_solution(9655403073603538711)
XLA Ops:
  5.6 3.4 shard_map.416
  10.5 5.2 %collective-permute-done.2 = bf16[112,1152]{1,0:T(8,128)(2,1)S(1)} collective-permute-done((bf16[112,1152]{1,0:T(8,128)(2,1)}, bf16[112,1152]{1,0:T(8,128)(2,1)S(1)}, u32[]{:S(2)}, u32[]{:S(2)}) %collective-permute-start.2) | collective-permute-done | bytes 258080 | tf_op jit(solution)/shard_map/ppermute | solution.py:489
  15.7 8.1 %collective-permute-done.3 = bf16[112,1152]{1,0:T(8,128)(2,1)S(1)} collective-permute-done((bf16[112,1152]{1,0:T(8,128)(2,1)}, bf16[112,1152]{1,0:T(8,128)(2,1)S(1)}, u32[]{:S(2)}, u32[]{:S(2)}) %collective-permute-start.3) | collective-permute-done | bytes 258080 | tf_op jit(solution)/shard_map/ppermute | solution.py:489
  28.6 3.5 collective-permute-done.7
  34.6 3.6 %collective-permute-done.8 = bf16[432,384]{1,0:T(8,128)(2,1)S(1)} collective-permute-done((bf16[432,384]{1,0:T(8,128)(2,1)}, bf16[432,384]{1,0:T(8,128)(2,1)S(1)}, u32[]{:S(2)}, u32[]{:S(2)}) %collective-permute-start.8) | collective-permute-done | bytes 331808 | tf_op jit(solution)/shard_map/ppermute | solution.py:489
  38.2 7.6 %collective-permute-done.9 = bf16[432,384]{1,0:T(8,128)(2,1)S(1)} collective-permute-done((bf16[432,384]{1,0:T(8,128)(2,1)}, bf16[432,384]{1,0:T(8,128)(2,1)S(1)}, u32[]{:S(2)}, u32[]{:S(2)}) %collective-permute-start.9) | collective-permute-done | bytes 331808 | tf_op jit(solution)/shard_map/ppermute | solution.py:489
  50.3 8.2 %shard_map.417 = (bf16[768,1152]{1,0:T(8,128)(2,1)}, bf16[4,400,768]{2,1,0:T(8,128)(2,1)}, bf16[4,384,384]{2,1,0:T(8,128)(2,1)}, bf16[4,400,384]{2,1,0:T(8,128)(2,1)}) custom-call(s32[3]{0:T(128)} %pad_add_fusion.place, bf16[400,768]{1,0:T(8,128)(2,1)} %copy-done.10, bf16[400,768]{1,0:T(8,128)(2,1)} %copy-done.17, bf16[400,768]{1,0:T(8,128)(2,1)} %copy-done.16, ...), custom_call_target="tpu_custom_call" | custom-call | flops 8800000000 | bytes 8388608 | tf_op jit(solution)/shard_map/pallas_call | solution.py:1114
  61.3 3.4 collective-permute-done.12
  65.9 3.3 collective-permute-done.13
  70.7 4.7 %collective-permute-done.14 = bf16[2,432,384]{2,1,0:T(8,128)(2,1)S(1)} collective-permute-done((bf16[2,432,384]{2,1,0:T(8,128)(2,1)S(1)}, bf16[2,432,384]{2,1,0:T(8,128)(2,1)S(1)}, u32[]{:S(2)}, u32[]{:S(2)}) %collective-permute-start.14) | collective-permute-done | bytes 663584 | tf_op jit(solution)/shard_map/ppermute | solution.py:484
  75.6 19.8 %shard_map.418 = (bf16[4,384,192]{2,1,0:T(8,128)(2,1)}, f32[4,192,384]{2,1,0:T(8,128)}, f32[4,3,1,384]{3,2,1,0:T(1,128)}, s32[2,4]{1,0:T(2,128)}) custom-call(s32[3]{0:T(128)} %pad_add_fusion.place, bf16[4,384,384]{2,1,0:T(8,128)(2,1)} %get-tuple-element.144.q_ref, bf16[4,400,384]{2,1,0:T(8,128)(2,1)} %get-tuple-element.145.own, bf16[4,400,384]{2,1,0:T(8,128)(2,1)} %copy-done.18), custom_call_target="tpu_custom_call" | custom-call | flops 27499999232 | bytes 26214400 | tf_op jit(solution)/shard_map/pallas_call | solution.py:1114
  96.8 8.2 %collective-permute-done.18 = bf16[432,384]{1,0:T(8,128)(2,1)S(1)} collective-permute-done((bf16[432,384]{1,0:T(8,128)(2,1)S(1)}, bf16[432,384]{1,0:T(8,128)(2,1)S(1)}, u32[]{:S(2)}, u32[]{:S(2)}) %collective-permute-start.18) | collective-permute-done | bytes 331808 | tf_op jit(solution)/shard_map/ppermute | solution.py:484
  120.8 5.1 %collective-permute-done.21.context2 = bf16[384,192]{1,0:T(8,128)(2,1)S(1)} collective-permute-done((bf16[384,192]{1,0:T(8,128)(2,1)}, bf16[384,192]{1,0:T(8,128)(2,1)S(1)}, u32[]{:S(2)}, u32[]{:S(2)}) %collective-permute-start.21) | collective-permute-done | bytes 147488 | tf_op jit(solution)/shard_map/ppermute | solution.py:484
  126.7 35.0 %shard_map.419 = (bf16[384,768]{1,0:T(8,128)(2,1)}, f32[384,768]{1,0:T(8,128)}, bf16[4,384,192]{2,1,0:T(8,128)(2,1)}, bf16[4,4,448,384]{3,2,1,0:T(8,128)(2,1)}, ...) custom-call(s32[3]{0:T(128)} %pad_add_fusion.place, bf16[384,192]{1,0:T(8,128)(2,1)} %get-tuple-element.280.context0, ...), custom_call_target="tpu_custom_call" | custom-call | flops 38499999744 | bytes 36700160 | tf_op jit(solution)/shard_map/pallas_call | solution.py:1114
  167.5 4.2 %collective-permute-done.29 = bf16[4,448,384]{2,1,0:T(8,128)(2,1)S(1)} collective-permute-done((bf16[4,448,384]{2,1,0:T(8,128)(2,1)}, bf16[4,448,384]{2,1,0:T(8,128)(2,1)S(1)}, u32[]{:S(2)}, u32[]{:S(2)}) %collective-permute-start.29) | collective-permute-done | bytes 1376288 | tf_op jit(solution)/shard_map/ppermute | solution.py:484
  179.1 30.6 %shard_map.420 = (bf16[4,384,768]{2,1,0:T(8,128)(2,1)}, bf16[4,384,384]{2,1,0:T(8,128)(2,1)}, bf16[4,384,384]{2,1,0:T(8,128)(2,1)}) custom-call(s32[3]{0:T(128)} %pad_add_fusion.place, s32[2,4]{1,0:T(2,128)} %get-tuple-element.163.bounds, bf16[4,384,384]{2,1,0:T(8,128)(2,1)} %get-tuple-element.144.q_ref, bf16[4,400,384]{2,1,0:T(8,128)(2,1)} %get-tuple-element.145.own, ...), custom_call_target="tpu_custom_call" | custom-call | flops 44000002048 | bytes 41943040 | tf_op jit(solution)/shard_map/pallas_call | solution.py:1114
  209.7 4.8 %collective-permute-start.34 = (bf16[4,384,384]{2,1,0:T(8,128)(2,1)}, bf16[4,384,384]{2,1,0:T(8,128)(2,1)S(1)}, u32[]{:S(2)}, u32[]{:S(2)}) collective-permute-start(bf16[4,384,384]{2,1,0:T(8,128)(2,1)} %get-tuple-element.183), channel_id=1, source_target_pairs={{0,4},{4,0},{8,12},{12,8},{16,20},{20,16},{24,28},{28,24},{1,5},{5... | collective-permute-start | bytes 3538952 | tf_op jit(solution)/shard_map/ppermute | solution.py:484
  218.3 10.1 %shard_map.421 = (bf16[4,384,384]{2,1,0:T(8,128)(2,1)}, bf16[4,112,1152]{2,1,0:T(8,128)(2,1)}, bf16[4,112,1152]{2,1,0:T(8,128)(2,1)}) custom-call(s32[3]{0:T(128)} %pad_add_fusion.place, bf16[4,400,768]{2,1,0:T(8,128)(2,1)} %get-tuple-element.180.tokens, bf16[4,384,768]{2,1,0:T(8,128)(2,1)} %get-tuple-element.181.dq, ...), custom_call_target="tpu_custom_call" | custom-call | flops 11000000512 | bytes 10485760 | tf_op jit(solution)/shard_map/pallas_call | solution.py:1114
  228.7 3.2 fusion.4
  233.3 7.8 %shard_map.422 = bf16[4,384,768]{2,1,0:T(8,128)(2,1)} custom-call(bf16[4,384,768]{2,1,0:T(8,128)(2,1)} %get-tuple-element.181.dq, bf16[4,384,384]{2,1,0:T(8,128)(2,1)} %get-tuple-element.185.dkv, bf16[768,1152]{1,0:T(8,128)(2,1)} %get-tuple-element.186.weight), custom_call_target="tpu_custom_call" | custom-call | flops 8800000000 | bytes 8388608 | tf_op jit(solution)/shard_map/pallas_call | solution.py:1114
  242.9 10.3 %collective-permute-start.36 = (bf16[112,1152]{1,0:T(8,128)(2,1)S(1)}, bf16[112,1152]{1,0:T(8,128)(2,1)S(1)}, u32[]{:S(2)}, u32[]{:S(2)}) collective-permute-start(bf16[112,1152]{1,0:T(8,128)(2,1)S(1)} %get-tuple-element.190), channel_id=1, source_target_pairs={{0,1},{1,2},{2,3},{3,0},{4,5},{5,6},{6,7},{7,4},{8,9},{9,10},{10,1... | collective-permute-start | bytes 774152 | tf_op jit(solution)/shard_map/ppermute | solution.py:489
  253.3 4.5 %collective-permute-start.37 = (bf16[112,1152]{1,0:T(8,128)(2,1)S(1)}, bf16[112,1152]{1,0:T(8,128)(2,1)S(1)}, u32[]{:S(2)}, u32[]{:S(2)}) collective-permute-start(bf16[112,1152]{1,0:T(8,128)(2,1)S(1)} %get-tuple-element.191), channel_id=1, source_target_pairs={{0,2},{1,3},{2,0},{3,1},{4,6},{5,7},{6,4},{7,5},{8,10},{9,11},{10,... | collective-permute-start | bytes 774152 | tf_op jit(solution)/shard_map/ppermute | solution.py:489
  262.8 6.6 %collective-permute-done.37 = bf16[112,1152]{1,0:T(8,128)(2,1)S(1)} collective-permute-done((bf16[112,1152]{1,0:T(8,128)(2,1)S(1)}, bf16[112,1152]{1,0:T(8,128)(2,1)S(1)}, u32[]{:S(2)}, u32[]{:S(2)}) %collective-permute-start.37) | collective-permute-done | bytes 258080 | tf_op jit(solution)/shard_map/ppermute | solution.py:489
  269.3 5.6 %collective-permute-start.38 = (bf16[112,1152]{1,0:T(8,128)(2,1)S(1)}, bf16[112,1152]{1,0:T(8,128)(2,1)S(1)}, u32[]{:S(2)}, u32[]{:S(2)}) collective-permute-start(bf16[112,1152]{1,0:T(8,128)(2,1)S(1)} %get-tuple-element.192), channel_id=1, source_target_pairs={{0,3},{1,0},{2,1},{3,2},{4,7},{5,4},{6,5},{7,6},{8,11},{9,8},{10,9... | collective-permute-start | bytes 774152 | tf_op jit(solution)/shard_map/ppermute | solution.py:489
  275.0 3.8 %collective-permute-done.38 = bf16[112,1152]{1,0:T(8,128)(2,1)S(1)} collective-permute-done((bf16[112,1152]{1,0:T(8,128)(2,1)S(1)}, bf16[112,1152]{1,0:T(8,128)(2,1)S(1)}, u32[]{:S(2)}, u32[]{:S(2)}) %collective-permute-start.38) | collective-permute-done | bytes 258080 | tf_op jit(solution)/shard_map/ppermute | solution.py:489
  285.6 4.0 %collective-permute-start.46 = (bf16[448,384]{1,0:T(8,128)(2,1)S(1)}, bf16[448,384]{1,0:T(8,128)(2,1)S(1)}, u32[]{:S(2)}, u32[]{:S(2)}) collective-permute-start(bf16[448,384]{1,0:T(8,128)(2,1)S(1)} %get-tuple-element.212), channel_id=1, source_target_pairs={{0,2},{1,3},{2,0},{3,1},{4,6},{5,7},{6,4},{7,5},{8,10},{9,11},{10,... | collective-permute-start | bytes 1032200 | tf_op jit(solution)/shard_map/ppermute | solution.py:489
  294.1 5.4 %collective-permute-done.48 = bf16[192,768]{1,0:T(8,128)(2,1)S(1)} collective-permute-done((bf16[192,768]{1,0:T(8,128)(2,1)S(1)}, bf16[192,768]{1,0:T(8,128)(2,1)S(1)}, u32[]{:S(2)}, u32[]{:S(2)}) %collective-permute-start.48) | collective-permute-done | bytes 294944 | tf_op jit(solution)/shard_map/ppermute | solution.py:484
  301.7 10.5 %collective-permute-done.46 = bf16[448,384]{1,0:T(8,128)(2,1)S(1)} collective-permute-done((bf16[448,384]{1,0:T(8,128)(2,1)S(1)}, bf16[448,384]{1,0:T(8,128)(2,1)S(1)}, u32[]{:S(2)}, u32[]{:S(2)}) %collective-permute-start.46) | collective-permute-done | bytes 344096 | tf_op jit(solution)/shard_map/ppermute | solution.py:489
  312.2 6.2 %collective-permute-done.47 = bf16[448,384]{1,0:T(8,128)(2,1)S(1)} collective-permute-done((bf16[448,384]{1,0:T(8,128)(2,1)S(1)}, bf16[448,384]{1,0:T(8,128)(2,1)S(1)}, u32[]{:S(2)}, u32[]{:S(2)}) %collective-permute-start.47) | collective-permute-done | bytes 344096 | tf_op jit(solution)/shard_map/ppermute | solution.py:489
  327.5 7.7 %collective-permute-done.55 = bf16[448,384]{1,0:T(8,128)(2,1)S(1)} collective-permute-done((bf16[448,384]{1,0:T(8,128)(2,1)S(1)}, bf16[448,384]{1,0:T(8,128)(2,1)S(1)}, u32[]{:S(2)}, u32[]{:S(2)}) %collective-permute-start.55) | collective-permute-done | bytes 344096 | tf_op jit(solution)/shard_map/ppermute | solution.py:484
  338.9 4.0 %shard_map.423 = (f32[192,768]{1,0:T(8,128)}, f32[192,768]{1,0:T(8,128)}, f32[192,768]{1,0:T(8,128)}, f32[192,768]{1,0:T(8,128)}, f32[192,768]{1,0:T(8,128)}, /*index=5*/f32[192,768]{1,0:T(8,128)}, f32[16,1152]{1,0:T(8,128)}) custom-call(s32[3]{0:T(128)} %pad_add_fusion.place, bf16[4,112,1152]{2,1,0:T(8,128)(2,1)} %copy-done.8, bf16[4,112,1152]{2,1,0:T(8,128)(2,1)} %copy-done.20), custom_call_target="tpu_custom_call" | custom-call | flops 4400000000 | bytes 4194304 | tf_op jit(solution)/shard_map/pallas_call | solution.py:1114
  347.8 4.5 %shard_map.424 = (f32[192,3072]{1,0:T(8,128)}, f32[768,768]{1,0:T(8,128)}, f32[192,768]{1,0:T(8,128)}, f32[16,384]{1,0:T(8,128)}) custom-call(s32[3]{0:T(128)} %pad_add_fusion.place, bf16[4,448,384]{2,1,0:T(8,128)(2,1)} %copy-done.4, bf16[4,448,384]{2,1,0:T(8,128)(2,1)} %collective-permute-done.57.other), custom_call_target="tpu_custom_call" | custom-call | flops 4400000000 | bytes 4194304 | tf_op jit(solution)/shard_map/pallas_call | solution.py:1114
  (216 shorter events, 101.2 us)
Async XLA Ops:
  2.5 21.3 %collective-permute-start = (bf16[400,768]{1,0:T(8,128)(2,1)S(1)}, bf16[400,768]{1,0:T(8,128)(2,1)S(1)}, u32[]{:S(2)}, u32[]{:S(2)}) collective-permute-start(bf16[400,768]{1,0:T(8,128)(2,1)S(1)} %fusion.11.t0.text), channel_id=1, source_target_pairs={{0,8},{4,12},{8,0},{12,4},{16,24},{20,28},{24,16},{28,20},{1,9},{5... | collective-permute-start | bytes 1843208 | tf_op jit(solution)/shard_map/ppermute | solution.py:484
  3.8 20.0 %collective-permute-start.1 = (bf16[400,768]{1,0:T(8,128)(2,1)S(1)}, bf16[400,768]{1,0:T(8,128)(2,1)S(1)}, u32[]{:S(2)}, u32[]{:S(2)}) collective-permute-start(bf16[400,768]{1,0:T(8,128)(2,1)S(1)} %fusion.11.t0.text), channel_id=1, source_target_pairs={{0,16},{4,20},{8,24},{12,28},{16,0},{20,4},{24,8},{28,12},{1,17},{... | collective-permute-start | bytes 1843208 | tf_op jit(solution)/shard_map/ppermute | solution.py:484
  10.3 13.4 %collective-permute-start.3 = (bf16[112,1152]{1,0:T(8,128)(2,1)}, bf16[112,1152]{1,0:T(8,128)(2,1)S(1)}, u32[]{:S(2)}, u32[]{:S(2)}) collective-permute-start(bf16[112,1152]{1,0:T(8,128)(2,1)} %get-tuple-element.134), channel_id=1, source_target_pairs={{0,3},{1,0},{2,1},{3,2},{4,7},{5,4},{6,5},{7,6},{8,11},{9,8},{10,9... | collective-permute-start | bytes 774152 | tf_op jit(solution)/shard_map/ppermute | solution.py:489
  25.4 12.8 %collective-permute-start.8 = (bf16[432,384]{1,0:T(8,128)(2,1)}, bf16[432,384]{1,0:T(8,128)(2,1)S(1)}, u32[]{:S(2)}, u32[]{:S(2)}) collective-permute-start(bf16[432,384]{1,0:T(8,128)(2,1)} %get-tuple-element.140), channel_id=1, source_target_pairs={{0,1},{1,2},{2,3},{3,0},{4,5},{5,6},{6,7},{7,4},{8,9},{9,10},{10,1... | collective-permute-start | bytes 995336 | tf_op jit(solution)/shard_map/ppermute | solution.py:489
  25.4 20.4 %collective-permute-start.9 = (bf16[432,384]{1,0:T(8,128)(2,1)}, bf16[432,384]{1,0:T(8,128)(2,1)S(1)}, u32[]{:S(2)}, u32[]{:S(2)}) collective-permute-start(bf16[432,384]{1,0:T(8,128)(2,1)} %get-tuple-element.140), channel_id=1, source_target_pairs={{0,3},{1,0},{2,1},{3,2},{4,7},{5,4},{6,5},{7,6},{8,11},{9,8},{10,9... | collective-permute-start | bytes 995336 | tf_op jit(solution)/shard_map/ppermute | solution.py:489
  59.0 16.4 %collective-permute-start.14 = (bf16[2,432,384]{2,1,0:T(8,128)(2,1)S(1)}, bf16[2,432,384]{2,1,0:T(8,128)(2,1)S(1)}, u32[]{:S(2)}, u32[]{:S(2)}) collective-permute-start(bf16[2,432,384]{2,1,0:T(8,128)(2,1)S(1)} %pad_maximum_fusion.5), channel_id=1, source_target_pairs={{0,8},{4,12},{8,0},{12,4},{16,24},{20,28},{24,16},{28,20},{1,9},{5... | collective-permute-start | bytes 1990664 | tf_op jit(solution)/shard_map/ppermute | solution.py:484
  61.1 34.4 %collective-permute-start.15 = (bf16[2,432,384]{2,1,0:T(8,128)(2,1)S(1)}, bf16[2,432,384]{2,1,0:T(8,128)(2,1)S(1)}, u32[]{:S(2)}, u32[]{:S(2)}) collective-permute-start(bf16[2,432,384]{2,1,0:T(8,128)(2,1)S(1)} %pad_maximum_fusion.5), channel_id=1, source_target_pairs={{0,16},{4,20},{8,24},{12,28},{16,0},{20,4},{24,8},{28,12},{1,17},{... | collective-permute-start | bytes 1990664 | tf_op jit(solution)/shard_map/ppermute | solution.py:484
  64.8 30.7 %collective-permute-start.16 = (bf16[2,432,384]{2,1,0:T(8,128)(2,1)S(1)}, bf16[2,432,384]{2,1,0:T(8,128)(2,1)S(1)}, u32[]{:S(2)}, u32[]{:S(2)}) collective-permute-start(bf16[2,432,384]{2,1,0:T(8,128)(2,1)S(1)} %pad_maximum_fusion.5), channel_id=1, source_target_pairs={{0,24},{4,28},{8,16},{12,20},{16,8},{20,12},{24,0},{28,4},{1,25},{... | collective-permute-start | bytes 1990664 | tf_op jit(solution)/shard_map/ppermute | solution.py:484
  69.2 27.6 %collective-permute-start.17 = (bf16[432,384]{1,0:T(8,128)(2,1)S(1)}, bf16[432,384]{1,0:T(8,128)(2,1)S(1)}, u32[]{:S(2)}, u32[]{:S(2)}) collective-permute-start(bf16[432,384]{1,0:T(8,128)(2,1)S(1)} %pad_maximum_fusion.6), channel_id=1, source_target_pairs={{0,8},{4,12},{8,0},{12,4},{16,24},{20,28},{24,16},{28,20},{1,9},{5... | collective-permute-start | bytes 995336 | tf_op jit(solution)/shard_map/ppermute | solution.py:484
  70.5 34.5 %collective-permute-start.18 = (bf16[432,384]{1,0:T(8,128)(2,1)S(1)}, bf16[432,384]{1,0:T(8,128)(2,1)S(1)}, u32[]{:S(2)}, u32[]{:S(2)}) collective-permute-start(bf16[432,384]{1,0:T(8,128)(2,1)S(1)} %pad_maximum_fusion.6), channel_id=1, source_target_pairs={{0,16},{4,20},{8,24},{12,28},{16,0},{20,4},{24,8},{28,12},{1,17},{... | collective-permute-start | bytes 995336 | tf_op jit(solution)/shard_map/ppermute | solution.py:484
  75.4 29.5 %collective-permute-start.19 = (bf16[432,384]{1,0:T(8,128)(2,1)S(1)}, bf16[432,384]{1,0:T(8,128)(2,1)S(1)}, u32[]{:S(2)}, u32[]{:S(2)}) collective-permute-start(bf16[432,384]{1,0:T(8,128)(2,1)S(1)} %pad_maximum_fusion.6), channel_id=1, source_target_pairs={{0,24},{4,28},{8,16},{12,20},{16,8},{20,12},{24,0},{28,4},{1,25},{... | collective-permute-start | bytes 995336 | tf_op jit(solution)/shard_map/ppermute | solution.py:484
  106.2 19.7 %collective-permute-start.23 = (bf16[4,2,432,384]{3,2,1,0:T(8,128)(2,1)S(1)}, bf16[4,2,432,384]{3,2,1,0:T(8,128)(2,1)}, u32[]{:S(2)}, u32[]{:S(2)}) collective-permute-start(bf16[4,2,432,384]{3,2,1,0:T(8,128)(2,1)S(1)} %pad_maximum_fusion.near_own), channel_id=1, source_target_pairs={{0,4},{4,0},{8,12},{12,8},{16,20},{20,16},{24,28},{28,24},{1,5},{5... | collective-permute-start | bytes 7962632 | tf_op jit(solution)/shard_map/ppermute | solution.py:484
  109.5 16.5 %collective-permute-start.24 = (bf16[4,432,384]{2,1,0:T(8,128)(2,1)}, bf16[4,432,384]{2,1,0:T(8,128)(2,1)}, u32[]{:S(2)}, u32[]{:S(2)}) collective-permute-start(bf16[4,432,384]{2,1,0:T(8,128)(2,1)} %pad_maximum_fusion.2.far_own), channel_id=1, source_target_pairs={{0,4},{4,0},{8,12},{12,8},{16,20},{20,16},{24,28},{28,24},{1,5},{5... | collective-permute-start | bytes 3981320 | tf_op jit(solution)/shard_map/ppermute | solution.py:484
  176.1 33.6 %collective-permute-start.30 = (bf16[2,448,384]{2,1,0:T(8,128)(2,1)S(1)}, bf16[2,448,384]{2,1,0:T(8,128)(2,1)S(1)}, u32[]{:S(2)}, u32[]{:S(2)}) collective-permute-start(bf16[2,448,384]{2,1,0:T(8,128)(2,1)S(1)} %get-tuple-element.175), channel_id=1, source_target_pairs={{0,8},{4,12},{8,0},{12,4},{16,24},{20,28},{24,16},{28,20},{1,9},{5... | collective-permute-start | bytes 2064392 | tf_op jit(solution)/shard_map/ppermute | solution.py:484
  176.4 33.3 %collective-permute-start.31 = (bf16[2,448,384]{2,1,0:T(8,128)(2,1)S(1)}, bf16[2,448,384]{2,1,0:T(8,128)(2,1)}, u32[]{:S(2)}, u32[]{:S(2)}) collective-permute-start(bf16[2,448,384]{2,1,0:T(8,128)(2,1)S(1)} %get-tuple-element.176), channel_id=1, source_target_pairs={{0,16},{4,20},{8,24},{12,28},{16,0},{20,4},{24,8},{28,12},{1,17},{... | collective-permute-start | bytes 2064392 | tf_op jit(solution)/shard_map/ppermute | solution.py:484
  177.3 32.4 %collective-permute-start.32 = (bf16[2,448,384]{2,1,0:T(8,128)(2,1)S(1)}, bf16[2,448,384]{2,1,0:T(8,128)(2,1)}, u32[]{:S(2)}, u32[]{:S(2)}) collective-permute-start(bf16[2,448,384]{2,1,0:T(8,128)(2,1)S(1)} %get-tuple-element.177), channel_id=1, source_target_pairs={{0,8},{4,12},{8,0},{12,4},{16,24},{20,28},{24,16},{28,20},{1,9},{5... | collective-permute-start | bytes 2064392 | tf_op jit(solution)/shard_map/ppermute | solution.py:484
  177.8 31.9 %collective-permute-start.33 = (bf16[2,448,384]{2,1,0:T(8,128)(2,1)S(1)}, bf16[2,448,384]{2,1,0:T(8,128)(2,1)}, u32[]{:S(2)}, u32[]{:S(2)}) collective-permute-start(bf16[2,448,384]{2,1,0:T(8,128)(2,1)S(1)} %get-tuple-element.178), channel_id=1, source_target_pairs={{0,16},{4,20},{8,24},{12,28},{16,0},{20,4},{24,8},{28,12},{1,17},{... | collective-permute-start | bytes 2064392 | tf_op jit(solution)/shard_map/ppermute | solution.py:484
  228.3 12.8 %collective-permute-start.35 = (bf16[4,112,1152]{2,1,0:T(8,128)(2,1)}, bf16[4,112,1152]{2,1,0:T(8,128)(2,1)S(1)}, u32[]{:S(2)}, u32[]{:S(2)}) collective-permute-start(bf16[4,112,1152]{2,1,0:T(8,128)(2,1)} %get-tuple-element.187), channel_id=1, source_target_pairs={{0,4},{4,0},{8,12},{12,8},{16,20},{20,16},{24,28},{28,24},{1,5},{5... | collective-permute-start | bytes 3096584 | tf_op jit(solution)/shard_map/ppermute | solution.py:484
  231.9 26.7 %collective-permute-start.43 = (bf16[2,448,384]{2,1,0:T(8,128)(2,1)}, bf16[2,448,384]{2,1,0:T(8,128)(2,1)}, u32[]{:S(2)}, u32[]{:S(2)}) collective-permute-start(bf16[2,448,384]{2,1,0:T(8,128)(2,1)} %get-tuple-element.199), channel_id=1, source_target_pairs={{0,8},{4,12},{8,0},{12,4},{16,24},{20,28},{24,16},{28,20},{1,9},{5... | collective-permute-start | bytes 2064392 | tf_op jit(solution)/shard_map/ppermute | solution.py:484
  233.1 26.1 %collective-permute-start.44 = (bf16[2,448,384]{2,1,0:T(8,128)(2,1)}, bf16[2,448,384]{2,1,0:T(8,128)(2,1)}, u32[]{:S(2)}, u32[]{:S(2)}) collective-permute-start(bf16[2,448,384]{2,1,0:T(8,128)(2,1)} %get-tuple-element.200), channel_id=1, source_target_pairs={{0,16},{4,20},{8,24},{12,28},{16,0},{20,4},{24,8},{28,12},{1,17},{... | collective-permute-start | bytes 2064392 | tf_op jit(solution)/shard_map/ppermute | solution.py:484
  242.9 18.6 %collective-permute-start.36 = (bf16[112,1152]{1,0:T(8,128)(2,1)S(1)}, bf16[112,1152]{1,0:T(8,128)(2,1)S(1)}, u32[]{:S(2)}, u32[]{:S(2)}) collective-permute-start(bf16[112,1152]{1,0:T(8,128)(2,1)S(1)} %get-tuple-element.190), channel_id=1, source_target_pairs={{0,1},{1,2},{2,3},{3,0},{4,5},{5,6},{6,7},{7,4},{8,9},{9,10},{10,1... | collective-permute-start | bytes 774152 | tf_op jit(solution)/shard_map/ppermute | solution.py:489
  253.3 16.1 %collective-permute-start.37 = (bf16[112,1152]{1,0:T(8,128)(2,1)S(1)}, bf16[112,1152]{1,0:T(8,128)(2,1)S(1)}, u32[]{:S(2)}, u32[]{:S(2)}) collective-permute-start(bf16[112,1152]{1,0:T(8,128)(2,1)S(1)} %get-tuple-element.191), channel_id=1, source_target_pairs={{0,2},{1,3},{2,0},{3,1},{4,6},{5,7},{6,4},{7,5},{8,10},{9,11},{10,... | collective-permute-start | bytes 774152 | tf_op jit(solution)/shard_map/ppermute | solution.py:489
  257.7 21.1 %collective-permute-start.39 = (bf16[192,768]{1,0:T(8,128)(2,1)S(1)}, bf16[192,768]{1,0:T(8,128)(2,1)S(1)}, u32[]{:S(2)}, u32[]{:S(2)}) collective-permute-start(bf16[192,768]{1,0:T(8,128)(2,1)S(1)} %get-tuple-element.193), channel_id=1, source_target_pairs={{0,8},{4,12},{8,0},{12,4},{16,24},{20,28},{24,16},{28,20},{1,9},{5... | collective-permute-start | bytes 884744 | tf_op jit(solution)/shard_map/ppermute | solution.py:484
  258.6 20.2 %collective-permute-start.40 = (bf16[192,768]{1,0:T(8,128)(2,1)S(1)}, bf16[192,768]{1,0:T(8,128)(2,1)S(1)}, u32[]{:S(2)}, u32[]{:S(2)}) collective-permute-start(bf16[192,768]{1,0:T(8,128)(2,1)S(1)} %get-tuple-element.194), channel_id=1, source_target_pairs={{0,16},{4,20},{8,24},{12,28},{16,0},{20,4},{24,8},{28,12},{1,17},{... | collective-permute-start | bytes 884744 | tf_op jit(solution)/shard_map/ppermute | solution.py:484
  259.2 19.6 %collective-permute-start.41 = (bf16[192,768]{1,0:T(8,128)(2,1)S(1)}, bf16[192,768]{1,0:T(8,128)(2,1)S(1)}, u32[]{:S(2)}, u32[]{:S(2)}) collective-permute-start(bf16[192,768]{1,0:T(8,128)(2,1)S(1)} %get-tuple-element.195), channel_id=1, source_target_pairs={{0,8},{4,12},{8,0},{12,4},{16,24},{20,28},{24,16},{28,20},{1,9},{5... | collective-permute-start | bytes 884744 | tf_op jit(solution)/shard_map/ppermute | solution.py:484
  261.5 17.3 %collective-permute-start.42 = (bf16[192,768]{1,0:T(8,128)(2,1)S(1)}, bf16[192,768]{1,0:T(8,128)(2,1)S(1)}, u32[]{:S(2)}, u32[]{:S(2)}) collective-permute-start(bf16[192,768]{1,0:T(8,128)(2,1)S(1)} %get-tuple-element.196), channel_id=1, source_target_pairs={{0,16},{4,20},{8,24},{12,28},{16,0},{20,4},{24,8},{28,12},{1,17},{... | collective-permute-start | bytes 884744 | tf_op jit(solution)/shard_map/ppermute | solution.py:484
  285.3 16.5 %collective-permute-start.45 = (bf16[448,384]{1,0:T(8,128)(2,1)S(1)}, bf16[448,384]{1,0:T(8,128)(2,1)S(1)}, u32[]{:S(2)}, u32[]{:S(2)}) collective-permute-start(bf16[448,384]{1,0:T(8,128)(2,1)S(1)} %get-tuple-element.211), channel_id=1, source_target_pairs={{0,1},{1,2},{2,3},{3,0},{4,5},{5,6},{6,7},{7,4},{8,9},{9,10},{10,1... | collective-permute-start | bytes 1032200 | tf_op jit(solution)/shard_map/ppermute | solution.py:489
  285.6 26.6 %collective-permute-start.46 = (bf16[448,384]{1,0:T(8,128)(2,1)S(1)}, bf16[448,384]{1,0:T(8,128)(2,1)S(1)}, u32[]{:S(2)}, u32[]{:S(2)}) collective-permute-start(bf16[448,384]{1,0:T(8,128)(2,1)S(1)} %get-tuple-element.212), channel_id=1, source_target_pairs={{0,2},{1,3},{2,0},{3,1},{4,6},{5,7},{6,4},{7,5},{8,10},{9,11},{10,... | collective-permute-start | bytes 1032200 | tf_op jit(solution)/shard_map/ppermute | solution.py:489
  289.6 28.8 %collective-permute-start.47 = (bf16[448,384]{1,0:T(8,128)(2,1)S(1)}, bf16[448,384]{1,0:T(8,128)(2,1)S(1)}, u32[]{:S(2)}, u32[]{:S(2)}) collective-permute-start(bf16[448,384]{1,0:T(8,128)(2,1)S(1)} %get-tuple-element.213), channel_id=1, source_target_pairs={{0,3},{1,0},{2,1},{3,2},{4,7},{5,4},{6,5},{7,6},{8,11},{9,8},{10,9... | collective-permute-start | bytes 1032200 | tf_op jit(solution)/shard_map/ppermute | solution.py:489
  320.3 14.9 %collective-permute-start.55 = (bf16[448,384]{1,0:T(8,128)(2,1)S(1)}, bf16[448,384]{1,0:T(8,128)(2,1)S(1)}, u32[]{:S(2)}, u32[]{:S(2)}) collective-permute-start(bf16[448,384]{1,0:T(8,128)(2,1)S(1)} %add_convert_fusion.3), channel_id=1, source_target_pairs={{0,24},{4,28},{8,16},{12,20},{16,8},{20,12},{24,0},{28,4},{1,25},{... | collective-permute-start | bytes 1032200 | tf_op jit(solution)/shard_map/ppermute | solution.py:484
  321.5 16.5 %collective-permute-start.56 = (bf16[4,112,1152]{2,1,0:T(8,128)(2,1)S(1)}, bf16[4,112,1152]{2,1,0:T(8,128)(2,1)S(1)}, u32[]{:S(2)}, u32[]{:S(2)}) collective-permute-start(bf16[4,112,1152]{2,1,0:T(8,128)(2,1)S(1)} %pad_maximum_fusion.4.own), channel_id=1, source_target_pairs={{0,4},{4,0},{8,12},{12,8},{16,20},{20,16},{24,28},{28,24},{1,5},{5... | collective-permute-start | bytes 3096584 | tf_op jit(solution)/shard_map/ppermute | solution.py:484
  335.5 12.4 %collective-permute-start.57 = (bf16[4,448,384]{2,1,0:T(8,128)(2,1)S(1)}, bf16[4,448,384]{2,1,0:T(8,128)(2,1)}, u32[]{:S(2)}, u32[]{:S(2)}) collective-permute-start(bf16[4,448,384]{2,1,0:T(8,128)(2,1)S(1)} %pad_maximum_fusion.1.own), channel_id=1, source_target_pairs={{0,4},{4,0},{8,12},{12,8},{16,20},{20,16},{24,28},{28,24},{1,5},{5... | collective-permute-start | bytes 4128776 | tf_op jit(solution)/shard_map/ppermute | solution.py:484
  (56 other events, 419.0 us)

commit v4 on v3

--- a/solution.py
+++ b/solution.py
@@ -489,9 +489,17 @@
     return lax.ppermute(value, "wa", [(i, (i + step) % count) for i in range(count)])
 
 
-def ring_far(one, three):
-    middle = one.shape[0] // 2
-    return jnp.concatenate([turned(one[:middle], 1), turned(three[middle:], 3)], axis=0)
+def narrowed(value, width):
+    return [value[:, at : at + width] for at in range(0, value.shape[1], width)]
+
+
+def widened(value, count):
+    rows = value.shape[0] // count
+    return jnp.concatenate([value[rows * k : rows * (k + 1)] for k in range(count)], axis=1)
+
+
+def ordered(*values):
+    return lax.optimization_barrier(values)
 
 
 def as_column(row):
@@ -600,16 +608,21 @@
     lax.fori_loop(0, CHIPS, piece, 0)
 
 
-def masked_keys(kv, flag):
-    wide = kv.astype(jnp.float32)
-    low = lax.broadcasted_iota(jnp.int32, kv.shape, 1) < HD
-    both = jnp.where(low, wide, pltpu.roll(wide, HD, 1))
-    return jnp.where(low == flag, 0.0, both)
+def ones_where(shape, test):
+    row = lax.broadcasted_iota(jnp.int32, shape, 0)
+    column = lax.broadcasted_iota(jnp.int32, shape, 1)
+    return jnp.where(test(row, column), 1.0, 0.0).astype(jnp.bfloat16)
+
+
+def unit(size):
+    return ones_where((size, size), lambda row, column: row == column)
 
 
 def attend_kernel(place, q_ref, own, other, out, turned_out, lse, bounds, keys, values, seg_col, seg_row, acc):
     tok = q_ref.shape[1]
     core = place[1]
+    twice = ones_where((2 * HD, 2 * HD), lambda row, column: row == lax.rem(column, HD))
+    upper = ones_where((HD, 2 * HD), lambda row, column: column == row + HD)
 
     def prepare(j, unused):
         for source, side in ((own, core), (other, 1 - core)):
@@ -623,8 +636,9 @@
             flag = column - 2.0 * segment == 1.0
             for h in range(3):
                 kv = source[j, :tok, 2 * HD * h : 2 * HD * (h + 1)]
-                keys[h, at, :] = masked_keys(kv, flag).astype(jnp.bfloat16)
-                values[h, :, at] = kv.astype(jnp.float32).T[HD:].astype(jnp.bfloat16)
+                low = lax.broadcasted_iota(jnp.int32, kv.shape, 1) < HD
+                keys[h, at, :] = jnp.where(low == flag, 0.0, plain_product(kv, twice)).astype(jnp.bfloat16)
+                values[h, :, at] = lanes_product(upper, kv).astype(jnp.bfloat16)
         return 0
 
     lax.fori_loop(0, CHIPS, prepare, 0)
@@ -686,21 +700,26 @@
     dq_ref,
     dkv_own,
     dkv_other,
-    keys,
+    sources,
     turned_keys,
-    values,
-    grad_keys,
-    grad_values,
+    grads,
     seg_col,
     seg_row,
     acc,
     grad,
+    pair,
+    mixed,
 ):
     tok = q_ref.shape[1]
     chip, core = place[0], place[1]
     wide = 2 * HD
     for m, piece in enumerate((grad0, grad1, grad2, grad3)):
         grad[jnp.bitwise_xor(chip, m)] = piece[...]
+    twice = ones_where((wide, wide), lambda row, column: row == lax.rem(column, HD))
+    turned_twice = ones_where((wide, wide), lambda row, column: column == lax.rem(row, HD))
+    folded = ones_where((wide, wide), lambda row, column: column == lax.rem(row, HD))
+    all_rows, group = unit(tok), unit(3 * HD)
+    pair[...] = jnp.zeros_like(pair)
 
     def prepare(j, unused):
         for source, side in ((own, core), (other, 1 - core)):
@@ -712,14 +731,18 @@
             segment = segment_of(column)
             seg_col[at, :] = segment
             flag = column - 2.0 * segment == 1.0
+            row_flag = tags - 2.0 * segment_of(tags) == 1.0
             for h in range(3):
                 kv = source[j, :tok, wide * h : wide * (h + 1)]
-                key = masked_keys(kv, flag)
-                keys[h, at, :] = key.astype(jnp.bfloat16)
-                turned_keys[h, :, at] = key.T.astype(jnp.bfloat16)
-                values[h, at, :] = kv
-                grad_keys[h, at, :] = jnp.zeros((tok, wide), jnp.float32)
-                grad_values[h, at, :] = jnp.zeros((tok, wide), jnp.float32)
+                low = lax.broadcasted_iota(jnp.int32, kv.shape, 1) < HD
+                sources[h, at, :wide] = jnp.where(low == flag, 0.0, plain_product(kv, twice)).astype(
+                    jnp.bfloat16
+                )
+                sources[h, at, wide:] = kv
+                both = lanes_product(turned_twice, kv)
+                low = lax.broadcasted_iota(jnp.int32, both.shape, 0) < HD
+                turned_keys[h, :, at] = jnp.where(low == row_flag, 0.0, both).astype(jnp.bfloat16)
+                grads[h, at, :] = jnp.zeros((tok, 2 * wide), jnp.float32)
         return 0
 
     lax.fori_loop(0, CHIPS, prepare, 0)
@@ -729,34 +752,33 @@
         seg = segment_of(tags)
         slot = jnp.bitwise_xor(chip, j)
         flag = as_column(tags - 2.0 * seg) == 1.0
-        turned_grad = grad[j].astype(jnp.float32).T
-        deltas, shifts, padded = [], [], []
+        turned_grad = lanes_product(group, grad[j])
+        deltas, shifts = [], []
         for h in range(3):
             rows = slice(HD * h, HD * (h + 1))
             deltas.append(jnp.sum(turned_grad[rows] * turned_out[j, rows, :], axis=0, keepdims=True))
             shifts.append(lse[j, h])
-            head = grad[j, :, rows]
-            padded.append(jnp.concatenate([jnp.zeros_like(head), head], axis=1))
+            pair[h, :tok, :wide] = q_ref[j, :, wide * h : wide * (h + 1)]
+            pair[h, tok:, wide + HD :] = grad[j, :, rows]
         acc[...] = jnp.zeros_like(acc)
 
         def step(t, carry):
             at = pl.ds(pl.multiple_of(t * KEY_BLOCK, KEY_BLOCK), KEY_BLOCK)
             column = seg_col[at, :]
             same = jnp.concatenate([column] * (tok // TILE), axis=1) == seg
+            both = [lanes_product(sources[h, at, :], pair[h]) for h in range(3)]
             for h in range(3):
-                q = q_ref[j, :, wide * h : wide * (h + 1)]
-                scores = lanes_product(keys[h, at, :], q)
-                probs = jnp.where(same, jnp.exp(scores - shifts[h]), 0.0)
-                grad_probs = lanes_product(values[h, at, :], padded[h])
-                grad_scores = (probs * (grad_probs - deltas[h])).astype(jnp.bfloat16)
-                grad_values[h, at, :] += plain_product(probs.astype(jnp.bfloat16), padded[h])
-                grad_keys[h, at, :] += plain_product(grad_scores, q)
-                acc[h] += plain_product(turned_keys[h, :, at], grad_scores)
+                probs = jnp.where(same, jnp.exp(both[h][:, :tok] - shifts[h]), 0.0)
+                mixed[h, :, :tok] = (probs * (both[h][:, tok:] - deltas[h])).astype(jnp.bfloat16)
+                mixed[h, :, tok:] = probs.astype(jnp.bfloat16)
+            for h in range(3):
+                grads[h, at, :] += plain_product(mixed[h], pair[h])
+                acc[h] += plain_product(turned_keys[h, :, at], mixed[h, :, :tok])
             return carry
 
         lax.fori_loop(bounds[0, j], bounds[1, j], step, 0)
         for h in range(3):
-            dq = acc[h].T * (HD**-0.5)
+            dq = lanes_product(all_rows, (acc[h] * (HD**-0.5)).astype(jnp.bfloat16))
             at = 2 * wide * h
             dq_ref[slot, :, at : at + wide] = jnp.where(flag, 0.0, dq).astype(jnp.bfloat16)
             dq_ref[slot, :, at + wide : at + 2 * wide] = jnp.where(flag, dq, 0.0).astype(jnp.bfloat16)
@@ -772,11 +794,10 @@
             tags = seg_row[shard][:1]
             flag = as_column(tags - 2.0 * segment_of(tags)) == 1.0
             for h in range(3):
-                both = grad_keys[h, at, :]
-                low = lax.broadcasted_iota(jnp.int32, both.shape, 1) < HD
-                picked = jnp.where(flag, pltpu.roll(both, HD, 1), both)
+                low = lax.broadcasted_iota(jnp.int32, (tok, wide), 1) < HD
+                dk = jnp.where(low == flag, 0.0, grads[h, at, :wide]).astype(jnp.bfloat16)
                 target[slot, :, wide * h : wide * (h + 1)] = jnp.where(
-                    low, picked, grad_values[h, at, :]
+                    low, plain_product(dk, folded), grads[h, at, wide:]
                 ).astype(jnp.bfloat16)
         return 0
 
@@ -1009,7 +1030,7 @@
         pltpu.make_async_copy(target, target, out_sems.at[sem]).wait()
 
 
-def head_grads_kernel(place, tokens, dq, dkv_own, dkv_other, dkv, kept, sent, acc):
+def head_grads_kernel(place, tokens, dq, dkv, kept, sent, acc):
     tok = dq.shape[1]
     core = place[1]
     wide = dq.shape[2]
@@ -1018,8 +1039,6 @@
 
     def piece(m, carry):
         text = tokens[m, :tok]
-        both = dkv_own[m].astype(jnp.float32) + dkv_other[m].astype(jnp.float32)
-        dkv[m] = both.astype(jnp.bfloat16)
         text_turned = text.astype(jnp.float32).T.astype(jnp.bfloat16)
         acc[:, :wide] += plain_product(text_turned, dq[m])
         acc[:, wide:] += plain_product(text_turned, dkv[m])
@@ -1038,10 +1057,12 @@
             target[z, rows:] = jnp.where(side == 0, sums, 0.0).astype(jnp.bfloat16)
 
 
-def token_grads_kernel(dq, dkv, weight, partial):
+def token_grads_kernel(dq, dkv_own, dkv_other, weight, dkv, partial):
     wide = dq.shape[2]
 
     def piece(m, carry):
+        both = dkv_own[m].astype(jnp.float32) + dkv_other[m].astype(jnp.float32)
+        dkv[m] = both.astype(jnp.bfloat16)
         partial[m] = (
             lanes_product(dq[m], weight[:, :wide]) + lanes_product(dkv[m], weight[:, wide:])
         ).astype(jnp.bfloat16)
@@ -1110,14 +1131,14 @@
     return pl.BlockSpec(memory_space=pl.ANY)
 
 
-def whole_call(kernel, operands, outs, scratch=(), micros=1):
+def whole_call(kernel, operands, outs, scratch=(), micros=1, mebibytes=16):
     return pl.pallas_call(
         kernel,
         out_shape=[jax.ShapeDtypeStruct(shape, dtype) for shape, dtype, _ in outs],
         in_specs=[spec() for _, spec in operands],
         out_specs=[spec() for _, _, spec in outs],
         scratch_shapes=list(scratch),
-        compiler_params=pltpu.CompilerParams(vmem_limit_bytes=58 << 20),
+        compiler_params=pltpu.CompilerParams(vmem_limit_bytes=mebibytes << 20),
         cost_estimate=pl.CostEstimate(
             flops=micros * FLOPS_PER_MICRO, bytes_accessed=micros << 20, transcendentals=0
         ),
@@ -1172,10 +1193,6 @@
     cut = tok // 2
     text_x, text_y = swapped(text, 2), swapped(text, 4)
 
-    def after(value, *earlier):
-        return lax.optimization_barrier((value, *earlier))[0]
-
-
     lines = (
         bias_wordword,
         bias_wordentity,
@@ -1199,18 +1216,27 @@
         [((half + TAG_ROWS, 6 * group), bf16, vmem), ((2 * rows + quarter, slot_w), bf16, vmem)],
         [pltpu.SemaphoreType.DMA((4,))],
         micros=3,
+        mebibytes=58,
     )
     one, three = turned(mine, 1), turned(mine, 3)
-    text_x, text_y, one, three = lax.optimization_barrier((text_x, text_y, one, three))
+    text_x, text_y, one, three, slot = ordered(text_x, text_y, one, three, slot)
     text_far = swapped(text_x[:cut], 4), swapped(text_y[cut:], 2)
-    two = ring_far(one, three)
-    slot = after(slot, text_x, text_y, one, three)
-    slot_one, slot_three = turned(slot, 1), turned(slot, 3)
-    *text_far, two, slot_one, slot_three = lax.optimization_barrier((*text_far, two, slot_one, slot_three))
-    near_slot = jnp.stack([slot_one, slot_three])
-    far_slot = ring_far(slot_one, slot_three)
+
+    split, wide = half // 2, 6 * group // slot_w
+    right = jnp.concatenate([*narrowed(one[:split], slot_w), slot], axis=0)
+    left = jnp.concatenate([*narrowed(three[split:], slot_w), slot], axis=0)
+    right, left = turned(right, 1), turned(left, 3)
+    *text_far, right, left = ordered(*text_far, right, left)
+    cut_right, cut_left = split * wide, (half + TAG_ROWS - split) * wide
+    two = jnp.concatenate([widened(right[:cut_right], wide), widened(left[:cut_left], wide)], axis=0)
+    near_slot = jnp.stack([right[cut_right:], left[cut_left:]])
+    middle = TAG_ROWS * (slot.shape[0] // TAG_ROWS // 2)
+    far_slot = turned(near_slot[0, :middle], 1), turned(near_slot[1, middle:], 3)
     mine = jnp.stack([mine, one, two, three])
     theirs = swapped(mine, 1)
+    near_x, near_y = swapped(near_slot, 2), swapped(near_slot, 4)
+    theirs, *far_slot = ordered(theirs, *far_slot)
+    far_slot = jnp.concatenate(far_slot, axis=0)
     order = (wa - jnp.arange(parts)) % parts
     vectors = jnp.take(mine[:, half + 1], order, axis=0).reshape(parts, 6, rows)
     vectors = jnp.pad(jnp.transpose(vectors, (1, 0, 2)).reshape(6, dmod), ((0, 2), (0, 0))).astype(f32)
@@ -1226,11 +1252,14 @@
             ((CHIPS, tok + TAG_ROWS, 2 * group), bf16, vmem),
         ],
         micros=8,
-    )
+        mebibytes=16,
+    )
+    kv, near_x, near_y, far_slot = ordered(kv, near_x, near_y, far_slot)
     kv_other = swapped(kv, 1)
-    kv_other, far_slot = lax.optimization_barrier((kv_other, far_slot))
-    far_slots = [far_slot] + [swapped(far_slot, 2 * m) for m in range(1, CHIPS)]
-    near_slots = [near_slot] + [swapped(near_slot, 2 * m) for m in range(1, CHIPS)]
+    to_x = jnp.concatenate([far_slot, near_y[1]], axis=0)
+    to_y = jnp.concatenate([far_slot, near_x[0]], axis=0)
+    kv_other, to_x, to_y = ordered(kv_other, to_x, to_y)
+    to_x, to_y, to_far = swapped(to_x, 2), swapped(to_y, 4), swapped(far_slot, 6)
 
     context, turned_out, lse, bounds = whole_call(
         attend_kernel,
@@ -1249,16 +1278,19 @@
             pltpu.VMEM((3, HD, tok), f32),
         ],
         micros=25,
-    )
-    barrier = lax.optimization_barrier((context, *near_slots, *far_slots))
-    context, near_slots, far_slots = barrier[0], jnp.stack(barrier[1 : 1 + CHIPS]), jnp.stack(barrier[1 + CHIPS :])
-    near_slots = near_slots, swapped(near_slots, 1)
-    far_slots = far_slots, swapped(far_slots, 1)
+        mebibytes=20,
+    )
+    context, to_x, to_y, to_far = ordered(context, to_x, to_y, to_far)
 
     def exchanged(value):
         return [value[0]] + [swapped(value[m], 2 * m) for m in range(1, CHIPS)]
 
     contexts = exchanged(context)
+    deep = slot.shape[0]
+    near_slots = jnp.stack([near_slot, near_x, near_y, jnp.stack([to_y[deep:], to_x[deep:]])])
+    near_slots = near_slots, swapped(near_slots, 1)
+    far_slots = jnp.stack([far_slot, to_x[:deep], to_y[:deep], to_far])
+    far_slots = far_slots, swapped(far_slots, 1)
 
     slot_rows = 2 * rows + quarter + TAG_ROWS
     result, grad_sum, grad_context, kept, sent_far, sent_near = whole_call(
@@ -1292,6 +1324,7 @@
             pltpu.SemaphoreType.DMA((3,)),
         ],
         micros=35,
+        mebibytes=50,
     )
     grad_pieces = exchanged(grad_context)
 
@@ -1325,17 +1358,18 @@
             ((CHIPS, tok, 2 * group), bf16, vmem),
         ],
         [
-            pltpu.VMEM((3, length, 2 * HD), bf16),
+            pltpu.VMEM((3, length, 4 * HD), bf16),
             pltpu.VMEM((3, 2 * HD, length), bf16),
-            pltpu.VMEM((3, length, 2 * HD), bf16),
-            pltpu.VMEM((3, length, 2 * HD), f32),
-            pltpu.VMEM((3, length, 2 * HD), f32),
+            pltpu.VMEM((3, length, 4 * HD), f32),
             pltpu.VMEM((length, TILE), f32),
             pltpu.VMEM((2 * CHIPS, 8, tok), f32),
             pltpu.VMEM((3, 2 * HD, tok), f32),
             pltpu.VMEM((CHIPS, tok, group), bf16),
+            pltpu.VMEM((3, 2 * tok, 4 * HD), bf16),
+            pltpu.VMEM((3, KEY_BLOCK, 2 * tok), bf16),
         ],
         micros=40,
+        mebibytes=36,
     )
     dq, dkv, dkv_sent, far_x, far_y, near_x, near_y = lax.optimization_barrier(
         (dq, dkv, dkv_sent, far_x, far_y, near_x, near_y)
@@ -1343,33 +1377,34 @@
     dkv_received = swapped(dkv_sent, 1)
     last_x = added(kept[1, lower], received[1, lower], far_y).astype(bf16)
     last_y = added(kept[2, upper], received[2, upper], far_x).astype(bf16)
-    last_x, last_y = lax.optimization_barrier((last_x, last_y))
+    last_x, last_y = ordered(last_x, last_y)
     last_x, last_y = swapped(last_x, 2), swapped(last_y, 4)
-    dkv, head_kept, head_sent = whole_call(
+    dkv, partial = whole_call(
+        token_grads_kernel,
+        [(a, vmem) for a in (dq, dkv, dkv_received, weight)],
+        [((CHIPS, tok, 2 * group), bf16, vmem), ((CHIPS, tok, dmod), bf16, vmem)],
+        micros=8,
+        mebibytes=16,
+    )
+    head_kept, head_sent = whole_call(
         head_grads_kernel,
-        [(place, smem)] + [(a, vmem) for a in (all_text, dq, dkv, dkv_received)],
+        [(place, smem)] + [(a, vmem) for a in (all_text, dq, dkv)],
         [
-            ((CHIPS, tok, 2 * group), bf16, vmem),
             ((parts, half + TAG_ROWS, 6 * group), bf16, vmem),
             ((parts, half + TAG_ROWS, 6 * group), bf16, vmem),
         ],
         [pltpu.VMEM((dmod, 6 * group), f32)],
         micros=10,
-    )
-    head_received = swapped(head_sent, 1)
-    (partial,) = whole_call(
-        token_grads_kernel,
-        [(a, vmem) for a in (dq, dkv, weight)],
-        [((CHIPS, tok, dmod), bf16, vmem)],
-        micros=8,
-    )
-    partial, head_received = lax.optimization_barrier((partial, head_received))
-
-    def parts_sent(value):
-        kept_part = lax.dynamic_index_in_dim(value, wa, 0, keepdims=False)
-        return [kept_part] + [
-            lax.dynamic_index_in_dim(value, (wa + k) % parts, 0, keepdims=False) for k in range(1, parts)
+        mebibytes=20,
+    )
+    head_kept, head_sent, last_x, last_y = ordered(head_kept, head_sent, last_x, last_y)
+
+    def parts_sent(*values):
+        shards = [
+            added(*(lax.dynamic_index_in_dim(v, (wa + k) % parts, 0, keepdims=False) for v in values))
+            for k in range(parts)
         ]
+        return [v.astype(bf16) for v in shards]
 
     def parts_moved(values):
         return [turned(v, k) for k, v in enumerate(values) if k]
@@ -1378,15 +1413,6 @@
         return [swapped(value, 2 * m) for m in range(1, CHIPS)]
 
     low, high = slice(0, cut), slice(cut, None)
-    head_parts = parts_sent(added(head_kept, head_received).astype(bf16))
-    text_sent = [partial[3, low], partial[3, high], partial[1, low], partial[2, high]]
-    barrier = lax.optimization_barrier((*head_parts, *text_sent))
-    head_parts, text_sent = barrier[:parts], barrier[parts:]
-    head_moved = parts_moved(head_parts)
-    text_moved = [swapped(v, 2 << (k % 2)) for k, v in enumerate(text_sent)]
-    barrier = lax.optimization_barrier((*head_moved, *text_moved, last_x, last_y))
-    head_moved, text_moved, last_x, last_y = barrier[:3], barrier[3:7], barrier[7], barrier[8]
-
     summed = jnp.concatenate(
         [
             added(kept[0, upper], received[0, upper], near_x, last_y),
@@ -1395,42 +1421,56 @@
         axis=0,
     ).astype(bf16)
     dense_parts = parts_sent(summed)
-    far_x, far_y, near_x, near_y = text_moved
-    text_x = added(partial[1, high], far_y).astype(bf16)
-    text_y = added(partial[2, low], far_x).astype(bf16)
+    text_x = jnp.stack([partial[3, low], partial[1, low]])
+    text_y = jnp.stack([partial[3, high], partial[2, high]])
+    *dense_parts, text_x, text_y = ordered(*dense_parts, text_x, text_y)
+    dense_moved = parts_moved(dense_parts)
+    head_received = swapped(head_sent, 1)
+    text_x, text_y = swapped(text_x, 2), swapped(text_y, 4)
+    *dense_moved, text_x, text_y, head_received = ordered(*dense_moved, text_x, text_y, head_received)
+
+    count = dmod // slot_w
+    dense_summed = added(dense_parts[0], *dense_moved).astype(bf16)
+    (far_x, near_x), (far_y, near_y) = text_x, text_y
+    last_x = added(partial[1, high], far_y).astype(bf16)
+    last_y = added(partial[2, low], far_x).astype(bf16)
+    to_x = jnp.concatenate([dense_summed, *narrowed(last_x, slot_w)], axis=0)
+    to_y = jnp.concatenate([dense_summed, *narrowed(last_y, slot_w)], axis=0)
+    head_parts = parts_sent(head_kept, head_received)
+    *head_parts, to_x, to_y, dense_summed = ordered(*head_parts, to_x, to_y, dense_summed)
+    head_moved = parts_moved(head_parts)
+    to_x, to_y, dense_far = swapped(to_x, 2), swapped(to_y, 4), swapped(dense_summed, 6)
+    *head_moved, to_x, to_y, dense_far = ordered(*head_moved, to_x, to_y, dense_far)
+
+    deep = dense_summed.shape[0]
+    dense_all = jnp.stack([dense_summed, to_x[:deep], to_y[:deep], dense_far])
     head_summed = added(head_parts[0], *head_moved).astype(bf16)
-    barrier = lax.optimization_barrier((*dense_parts, text_x, text_y, head_summed))
-    dense_parts, text_x, text_y, head_summed = barrier[:parts], *barrier[parts:]
-    dense_moved = parts_moved(dense_parts)
-    text_x, text_y = swapped(text_x, 2), swapped(text_y, 4)
+    head_summed, dense_all = ordered(head_summed, dense_all)
     head_moved = chips_moved(head_summed)
-    barrier = lax.optimization_barrier((*dense_moved, text_x, text_y, *head_moved))
-    dense_moved, text_x, text_y, head_moved = barrier[:3], barrier[3], barrier[4], barrier[5:]
-
-    dense_summed = added(dense_parts[0], *dense_moved).astype(bf16)
-    head_all = jnp.stack([head_summed, *head_moved])
-    dense_summed, head_all = lax.optimization_barrier((dense_summed, head_all))
-    dense_moved = chips_moved(dense_summed)
-    *out_heads, sums = whole_call(
-        unpack_heads_kernel,
-        [(place, smem), (head_all, vmem), (swapped(head_all, 1), vmem)],
-        [((rows, dmod), f32, vmem) for _ in range(6)] + [((TAG_ROWS, 6 * group), f32, vmem)],
-        micros=4,
-    )
-    input_grads = grad_sum + jnp.concatenate(
-        [added(partial[0, low], near_x, text_y), added(partial[0, high], text_x, near_y)], axis=0
-    )
-    *dense_moved, input_grads = lax.optimization_barrier((*dense_moved, input_grads))
-    dense_all = jnp.stack([dense_summed, *dense_moved])
+    dense_other = swapped(dense_all, 1)
     out_inner, out_outer, out_output, small = whole_call(
         unpack_dense_kernel,
-        [(place, smem), (dense_all, vmem), (swapped(dense_all, 1), vmem)],
+        [(place, smem), (dense_all, vmem), (dense_other, vmem)],
         [
             ((rows, ff), f32, vmem),
             (outer_weight.shape, f32, vmem),
             ((rows, dmod), f32, vmem),
             ((TAG_ROWS, slot_w), f32, vmem),
         ],
+        micros=4,
+    )
+    last_x, last_y = widened(to_x[deep:], count), widened(to_y[deep:], count)
+    input_grads = grad_sum + jnp.concatenate(
+        [added(partial[0, low], near_x, last_y), added(partial[0, high], last_x, near_y)], axis=0
+    )
+    *head_moved, out_inner, out_outer, out_output, small, input_grads = ordered(
+        *head_moved, out_inner, out_outer, out_output, small, input_grads
+    )
+    head_all = jnp.stack([head_summed, *head_moved])
+    *out_heads, sums = whole_call(
+        unpack_heads_kernel,
+        [(place, smem), (head_all, vmem), (swapped(head_all, 1), vmem)],
+        [((rows, dmod), f32, vmem) for _ in range(6)] + [((TAG_ROWS, 6 * group), f32, vmem)],
         micros=4,
     )
 

time: 354 us -> 321 us (0.907)
  Pallas kernels: 123 us -> 105 us
  starting transfers between devices: 73.6 us -> 59.8 us
  local copies, waits for them, and re-layouts: 20.4 us -> 16.3 us
    ppermute x14 -> x12, starting transfers between devices: 31.7 us -> 11.2 us  [turned(): lax.ppermute(value, 'wa', [(i, (i + step) % count) for i in range(count)])]
    pallas_call x9, Pallas kernels: 123 us -> 105 us  [whole_call(): pl.pallas_call(kernel, out_shape=[jax.ShapeDtypeStruct(shape, dtype) for...]
    ppermute x44 -> x39, waiting for transfers between devices: 54.4 us -> 37.5 us  [swapped(): return lax.ppermute(value, 'ctx', [(i, i ^ step) for i in range(count)])]
    ppermute x14 -> x12, waiting for transfers between devices: 63.6 us -> 79.6 us  [turned(): lax.ppermute(value, 'wa', [(i, (i + step) % count) for i in range(count)])]
    ppermute x44 -> x39, starting transfers between devices: 41.9 us -> 48.6 us  [swapped(): return lax.ppermute(value, 'ctx', [(i, i ^ step) for i in range(count)])]
    unnamed x63 -> x57, local copies, waits for them, and re-layouts: 6.61 us -> 8.76 us
  transfers between devices with their start and end apart: 58 -> 51, of which waited for: 28 -> 21; matrix products, arithmetic and copies ran while one was open for 7% -> 6% of each run, Pallas kernels for 18% -> 21%
where the time goes in v4:
time: 321 us; the launch traced here: 320 us
  waiting for transfers between devices  117 us (36%)
  Pallas kernels  105 us (33%)
  starting transfers between devices  59.8 us (19%)
  other arithmetic  20.5 us (6%)
  local copies, waits for them, and re-layouts  16.3 us (5%)
    pallas_call x9, Pallas kernels, whole_call(): pl.pallas_call(kernel, out_shape=[jax.ShapeDtypeStruct(shape, dtype) for...  105 us
    ppermute x12, waiting for transfers between devices, turned(): lax.ppermute(value, 'wa', [(i, (i + step) % count) for i in range(count)])  79.6 us
    ppermute x39, starting transfers between devices, swapped(): return lax.ppermute(value, 'ctx', [(i, i ^ step) for i in range(count)])  48.6 us
    ppermute x39, waiting for transfers between devices, swapped(): return lax.ppermute(value, 'ctx', [(i, i ^ step) for i in range(count)])  37.5 us
    ppermute x12, starting transfers between devices, turned(): lax.ppermute(value, 'wa', [(i, (i + step) % count) for i in range(count)])  11.2 us
    unnamed x57, local copies, waits for them, and re-layouts  8.76 us
  transfers between devices with their start and end apart: 51, of which 21 were waited for; matrix products, arithmetic and copies ran while one was open for 6% of the time, Pallas kernels for 21%

profile of v4, /device:TPU:9, one launch (start us, length us, event | category | flops | bytes accessed | tf_op | source)
XLA Modules:
  0.0 320.0 jit_solution(8981492992125363949)
XLA Ops:
  5.6 3.4 %shard_map.416 = (bf16[112,1152]{1,0:T(8,128)(2,1)}, bf16[432,384]{1,0:T(8,128)(2,1)}) custom-call(s32[3]{0:T(128)} %pad_add_fusion.place, bf16[192,768]{1,0:T(8,128)(2,1)} %ww.1, bf16[192,768]{1,0:T(8,128)(2,1)} %we.1, bf16[192,768]{1,0:T(8,128)(2,1)} %ew.1, bf16[192,768]{1,0:T(8,128)(2,1)} %ee.1, bf16[192,768]{1,0:T(8,128)(2,1)} %key.1, ...), custom_call_target="tpu_custom_call" | custom-call | flops 3300000000 | bytes 3145728 | tf_op jit(solution)/shard_map/pallas_call | solution.py:1135
  10.5 5.2 %collective-permute-done.2 = bf16[112,1152]{1,0:T(8,128)(2,1)S(1)} collective-permute-done((bf16[112,1152]{1,0:T(8,128)(2,1)}, bf16[112,1152]{1,0:T(8,128)(2,1)S(1)}, u32[]{:S(2)}, u32[]{:S(2)}) %collective-permute-start.2) | collective-permute-done | bytes 258080 | tf_op jit(solution)/shard_map/ppermute | solution.py:489
  15.7 8.0 %collective-permute-done.3 = bf16[112,1152]{1,0:T(8,128)(2,1)S(1)} collective-permute-done((bf16[112,1152]{1,0:T(8,128)(2,1)}, bf16[112,1152]{1,0:T(8,128)(2,1)S(1)}, u32[]{:S(2)}, u32[]{:S(2)}) %collective-permute-start.3) | collective-permute-done | bytes 258080 | tf_op jit(solution)/shard_map/ppermute | solution.py:489
  27.1 6.9 %collective-permute-done.4.t3a = bf16[192,768]{1,0:T(8,128)(2,1)S(1)} collective-permute-done((bf16[192,768]{1,0:T(8,128)(2,1)S(1)}, bf16[192,768]{1,0:T(8,128)(2,1)S(1)}, u32[]{:S(2)}, u32[]{:S(2)}) %collective-permute-start.4) | collective-permute-done | bytes 294944 | tf_op jit(solution)/shard_map/ppermute | solution.py:484
  34.5 11.0 %collective-permute-done.6 = bf16[576,384]{1,0:T(8,128)(2,1)S(1)} collective-permute-done((bf16[576,384]{1,0:T(8,128)(2,1)S(1)}, bf16[576,384]{1,0:T(8,128)(2,1)S(1)}, u32[]{:S(2)}, u32[]{:S(2)}) %collective-permute-start.6) | collective-permute-done | bytes 442400 | tf_op jit(solution)/shard_map/ppermute | solution.py:489
  45.8 2.2 collective-permute-start.8
  50.6 8.1 %collective-permute-done.9 = bf16[208,384]{1,0:T(8,128)(2,1)S(1)} collective-permute-done((bf16[208,384]{1,0:T(8,128)(2,1)S(1)}, bf16[208,384]{1,0:T(8,128)(2,1)S(1)}, u32[]{:S(2)}, u32[]{:S(2)}) %collective-permute-start.9) | collective-permute-done | bytes 159776 | tf_op jit(solution)/shard_map/ppermute | solution.py:489
  58.7 4.6 %shard_map.417 = (bf16[768,1152]{1,0:T(8,128)(2,1)S(1)}, bf16[4,400,768]{2,1,0:T(8,128)(2,1)S(1)}, bf16[4,384,384]{2,1,0:T(8,128)(2,1)S(1)}, bf16[4,400,384]{2,1,0:T(8,128)(2,1)S(1)}) custom-call(s32[3]{0:T(128)S(1)} %copy-done, bf16[400,768]{1,0:T(8,128)(2,1)S(1)} %fusion.13.t0.text, bf16[400,768]{1,0:T(8,128)(2,1)S(1)} %collective-permute-done.t1, ...), custom_call_target="tpu_custom_call" | custom-call | flops 8800000000 | bytes 8388608 | tf_op jit(solution)/shard_map/pallas_call | solution.py:1135
  71.7 18.5 %shard_map.418 = (bf16[4,384,192]{2,1,0:T(8,128)(2,1)S(1)}, f32[4,192,384]{2,1,0:T(8,128)S(1)}, f32[4,3,1,384]{3,2,1,0:T(1,128)S(1)}, s32[2,4]{1,0:T(2,128)S(1)}) custom-call(s32[3]{0:T(128)S(1)} %copy-done, bf16[4,384,384]{2,1,0:T(8,128)(2,1)S(1)} %get-tuple-element.148.q_ref, bf16[4,400,384]{2,1,0:T(8,128)(2,1)S(1)} %get-tuple-element.152.own, ...), custom_call_target="tpu_custom_call" | custom-call | flops 27499999232 | bytes 26214400 | tf_op jit(solution)/shard_map/pallas_call | solution.py:1135
  94.8 6.1 %collective-permute-start.20 = (bf16[4,2,432,384]{3,2,1,0:T(8,128)(2,1)}, bf16[4,2,432,384]{3,2,1,0:T(8,128)(2,1)}, u32[]{:S(2)}, u32[]{:S(2)}) collective-permute-start(bf16[4,2,432,384]{3,2,1,0:T(8,128)(2,1)} %pad_maximum_fusion.near_own), channel_id=1, source_target_pairs={{0,4},{4,0},{8,12},{12,8},{16,20},{20,16},{24,28},{28,24},{1,5},{5... | collective-permute-start | bytes 7962632 | tf_op jit(solution)/shard_map/ppermute | solution.py:484
  107.2 3.3 %collective-permute-done.17.context1 = bf16[384,192]{1,0:T(8,128)(2,1)S(1)} collective-permute-done((bf16[384,192]{1,0:T(8,128)(2,1)}, bf16[384,192]{1,0:T(8,128)(2,1)S(1)}, u32[]{:S(2)}, u32[]{:S(2)}) %collective-permute-start.17) | collective-permute-done | bytes 147488 | tf_op jit(solution)/shard_map/ppermute | solution.py:484
  110.5 5.2 %collective-permute-done.19.context3 = bf16[384,192]{1,0:T(8,128)(2,1)S(1)} collective-permute-done((bf16[384,192]{1,0:T(8,128)(2,1)S(1)}, bf16[384,192]{1,0:T(8,128)(2,1)S(1)}, u32[]{:S(2)}, u32[]{:S(2)}) %collective-permute-start.19) | collective-permute-done | bytes 147488 | tf_op jit(solution)/shard_map/ppermute | solution.py:484
  116.7 33.9 %shard_map.419 = (bf16[384,768]{1,0:T(8,128)(2,1)}, f32[384,768]{1,0:T(8,128)}, bf16[4,384,192]{2,1,0:T(8,128)(2,1)S(1)}, bf16[4,4,448,384]{3,2,1,0:T(8,128)(2,1...) custom-call(s32[3]{0:T(128)S(1)} %copy-done, bf16[384,192]{1,0:T(8,128)(2,1)S(1)} %get-tuple-element.284.context0, ...), custom_call_target="tpu_custom_call" | custom-call | flops 38499999744 | bytes 36700160 | tf_op jit(solution)/shard_map/pallas_call | solution.py:1135
  154.9 6.0 %collective-permute-done.25 = bf16[4,448,384]{2,1,0:T(8,128)(2,1)S(1)} collective-permute-done((bf16[4,448,384]{2,1,0:T(8,128)(2,1)}, bf16[4,448,384]{2,1,0:T(8,128)(2,1)S(1)}, u32[]{:S(2)}, u32[]{:S(2)}) %collective-permute-start.25) | collective-permute-done | bytes 1376288 | tf_op jit(solution)/shard_map/ppermute | solution.py:484
  162.7 2.8 fusion.10
  168.5 28.0 %shard_map.420 = (bf16[4,384,768]{2,1,0:T(8,128)(2,1)S(1)}, bf16[4,384,384]{2,1,0:T(8,128)(2,1)S(1)}, bf16[4,384,384]{2,1,0:T(8,128)(2,1)S(1)}) custom-call(s32[3]{0:T(128)S(1)} %copy-done, s32[2,4]{1,0:T(2,128)S(1)} %get-tuple-element.166.bounds, bf16[4,384,384]{2,1,0:T(8,128)(2,1)S(1)} %copy-done.14, bf16[4,400,384]{2,1,0:T(8,128)(2,1)S(1)} %get-tuple-element.152.own, ...), custom_call_target="tpu_custom_call" | custom-call | flops 44000002048 | bytes 41943040 | tf_op jit(solution)/shard_map/pallas_call | solution.py:1135
  200.6 11.1 %collective-permute-start.31 = (bf16[4,384,384]{2,1,0:T(8,128)(2,1)S(1)}, bf16[4,384,384]{2,1,0:T(8,128)(2,1)S(1)}, u32[]{:S(2)}, u32[]{:S(2)}) collective-permute-start(bf16[4,384,384]{2,1,0:T(8,128)(2,1)S(1)} %get-tuple-element.186), channel_id=1, source_target_pairs={{0,4},{4,0},{8,12},{12,8},{16,20},{20,16},{24,28},{28,24},{1,5},{5... | collective-permute-start | bytes 3538952 | tf_op jit(solution)/shard_map/ppermute | solution.py:484
  211.6 2.8 fusion.6
  216.1 3.8 %shard_map.421 = (bf16[4,384,384]{2,1,0:T(8,128)(2,1)S(1)}, bf16[4,384,768]{2,1,0:T(8,128)(2,1)S(1)}) custom-call(bf16[4,384,768]{2,1,0:T(8,128)(2,1)S(1)} %copy-done.6, bf16[4,384,384]{2,1,0:T(8,128)(2,1)S(1)} %copy-done.12, bf16[4,384,384]{2,1,0:T(8,128)(2,1)S(1)} %collective-permute-done.31.dkv_other, bf16[768,1152]{1,0:T(8,128)(2,1)S(1)} %copy-done.10), custom_call_target="tpu_custom_call" | custom-call | flops 8800000000 | bytes 8388608 | tf_op jit(solution)/shard_map/pallas_call | solution.py:1135
  220.1 6.2 %shard_map.422 = (bf16[4,112,1152]{2,1,0:T(8,128)(2,1)S(1)}, bf16[4,112,1152]{2,1,0:T(8,128)(2,1)S(1)}) custom-call(s32[3]{0:T(128)S(1)} %copy-done, bf16[4,400,768]{2,1,0:T(8,128)(2,1)S(1)} %copy-done.8, bf16[4,384,768]{2,1,0:T(8,128)(2,1)S(1)} %copy-done.6, bf16[4,384,384]{2,1,0:T(8,128)(2,1)S(1)} %get-tuple-element.188.dkv), custom_call_target="tpu_custom_call" | custom-call | flops 11000000512 | bytes 10485760 | tf_op jit(solution)/shard_map/pallas_call | solution.py:1135
  226.2 5.3 %collective-permute-done.32 = bf16[2,448,384]{2,1,0:T(8,128)(2,1)S(1)} collective-permute-done((bf16[2,448,384]{2,1,0:T(8,128)(2,1)S(1)}, bf16[2,448,384]{2,1,0:T(8,128)(2,1)S(1)}, u32[]{:S(2)}, u32[]{:S(2)}) %collective-permute-start.32) | collective-permute-done | bytes 688160 | tf_op jit(solution)/shard_map/ppermute | solution.py:484
  232.7 2.4 fusion.3
  237.5 8.1 %collective-permute-done.34 = bf16[448,384]{1,0:T(8,128)(2,1)S(1)} collective-permute-done((bf16[448,384]{1,0:T(8,128)(2,1)S(1)}, bf16[448,384]{1,0:T(8,128)(2,1)S(1)}, u32[]{:S(2)}, u32[]{:S(2)}) %collective-permute-start.34) | collective-permute-done | bytes 344096 | tf_op jit(solution)/shard_map/ppermute | solution.py:489
  245.6 20.1 %collective-permute-done.35 = bf16[448,384]{1,0:T(8,128)(2,1)S(1)} collective-permute-done((bf16[448,384]{1,0:T(8,128)(2,1)S(1)}, bf16[448,384]{1,0:T(8,128)(2,1)S(1)}, u32[]{:S(2)}, u32[]{:S(2)}) %collective-permute-start.35) | collective-permute-done | bytes 344096 | tf_op jit(solution)/shard_map/ppermute | solution.py:489
  269.3 3.1 collective-permute-start.41
  272.4 2.3 collective-permute-done.40
  274.7 3.2 collective-permute-start.42
  277.9 11.7 %collective-permute-done.41 = bf16[112,1152]{1,0:T(8,128)(2,1)S(1)} collective-permute-done((bf16[112,1152]{1,0:T(8,128)(2,1)S(1)}, bf16[112,1152]{1,0:T(8,128)(2,1)S(1)}, u32[]{:S(2)}, u32[]{:S(2)}) %collective-permute-start.41) | collective-permute-done | bytes 258080 | tf_op jit(solution)/shard_map/ppermute | solution.py:489
  289.5 5.0 %collective-permute-done.42 = bf16[112,1152]{1,0:T(8,128)(2,1)S(1)} collective-permute-done((bf16[112,1152]{1,0:T(8,128)(2,1)S(1)}, bf16[112,1152]{1,0:T(8,128)(2,1)S(1)}, u32[]{:S(2)}, u32[]{:S(2)}) %collective-permute-start.42) | collective-permute-done | bytes 258080 | tf_op jit(solution)/shard_map/ppermute | solution.py:489
  300.7 3.3 %shard_map.423 = (f32[192,3072]{1,0:T(8,128)}, f32[768,768]{1,0:T(8,128)}, f32[192,768]{1,0:T(8,128)}, f32[16,384]{1,0:T(8,128)S(1)}) custom-call(s32[3]{0:T(128)S(1)} %copy-done, bf16[4,448,384]{2,1,0:T(8,128)(2,1)S(1)} %pad_maximum_fusion.1.own, bf16[4,448,384]{2,1,0:T(8,128)(2,1)S(1)} %collective-permute-done.49.other), custom_call_target="tpu_custom_call" | custom-call | flops 4400000000 | bytes 4194304 | tf_op jit(solution)/shard_map/pallas_call | solution.py:1135
  304.3 5.5 %collective-permute-done.48 = bf16[112,1152]{1,0:T(8,128)(2,1)S(1)} collective-permute-done((bf16[112,1152]{1,0:T(8,128)(2,1)S(1)}, bf16[112,1152]{1,0:T(8,128)(2,1)S(1)}, u32[]{:S(2)}, u32[]{:S(2)}) %collective-permute-start.48) | collective-permute-done | bytes 258080 | tf_op jit(solution)/shard_map/ppermute | solution.py:484
  313.4 3.0 shard_map.424
  (215 shorter events, 68.2 us)
Async XLA Ops:
  2.5 21.3 %collective-permute-start = (bf16[400,768]{1,0:T(8,128)(2,1)S(1)}, bf16[400,768]{1,0:T(8,128)(2,1)S(1)}, u32[]{:S(2)}, u32[]{:S(2)}) collective-permute-start(bf16[400,768]{1,0:T(8,128)(2,1)S(1)} %fusion.13.t0.text), channel_id=1, source_target_pairs={{0,8},{4,12},{8,0},{12,4},{16,24},{20,28},{24,16},{28,20},{1,9},{5... | collective-permute-start | bytes 1843208 | tf_op jit(solution)/shard_map/ppermute | solution.py:484
  3.7 20.0 %collective-permute-start.1 = (bf16[400,768]{1,0:T(8,128)(2,1)S(1)}, bf16[400,768]{1,0:T(8,128)(2,1)S(1)}, u32[]{:S(2)}, u32[]{:S(2)}) collective-permute-start(bf16[400,768]{1,0:T(8,128)(2,1)S(1)} %fusion.13.t0.text), channel_id=1, source_target_pairs={{0,16},{4,20},{8,24},{12,28},{16,0},{20,4},{24,8},{28,12},{1,17},{... | collective-permute-start | bytes 1843208 | tf_op jit(solution)/shard_map/ppermute | solution.py:484
  10.3 13.4 %collective-permute-start.3 = (bf16[112,1152]{1,0:T(8,128)(2,1)}, bf16[112,1152]{1,0:T(8,128)(2,1)S(1)}, u32[]{:S(2)}, u32[]{:S(2)}) collective-permute-start(bf16[112,1152]{1,0:T(8,128)(2,1)} %get-tuple-element.136), channel_id=1, source_target_pairs={{0,3},{1,0},{2,1},{3,2},{4,7},{5,4},{6,5},{7,6},{8,11},{9,8},{10,9... | collective-permute-start | bytes 774152 | tf_op jit(solution)/shard_map/ppermute | solution.py:489
  24.8 20.8 %collective-permute-start.7 = (bf16[624,384]{1,0:T(8,128)(2,1)S(1)}, bf16[624,384]{1,0:T(8,128)(2,1)S(1)}, u32[]{:S(2)}, u32[]{:S(2)}) collective-permute-start(bf16[624,384]{1,0:T(8,128)(2,1)S(1)} %pad_maximum_fusion.12), channel_id=1, source_target_pairs={{0,3},{1,0},{2,1},{3,2},{4,7},{5,4},{6,5},{7,6},{8,11},{9,8},{10,9... | collective-permute-start | bytes 1437704 | tf_op jit(solution)/shard_map/ppermute | solution.py:489
  25.0 20.6 %collective-permute-start.6 = (bf16[576,384]{1,0:T(8,128)(2,1)S(1)}, bf16[576,384]{1,0:T(8,128)(2,1)S(1)}, u32[]{:S(2)}, u32[]{:S(2)}) collective-permute-start(bf16[576,384]{1,0:T(8,128)(2,1)S(1)} %pad_maximum_fusion.13), channel_id=1, source_target_pairs={{0,1},{1,2},{2,3},{3,0},{4,5},{5,6},{6,7},{7,4},{8,9},{9,10},{10,1... | collective-permute-start | bytes 1327112 | tf_op jit(solution)/shard_map/ppermute | solution.py:489
  45.8 12.8 %collective-permute-start.8 = (bf16[4,112,1152]{2,1,0:T(8,128)(2,1)S(1)}, bf16[4,112,1152]{2,1,0:T(8,128)(2,1)S(1)}, u32[]{:S(2)}, u32[]{:S(2)}) collective-permute-start(bf16[4,112,1152]{2,1,0:T(8,128)(2,1)S(1)} %pad_maximum_fusion.3.mine), channel_id=1, source_target_pairs={{0,4},{4,0},{8,12},{12,8},{16,20},{20,16},{24,28},{28,24},{1,5},{5... | collective-permute-start | bytes 3096584 | tf_op jit(solution)/shard_map/ppermute | solution.py:484
  50.0 16.0 %collective-permute-start.11 = (bf16[2,432,384]{2,1,0:T(8,128)(2,1)S(1)}, bf16[2,432,384]{2,1,0:T(8,128)(2,1)S(1)}, u32[]{:S(2)}, u32[]{:S(2)}) collective-permute-start(bf16[2,432,384]{2,1,0:T(8,128)(2,1)S(1)} %get-tuple-element.290), channel_id=1, source_target_pairs={{0,8},{4,12},{8,0},{12,4},{16,24},{20,28},{24,16},{28,20},{1,9},{5... | collective-permute-start | bytes 1990664 | tf_op jit(solution)/shard_map/ppermute | solution.py:484
  50.3 15.6 %collective-permute-start.12 = (bf16[2,432,384]{2,1,0:T(8,128)(2,1)S(1)}, bf16[2,432,384]{2,1,0:T(8,128)(2,1)S(1)}, u32[]{:S(2)}, u32[]{:S(2)}) collective-permute-start(bf16[2,432,384]{2,1,0:T(8,128)(2,1)S(1)} %get-tuple-element.290), channel_id=1, source_target_pairs={{0,16},{4,20},{8,24},{12,28},{16,0},{20,4},{24,8},{28,12},{1,17},{... | collective-permute-start | bytes 1990664 | tf_op jit(solution)/shard_map/ppermute | solution.py:484
  67.7 22.5 %collective-permute-start.16 = (bf16[432,384]{1,0:T(8,128)(2,1)S(1)}, bf16[432,384]{1,0:T(8,128)(2,1)S(1)}, u32[]{:S(2)}, u32[]{:S(2)}) collective-permute-start(bf16[432,384]{1,0:T(8,128)(2,1)S(1)} %pad_maximum_fusion.14), channel_id=1, source_target_pairs={{0,24},{4,28},{8,16},{12,20},{16,8},{20,12},{24,0},{28,4},{1,25},{... | collective-permute-start | bytes 995336 | tf_op jit(solution)/shard_map/ppermute | solution.py:484
  70.2 21.1 %collective-permute-start.14 = (bf16[864,384]{1,0:T(8,128)(2,1)S(1)}, bf16[864,384]{1,0:T(8,128)(2,1)S(1)}, u32[]{:S(2)}, u32[]{:S(2)}) collective-permute-start(bf16[864,384]{1,0:T(8,128)(2,1)S(1)} %get-tuple-element.158), channel_id=1, source_target_pairs={{0,8},{4,12},{8,0},{12,4},{16,24},{20,28},{24,16},{28,20},{1,9},{5... | collective-permute-start | bytes 1990664 | tf_op jit(solution)/shard_map/ppermute | solution.py:484
  71.4 21.1 %collective-permute-start.15 = (bf16[864,384]{1,0:T(8,128)(2,1)S(1)}, bf16[864,384]{1,0:T(8,128)(2,1)S(1)}, u32[]{:S(2)}, u32[]{:S(2)}) collective-permute-start(bf16[864,384]{1,0:T(8,128)(2,1)S(1)} %get-tuple-element.159), channel_id=1, source_target_pairs={{0,16},{4,20},{8,24},{12,28},{16,0},{20,4},{24,8},{28,12},{1,17},{... | collective-permute-start | bytes 1990664 | tf_op jit(solution)/shard_map/ppermute | solution.py:484
  94.8 20.9 %collective-permute-start.20 = (bf16[4,2,432,384]{3,2,1,0:T(8,128)(2,1)}, bf16[4,2,432,384]{3,2,1,0:T(8,128)(2,1)}, u32[]{:S(2)}, u32[]{:S(2)}) collective-permute-start(bf16[4,2,432,384]{3,2,1,0:T(8,128)(2,1)} %pad_maximum_fusion.near_own), channel_id=1, source_target_pairs={{0,4},{4,0},{8,12},{12,8},{16,20},{20,16},{24,28},{28,24},{1,5},{5... | collective-permute-start | bytes 7962632 | tf_op jit(solution)/shard_map/ppermute | solution.py:484
  102.1 13.5 %collective-permute-start.21 = (bf16[4,432,384]{2,1,0:T(8,128)(2,1)}, bf16[4,432,384]{2,1,0:T(8,128)(2,1)}, u32[]{:S(2)}, u32[]{:S(2)}) collective-permute-start(bf16[4,432,384]{2,1,0:T(8,128)(2,1)} %pad_maximum_fusion.2.far_own), channel_id=1, source_target_pairs={{0,4},{4,0},{8,12},{12,8},{16,20},{20,16},{24,28},{28,24},{1,5},{5... | collective-permute-start | bytes 3981320 | tf_op jit(solution)/shard_map/ppermute | solution.py:484
  152.2 13.3 %collective-permute-start.22 = (bf16[384,192]{1,0:T(8,128)(2,1)S(1)}, bf16[384,192]{1,0:T(8,128)(2,1)S(1)}, u32[]{:S(2)}, u32[]{:S(2)}) collective-permute-start(bf16[384,192]{1,0:T(8,128)(2,1)S(1)} %get-tuple-element.279), channel_id=1, source_target_pairs={{0,8},{4,12},{8,0},{12,4},{16,24},{20,28},{24,16},{28,20},{1,9},{5... | collective-permute-start | bytes 442376 | tf_op jit(solution)/shard_map/ppermute | solution.py:484
  152.6 12.9 %collective-permute-start.23 = (bf16[384,192]{1,0:T(8,128)(2,1)S(1)}, bf16[384,192]{1,0:T(8,128)(2,1)S(1)}, u32[]{:S(2)}, u32[]{:S(2)}) collective-permute-start(bf16[384,192]{1,0:T(8,128)(2,1)S(1)} %get-tuple-element.278), channel_id=1, source_target_pairs={{0,16},{4,20},{8,24},{12,28},{16,0},{20,4},{24,8},{28,12},{1,17},{... | collective-permute-start | bytes 442376 | tf_op jit(solution)/shard_map/ppermute | solution.py:484
  165.5 33.5 %collective-permute-start.27 = (bf16[2,448,384]{2,1,0:T(8,128)(2,1)S(1)}, bf16[2,448,384]{2,1,0:T(8,128)(2,1)S(1)}, u32[]{:S(2)}, u32[]{:S(2)}) collective-permute-start(bf16[2,448,384]{2,1,0:T(8,128)(2,1)S(1)} %get-tuple-element.180), channel_id=1, source_target_pairs={{0,8},{4,12},{8,0},{12,4},{16,24},{20,28},{24,16},{28,20},{1,9},{5... | collective-permute-start | bytes 2064392 | tf_op jit(solution)/shard_map/ppermute | solution.py:484
  165.9 33.1 %collective-permute-start.28 = (bf16[2,448,384]{2,1,0:T(8,128)(2,1)S(1)}, bf16[2,448,384]{2,1,0:T(8,128)(2,1)S(1)}, u32[]{:S(2)}, u32[]{:S(2)}) collective-permute-start(bf16[2,448,384]{2,1,0:T(8,128)(2,1)S(1)} %get-tuple-element.181), channel_id=1, source_target_pairs={{0,16},{4,20},{8,24},{12,28},{16,0},{20,4},{24,8},{28,12},{1,17},{... | collective-permute-start | bytes 2064392 | tf_op jit(solution)/shard_map/ppermute | solution.py:484
  167.2 31.9 %collective-permute-start.29 = (bf16[2,448,384]{2,1,0:T(8,128)(2,1)S(1)}, bf16[2,448,384]{2,1,0:T(8,128)(2,1)S(1)}, u32[]{:S(2)}, u32[]{:S(2)}) collective-permute-start(bf16[2,448,384]{2,1,0:T(8,128)(2,1)S(1)} %get-tuple-element.182), channel_id=1, source_target_pairs={{0,8},{4,12},{8,0},{12,4},{16,24},{20,28},{24,16},{28,20},{1,9},{5... | collective-permute-start | bytes 2064392 | tf_op jit(solution)/shard_map/ppermute | solution.py:484
  167.4 31.6 %collective-permute-start.30 = (bf16[2,448,384]{2,1,0:T(8,128)(2,1)S(1)}, bf16[2,448,384]{2,1,0:T(8,128)(2,1)S(1)}, u32[]{:S(2)}, u32[]{:S(2)}) collective-permute-start(bf16[2,448,384]{2,1,0:T(8,128)(2,1)S(1)} %get-tuple-element.183), channel_id=1, source_target_pairs={{0,16},{4,20},{8,24},{12,28},{16,0},{20,4},{24,8},{28,12},{1,17},{... | collective-permute-start | bytes 2064392 | tf_op jit(solution)/shard_map/ppermute | solution.py:484
  200.6 15.5 %collective-permute-start.31 = (bf16[4,384,384]{2,1,0:T(8,128)(2,1)S(1)}, bf16[4,384,384]{2,1,0:T(8,128)(2,1)S(1)}, u32[]{:S(2)}, u32[]{:S(2)}) collective-permute-start(bf16[4,384,384]{2,1,0:T(8,128)(2,1)S(1)} %get-tuple-element.186), channel_id=1, source_target_pairs={{0,4},{4,0},{8,12},{12,8},{16,20},{20,16},{24,28},{28,24},{1,5},{5... | collective-permute-start | bytes 3538952 | tf_op jit(solution)/shard_map/ppermute | solution.py:484
  214.5 17.1 %collective-permute-start.32 = (bf16[2,448,384]{2,1,0:T(8,128)(2,1)S(1)}, bf16[2,448,384]{2,1,0:T(8,128)(2,1)S(1)}, u32[]{:S(2)}, u32[]{:S(2)}) collective-permute-start(bf16[2,448,384]{2,1,0:T(8,128)(2,1)S(1)} %get-tuple-element.193), channel_id=1, source_target_pairs={{0,8},{4,12},{8,0},{12,4},{16,24},{20,28},{24,16},{28,20},{1,9},{5... | collective-permute-start | bytes 2064392 | tf_op jit(solution)/shard_map/ppermute | solution.py:484
  214.8 16.8 %collective-permute-start.33 = (bf16[2,448,384]{2,1,0:T(8,128)(2,1)S(1)}, bf16[2,448,384]{2,1,0:T(8,128)(2,1)S(1)}, u32[]{:S(2)}, u32[]{:S(2)}) collective-permute-start(bf16[2,448,384]{2,1,0:T(8,128)(2,1)S(1)} %get-tuple-element.194), channel_id=1, source_target_pairs={{0,16},{4,20},{8,24},{12,28},{16,0},{20,4},{24,8},{28,12},{1,17},{... | collective-permute-start | bytes 2064392 | tf_op jit(solution)/shard_map/ppermute | solution.py:484
  231.6 34.2 %collective-permute-start.39 = (bf16[4,112,1152]{2,1,0:T(8,128)(2,1)S(1)}, bf16[4,112,1152]{2,1,0:T(8,128)(2,1)S(1)}, u32[]{:S(2)}, u32[]{:S(2)}) collective-permute-start(bf16[4,112,1152]{2,1,0:T(8,128)(2,1)S(1)} %get-tuple-element.206), channel_id=1, source_target_pairs={{0,4},{4,0},{8,12},{12,8},{16,20},{20,16},{24,28},{28,24},{1,5},{5... | collective-permute-start | bytes 3096584 | tf_op jit(solution)/shard_map/ppermute | solution.py:484
  235.9 29.8 %collective-permute-start.37 = (bf16[2,192,768]{2,1,0:T(8,128)(2,1)S(1)}, bf16[2,192,768]{2,1,0:T(8,128)(2,1)S(1)}, u32[]{:S(2)}, u32[]{:S(2)}) collective-permute-start(bf16[2,192,768]{2,1,0:T(8,128)(2,1)S(1)} %pad_maximum_fusion.10), channel_id=1, source_target_pairs={{0,8},{4,12},{8,0},{12,4},{16,24},{20,28},{24,16},{28,20},{1,9},{5... | collective-permute-start | bytes 1769480 | tf_op jit(solution)/shard_map/ppermute | solution.py:484
  237.2 28.6 %collective-permute-start.38 = (bf16[2,192,768]{2,1,0:T(8,128)(2,1)S(1)}, bf16[2,192,768]{2,1,0:T(8,128)(2,1)S(1)}, u32[]{:S(2)}, u32[]{:S(2)}) collective-permute-start(bf16[2,192,768]{2,1,0:T(8,128)(2,1)S(1)} %pad_maximum_fusion.11), channel_id=1, source_target_pairs={{0,16},{4,20},{8,24},{12,28},{16,0},{20,4},{24,8},{28,12},{1,17},{... | collective-permute-start | bytes 1769480 | tf_op jit(solution)/shard_map/ppermute | solution.py:484
  237.5 28.2 %collective-permute-start.35 = (bf16[448,384]{1,0:T(8,128)(2,1)S(1)}, bf16[448,384]{1,0:T(8,128)(2,1)S(1)}, u32[]{:S(2)}, u32[]{:S(2)}) collective-permute-start(bf16[448,384]{1,0:T(8,128)(2,1)S(1)} %get-tuple-element.202), channel_id=1, source_target_pairs={{0,2},{1,3},{2,0},{3,1},{4,6},{5,7},{6,4},{7,5},{8,10},{9,11},{10,... | collective-permute-start | bytes 1032200 | tf_op jit(solution)/shard_map/ppermute | solution.py:489
  245.6 20.1 %collective-permute-start.36 = (bf16[448,384]{1,0:T(8,128)(2,1)S(1)}, bf16[448,384]{1,0:T(8,128)(2,1)S(1)}, u32[]{:S(2)}, u32[]{:S(2)}) collective-permute-start(bf16[448,384]{1,0:T(8,128)(2,1)S(1)} %get-tuple-element.203), channel_id=1, source_target_pairs={{0,3},{1,0},{2,1},{3,2},{4,7},{5,4},{6,5},{7,6},{8,11},{9,8},{10,9... | collective-permute-start | bytes 1032200 | tf_op jit(solution)/shard_map/ppermute | solution.py:489
  266.5 28.0 %collective-permute-start.43 = (bf16[832,384]{1,0:T(8,128)(2,1)S(1)}, bf16[832,384]{1,0:T(8,128)(2,1)S(1)}, u32[]{:S(2)}, u32[]{:S(2)}) collective-permute-start(bf16[832,384]{1,0:T(8,128)(2,1)S(1)} %get-tuple-element.218), channel_id=1, source_target_pairs={{0,8},{4,12},{8,0},{12,4},{16,24},{20,28},{24,16},{28,20},{1,9},{5... | collective-permute-start | bytes 1916936 | tf_op jit(solution)/shard_map/ppermute | solution.py:484
  267.8 26.8 %collective-permute-start.44 = (bf16[832,384]{1,0:T(8,128)(2,1)S(1)}, bf16[832,384]{1,0:T(8,128)(2,1)S(1)}, u32[]{:S(2)}, u32[]{:S(2)}) collective-permute-start(bf16[832,384]{1,0:T(8,128)(2,1)S(1)} %get-tuple-element.219), channel_id=1, source_target_pairs={{0,16},{4,20},{8,24},{12,28},{16,0},{20,4},{24,8},{28,12},{1,17},{... | collective-permute-start | bytes 1916936 | tf_op jit(solution)/shard_map/ppermute | solution.py:484
  268.1 26.4 %collective-permute-start.45 = (bf16[448,384]{1,0:T(8,128)(2,1)S(1)}, bf16[448,384]{1,0:T(8,128)(2,1)S(1)}, u32[]{:S(2)}, u32[]{:S(2)}) collective-permute-start(bf16[448,384]{1,0:T(8,128)(2,1)S(1)} %add_convert_fusion.2), channel_id=1, source_target_pairs={{0,24},{4,28},{8,16},{12,20},{16,8},{20,12},{24,0},{28,4},{1,25},{... | collective-permute-start | bytes 1032200 | tf_op jit(solution)/shard_map/ppermute | solution.py:484
  269.3 20.3 %collective-permute-start.41 = (bf16[112,1152]{1,0:T(8,128)(2,1)S(1)}, bf16[112,1152]{1,0:T(8,128)(2,1)S(1)}, u32[]{:S(2)}, u32[]{:S(2)}) collective-permute-start(bf16[112,1152]{1,0:T(8,128)(2,1)S(1)} %get-tuple-element.216), channel_id=1, source_target_pairs={{0,2},{1,3},{2,0},{3,1},{4,6},{5,7},{6,4},{7,5},{8,10},{9,11},{10,... | collective-permute-start | bytes 774152 | tf_op jit(solution)/shard_map/ppermute | solution.py:489
  274.7 19.8 %collective-permute-start.42 = (bf16[112,1152]{1,0:T(8,128)(2,1)S(1)}, bf16[112,1152]{1,0:T(8,128)(2,1)S(1)}, u32[]{:S(2)}, u32[]{:S(2)}) collective-permute-start(bf16[112,1152]{1,0:T(8,128)(2,1)S(1)} %get-tuple-element.217), channel_id=1, source_target_pairs={{0,3},{1,0},{2,1},{3,2},{4,7},{5,4},{6,5},{7,6},{8,11},{9,8},{10,9... | collective-permute-start | bytes 774152 | tf_op jit(solution)/shard_map/ppermute | solution.py:489
  (46 other events, 319.5 us)

commit v5 on v4

--- a/solution.py
+++ b/solution.py
@@ -836,10 +836,10 @@
     inner_shard,
     outer_shard,
     output_shard,
-    near_own,
-    near_other,
-    far_own,
-    far_other,
+    first_own,
+    first_other,
+    second_own,
+    second_other,
     result,
     grad_sum,
     grad_context,
@@ -881,50 +881,47 @@
     pltpu.make_async_copy(
         inner_shard, inner_w.at[pl.ds(pl.multiple_of(rows * wa, 16), rows), :], in_sems.at[1]
     ).start()
+    deep = first_own.shape[0] // 7
+    places = [(0, 0, 0, 1), (0, 1, 0, 3), (0, 2, 1, 1), (0, 3, 1, 3), (0, 4, 2, 1), (0, 5, 2, 3), (0, 6, 0, 2)]
+    places += [(1, 0, 1, 2), (1, 1, 3, 3), (1, 2, 2, 2), (1, 3, 3, 1), (1, 4, 3, 2)]
+    sides = []
+    for which, at, m, k in places:
+        g = jnp.bitwise_xor(chip, m)
+        z = lax.rem(wa - k + parts, parts)
+        sides.append(((first_own, second_own)[which], deep * at, g, core, z))
+        sides.append(((first_other, second_other)[which], deep * at, g, 1 - core, z))
+    for source, at, g, side, z in sides:
+        pltpu.make_async_copy(
+            source.at[pl.ds(at + 2 * rows, quarter), :],
+            output_w.at[
+                pl.ds(pl.multiple_of(rows * z + quarter * g, 16), quarter),
+                pl.ds(pl.multiple_of(slot_w * side, TILE), slot_w),
+            ],
+            in_sems.at[0],
+        ).start()
+    for source, at, g, side, z in sides:
+        pltpu.make_async_copy(
+            source.at[pl.ds(at, rows), :],
+            inner_w.at[
+                pl.ds(pl.multiple_of(rows * z, 16), rows),
+                pl.ds(pl.multiple_of(slot_w * (2 * g + side), TILE), slot_w),
+            ],
+            in_sems.at[1],
+        ).start()
     pltpu.make_async_copy(
         outer_shard, outer_w.at[pl.ds(pl.multiple_of(dmod * wa, 16), dmod), :], in_sems.at[2]
     ).start()
-
-    def fetch(m, unused):
-        g = jnp.bitwise_xor(chip, m)
-        for source, side, far in (
-            (near_own, core, 0),
-            (near_other, 1 - core, 0),
-            (far_own, core, 1),
-            (far_other, 1 - core, 1),
-        ):
-            s = 2 * g + side
-            for u in range(2 - far):
-                z = lax.rem(wa - 1 - far - 2 * u + parts, parts)
-                piece = source.at[m] if far else source.at[m, u]
-                pltpu.make_async_copy(
-                    piece.at[pl.ds(2 * rows, quarter), :],
-                    output_w.at[
-                        pl.ds(pl.multiple_of(rows * z + quarter * g, 16), quarter),
-                        pl.ds(pl.multiple_of(slot_w * side, TILE), slot_w),
-                    ],
-                    in_sems.at[0],
-                ).start()
-                pltpu.make_async_copy(
-                    piece.at[pl.ds(0, rows), :],
-                    inner_w.at[
-                        pl.ds(pl.multiple_of(rows * z, 16), rows),
-                        pl.ds(pl.multiple_of(slot_w * s, TILE), slot_w),
-                    ],
-                    in_sems.at[1],
-                ).start()
-                for v in range(2):
-                    pltpu.make_async_copy(
-                        piece.at[pl.ds(rows + half * v, half), :],
-                        outer_w.at[
-                            pl.ds(pl.multiple_of(dmod * z + half * s, 16), half),
-                            pl.ds(slot_w * v, slot_w),
-                        ],
-                        in_sems.at[2],
-                    ).start()
-        return 0
-
-    lax.fori_loop(0, CHIPS, fetch, 0)
+    for source, at, g, side, z in sides:
+        for v in range(2):
+            pltpu.make_async_copy(
+                source.at[pl.ds(at + rows + half * v, half), :],
+                outer_w.at[
+                    pl.ds(pl.multiple_of(dmod * z + half * (2 * g + side), 16), half),
+                    pl.ds(slot_w * v, slot_w),
+                ],
+                in_sems.at[2],
+            ).start()
+
     names = ("outb", "g1", "s1", "outerb", "g2", "s2")
     vec = {name: vectors[k : k + 1, :] for k, name in enumerate(names)}
 
@@ -936,18 +933,18 @@
     low = first.astype(bf16)
 
     pltpu.make_async_copy(inner_w, inner_w, in_sems.at[1]).wait()
-    pltpu.make_async_copy(outer_w, outer_w, in_sems.at[2]).wait()
-
-    def forward(s, ffn):
-        at = pl.ds(pl.multiple_of(slot_w * s, TILE), slot_w)
+
+    def forward(s, carry):
+        at = pl.ds(pl.multiple_of(2 * slot_w * s, TILE), 2 * slot_w)
         inner = plain_product(low, inner_w[:, at]) + inner_bias[:, at]
         cdf = 0.5 + 0.5 * lax.erf(inner * (0.5**0.5))
-        active = (inner * cdf).astype(bf16)
-        hidden[:, at] = active
+        hidden[:, at] = (inner * cdf).astype(bf16)
         slope[:, at] = cdf + inner * (jnp.exp(-0.5 * inner * inner) * (0.5 / jnp.pi) ** 0.5)
-        return ffn + plain_product(active, outer_w[at, :])
-
-    ffn = lax.fori_loop(0, 2 * CHIPS, forward, jnp.broadcast_to(vec["outerb"], (tok, dmod)))
+        return carry
+
+    lax.fori_loop(0, CHIPS, forward, 0)
+    pltpu.make_async_copy(outer_w, outer_w, in_sems.at[2]).wait()
+    ffn = plain_product(hidden[...], outer_w[...]) + vec["outerb"]
     second, unit_two, inverse_two = normed(first + ffn, vec["g2"], vec["s2"])
     result[...] = second.astype(bf16)
     grad_out = cotangent[...].astype(f32)
@@ -966,16 +963,19 @@
     put(10, summed_rows(grad_out))
     low_turned = low.astype(f32).T.astype(bf16)
 
-    def backward(s, grad_first):
-        at = pl.ds(pl.multiple_of(slot_w * s, TILE), slot_w)
+    def backward(s, carry):
+        at = pl.ds(pl.multiple_of(2 * slot_w * s, TILE), 2 * slot_w)
         grad_hidden = lanes_product(low_two, outer_w[at, :])
         grad_inner = (grad_hidden * slope[:, at]).astype(bf16)
         outer_g[at, :] = rows_product(hidden[:, at], low_two).astype(bf16)
+        hidden[:, at] = grad_inner
         inner_g[:, at] = plain_product(low_turned, grad_inner).astype(bf16)
-        sums[s // 2, pl.ds(12 + lax.rem(s, 2), 1), :] = summed_rows(grad_inner.astype(f32))
-        return grad_first + lanes_product(grad_inner, inner_w[:, at])
-
-    grad_first = lax.fori_loop(0, 2 * CHIPS, backward, grad_two)
+        totals = summed_rows(grad_inner.astype(f32))
+        sums[s, 12:13, :] = totals[:, :slot_w]
+        sums[s, 13:14, :] = totals[:, slot_w:]
+        return carry
+
+    lax.fori_loop(0, CHIPS, backward, 0)
 
     def targets():
         for m in range(CHIPS):
@@ -1000,6 +1000,7 @@
                 out_sems.at[sem],
             ).start()
 
+    grad_first = grad_two + lanes_product(hidden[...], inner_w[...])
     put(2, summed_rows(grad_first * unit_one))
     put(4, summed_rows(grad_first))
     grad_one = normed_back(grad_first, unit_one, inverse_one, vec["g1"])
@@ -1187,12 +1188,6 @@
     ff = inner_weight.shape[1]
     slot_w = ff // (2 * CHIPS)
 
-    tags = (segment_ids[0] * 2 + token_types[0]).astype(bf16)
-    tag_rows = jnp.pad(tags[None], ((0, TAG_ROWS - 1), (0, dmod - tok)))
-    text = jnp.concatenate([inputs, tag_rows], axis=0)
-    cut = tok // 2
-    text_x, text_y = swapped(text, 2), swapped(text, 4)
-
     lines = (
         bias_wordword,
         bias_wordentity,
@@ -1218,6 +1213,13 @@
         micros=3,
         mebibytes=58,
     )
+    inputs, mine, slot = ordered(inputs, mine, slot)
+    tags = (segment_ids[0] * 2 + token_types[0]).astype(bf16)
+    tag_rows = jnp.pad(tags[None], ((0, TAG_ROWS - 1), (0, dmod - tok)))
+    text = jnp.concatenate([inputs, tag_rows], axis=0)
+    cut = tok // 2
+    text_x, text_y = swapped(text, 2), swapped(text, 4)
+
     one, three = turned(mine, 1), turned(mine, 3)
     text_x, text_y, one, three, slot = ordered(text_x, text_y, one, three, slot)
     text_far = swapped(text_x[:cut], 4), swapped(text_y[cut:], 2)
@@ -1256,10 +1258,12 @@
     )
     kv, near_x, near_y, far_slot = ordered(kv, near_x, near_y, far_slot)
     kv_other = swapped(kv, 1)
+    first_slots = jnp.concatenate([*near_slot, *near_x, *near_y, far_slot], axis=0)
     to_x = jnp.concatenate([far_slot, near_y[1]], axis=0)
     to_y = jnp.concatenate([far_slot, near_x[0]], axis=0)
-    kv_other, to_x, to_y = ordered(kv_other, to_x, to_y)
+    kv_other, to_x, to_y, first_slots = ordered(kv_other, to_x, to_y, first_slots)
     to_x, to_y, to_far = swapped(to_x, 2), swapped(to_y, 4), swapped(far_slot, 6)
+    first_other = swapped(first_slots, 1)
 
     context, turned_out, lse, bounds = whole_call(
         attend_kernel,
@@ -1280,17 +1284,14 @@
         micros=25,
         mebibytes=20,
     )
-    context, to_x, to_y, to_far = ordered(context, to_x, to_y, to_far)
+    context, to_x, to_y, to_far, first_other = ordered(context, to_x, to_y, to_far, first_other)
 
     def exchanged(value):
         return [value[0]] + [swapped(value[m], 2 * m) for m in range(1, CHIPS)]
 
     contexts = exchanged(context)
-    deep = slot.shape[0]
-    near_slots = jnp.stack([near_slot, near_x, near_y, jnp.stack([to_y[deep:], to_x[deep:]])])
-    near_slots = near_slots, swapped(near_slots, 1)
-    far_slots = jnp.stack([far_slot, to_x[:deep], to_y[:deep], to_far])
-    far_slots = far_slots, swapped(far_slots, 1)
+    second_slots = jnp.concatenate([to_x, to_y, to_far], axis=0)
+    second_other = swapped(second_slots, 1)
 
     slot_rows = 2 * rows + quarter + TAG_ROWS
     result, grad_sum, grad_context, kept, sent_far, sent_near = whole_call(
@@ -1299,7 +1300,7 @@
         + [(a, vmem) for a in (*contexts, text, cotangent[0], vectors, full_inner_bias)]
         + [
             (a, hbm)
-            for a in (inner_weight, outer_weight, output_weight, *near_slots, *far_slots)
+            for a in (inner_weight, outer_weight, output_weight, first_slots, first_other, second_slots, second_other)
         ],
         [
             ((tok, dmod), bf16, vmem),
@@ -1323,7 +1324,7 @@
             pltpu.SemaphoreType.DMA((3,)),
             pltpu.SemaphoreType.DMA((3,)),
         ],
-        micros=35,
+        micros=26,
         mebibytes=50,
     )
     grad_pieces = exchanged(grad_context)
@@ -1368,7 +1369,7 @@
             pltpu.VMEM((3, 2 * tok, 4 * HD), bf16),
             pltpu.VMEM((3, KEY_BLOCK, 2 * tok), bf16),
         ],
-        micros=40,
+        micros=34,
         mebibytes=36,
     )
     dq, dkv, dkv_sent, far_x, far_y, near_x, near_y = lax.optimization_barrier(

time: 321 us -> 312 us (0.972)
  other arithmetic: 20.5 us -> 14.5 us
  waiting for transfers between devices: 117 us -> 113 us
    ppermute x12, starting transfers between devices: 11.2 us -> 25.7 us  [turned(): lax.ppermute(value, 'wa', [(i, (i + step) % count) for i in range(count)])]
    ppermute x39, starting transfers between devices: 48.6 us -> 37.2 us  [swapped(): return lax.ppermute(value, 'ctx', [(i, i ^ step) for i in range(count)])]
    another operation x5 -> x2, other arithmetic: 5.93 us -> 2.48 us
    unnamed x57 -> x75, local copies, waits for them, and re-layouts: 8.76 us -> 11.2 us
  transfers between devices with their start and end apart: 51 -> 51, of which waited for: 21 -> 21; matrix products, arithmetic and copies ran while one was open for 6% -> 5% of each run, Pallas kernels for 21% -> 22%
where the time goes in v5:
time: 312 us; the launch traced here: 314 us
  waiting for transfers between devices  113 us (36%)
  Pallas kernels  102 us (33%)
  starting transfers between devices  62.9 us (20%)
  local copies, waits for them, and re-layouts  19.4 us (6%)
  other arithmetic  14.5 us (5%)
    pallas_call x9, Pallas kernels, whole_call(): pl.pallas_call(kernel, out_shape=[jax.ShapeDtypeStruct(shape, dtype) for...  102 us
    ppermute x12, waiting for transfers between devices, turned(): lax.ppermute(value, 'wa', [(i, (i + step) % count) for i in range(count)])  78.8 us
    ppermute x39, starting transfers between devices, swapped(): return lax.ppermute(value, 'ctx', [(i, i ^ step) for i in range(count)])  37.2 us
    ppermute x39, waiting for transfers between devices, swapped(): return lax.ppermute(value, 'ctx', [(i, i ^ step) for i in range(count)])  34.6 us
    ppermute x12, starting transfers between devices, turned(): lax.ppermute(value, 'wa', [(i, (i + step) % count) for i in range(count)])  25.7 us
    unnamed x75, local copies, waits for them, and re-layouts  11.2 us
  transfers between devices with their start and end apart: 51, of which 21 were waited for; matrix products, arithmetic and copies ran while one was open for 5% of the time, Pallas kernels for 22%

profile of v5, /device:TPU:9, one launch (start us, length us, event | category | flops | bytes accessed | tf_op | source)
XLA Modules:
  0.0 313.8 jit_solution(4278866897772748310)
XLA Ops:
  1.3 3.4 %shard_map.416 = (bf16[112,1152]{1,0:T(8,128)(2,1)}, bf16[432,384]{1,0:T(8,128)(2,1)}) custom-call(s32[3]{0:T(128)} %pad_add_fusion.place, bf16[192,768]{1,0:T(8,128)(2,1)} %ww.1, bf16[192,768]{1,0:T(8,128)(2,1)} %we.1, bf16[192,768]{1,0:T(8,128)(2,1)} %ew.1, bf16[192,768]{1,0:T(8,128)(2,1)} %ee.1, bf16[192,768]{1,0:T(8,128)(2,1)} %key.1, ...), custom_call_target="tpu_custom_call" | custom-call | flops 3300000000 | bytes 3145728 | tf_op jit(solution)/shard_map/pallas_call | solution.py:1136
  8.8 5.2 %collective-permute-done.2 = bf16[112,1152]{1,0:T(8,128)(2,1)S(1)} collective-permute-done((bf16[112,1152]{1,0:T(8,128)(2,1)}, bf16[112,1152]{1,0:T(8,128)(2,1)S(1)}, u32[]{:S(2)}, u32[]{:S(2)}) %collective-permute-start.2) | collective-permute-done | bytes 258080 | tf_op jit(solution)/shard_map/ppermute | solution.py:489
  14.0 8.0 %collective-permute-done.3 = bf16[112,1152]{1,0:T(8,128)(2,1)S(1)} collective-permute-done((bf16[112,1152]{1,0:T(8,128)(2,1)}, bf16[112,1152]{1,0:T(8,128)(2,1)S(1)}, u32[]{:S(2)}, u32[]{:S(2)}) %collective-permute-start.3) | collective-permute-done | bytes 258080 | tf_op jit(solution)/shard_map/ppermute | solution.py:489
  24.4 6.9 %collective-permute-done.4.t3a = bf16[192,768]{1,0:T(8,128)(2,1)S(1)} collective-permute-done((bf16[192,768]{1,0:T(8,128)(2,1)S(1)}, bf16[192,768]{1,0:T(8,128)(2,1)S(1)}, u32[]{:S(2)}, u32[]{:S(2)}) %collective-permute-start.4) | collective-permute-done | bytes 294944 | tf_op jit(solution)/shard_map/ppermute | solution.py:484
  31.8 12.1 %collective-permute-done.6 = bf16[576,384]{1,0:T(8,128)(2,1)S(1)} collective-permute-done((bf16[576,384]{1,0:T(8,128)(2,1)S(1)}, bf16[576,384]{1,0:T(8,128)(2,1)S(1)}, u32[]{:S(2)}, u32[]{:S(2)}) %collective-permute-start.6) | collective-permute-done | bytes 442400 | tf_op jit(solution)/shard_map/ppermute | solution.py:489
  49.5 6.6 %collective-permute-done.9 = bf16[208,384]{1,0:T(8,128)(2,1)S(1)} collective-permute-done((bf16[208,384]{1,0:T(8,128)(2,1)S(1)}, bf16[208,384]{1,0:T(8,128)(2,1)S(1)}, u32[]{:S(2)}, u32[]{:S(2)}) %collective-permute-start.9) | collective-permute-done | bytes 159776 | tf_op jit(solution)/shard_map/ppermute | solution.py:489
  56.1 4.6 %shard_map.417 = (bf16[768,1152]{1,0:T(8,128)(2,1)S(1)}, bf16[4,400,768]{2,1,0:T(8,128)(2,1)S(1)}, bf16[4,384,384]{2,1,0:T(8,128)(2,1)S(1)}, bf16[4,400,384]{2,1,0:T(8,128)(2,1)S(1)}) custom-call(s32[3]{0:T(128)S(1)} %copy-done, bf16[400,768]{1,0:T(8,128)(2,1)S(1)} %fusion.13.t0.text, bf16[400,768]{1,0:T(8,128)(2,1)S(1)} %collective-permute-done.t1, ...), custom_call_target="tpu_custom_call" | custom-call | flops 8800000000 | bytes 8388608 | tf_op jit(solution)/shard_map/pallas_call | solution.py:1136
  65.6 2.1 collective-permute-start.16
  70.9 20.5 %shard_map.418 = (bf16[4,384,192]{2,1,0:T(8,128)(2,1)S(1)}, f32[4,192,384]{2,1,0:T(8,128)S(1)}, f32[4,3,1,384]{3,2,1,0:T(1,128)S(1)}, s32[2,4]{1,0:T(2,128)S(1)}) custom-call(s32[3]{0:T(128)S(1)} %copy-done, bf16[4,384,384]{2,1,0:T(8,128)(2,1)S(1)} %get-tuple-element.156.q_ref, bf16[4,400,384]{2,1,0:T(8,128)(2,1)S(1)} %get-tuple-element.160.own, ...), custom_call_target="tpu_custom_call" | custom-call | flops 27499999232 | bytes 26214400 | tf_op jit(solution)/shard_map/pallas_call | solution.py:1136
  99.6 3.3 %collective-permute-done.18.context1 = bf16[384,192]{1,0:T(8,128)(2,1)S(1)} collective-permute-done((bf16[384,192]{1,0:T(8,128)(2,1)}, bf16[384,192]{1,0:T(8,128)(2,1)S(1)}, u32[]{:S(2)}, u32[]{:S(2)}) %collective-permute-start.18) | collective-permute-done | bytes 147488 | tf_op jit(solution)/shard_map/ppermute | solution.py:484
  103.1 4.4 %collective-permute-done.20.context3 = bf16[384,192]{1,0:T(8,128)(2,1)S(1)} collective-permute-done((bf16[384,192]{1,0:T(8,128)(2,1)}, bf16[384,192]{1,0:T(8,128)(2,1)S(1)}, u32[]{:S(2)}, u32[]{:S(2)}) %collective-permute-start.20) | collective-permute-done | bytes 147488 | tf_op jit(solution)/shard_map/ppermute | solution.py:484
  108.4 25.6 %shard_map.419 = (bf16[384,768]{1,0:T(8,128)(2,1)}, f32[384,768]{1,0:T(8,128)}, bf16[4,384,192]{2,1,0:T(8,128)(2,1)S(1)}, bf16[4,4,448,384]{3,2,1,0:T(8,128)(2,1...) custom-call(s32[3]{0:T(128)S(1)} %copy-done, bf16[384,192]{1,0:T(8,128)(2,1)S(1)} %get-tuple-element.294.context0, ...), custom_call_target="tpu_custom_call" | custom-call | flops 28600000512 | bytes 27262976 | tf_op jit(solution)/shard_map/pallas_call | solution.py:1136
  138.4 6.0 %collective-permute-done.25 = bf16[4,448,384]{2,1,0:T(8,128)(2,1)S(1)} collective-permute-done((bf16[4,448,384]{2,1,0:T(8,128)(2,1)}, bf16[4,448,384]{2,1,0:T(8,128)(2,1)S(1)}, u32[]{:S(2)}, u32[]{:S(2)}) %collective-permute-start.25) | collective-permute-done | bytes 1376288 | tf_op jit(solution)/shard_map/ppermute | solution.py:484
  146.2 2.8 fusion.10
  152.1 31.3 %shard_map.420 = (bf16[4,384,768]{2,1,0:T(8,128)(2,1)S(1)}, bf16[4,384,384]{2,1,0:T(8,128)(2,1)S(1)}, bf16[4,384,384]{2,1,0:T(8,128)(2,1)S(1)}) custom-call(s32[3]{0:T(128)S(1)} %copy-done, s32[2,4]{1,0:T(2,128)S(1)} %get-tuple-element.176.bounds, bf16[4,384,384]{2,1,0:T(8,128)(2,1)S(1)} %copy-done.14, bf16[4,400,384]{2,1,0:T(8,128)(2,1)S(1)} %get-tuple-element.160.own, ...), custom_call_target="tpu_custom_call" | custom-call | flops 37399998464 | bytes 35651584 | tf_op jit(solution)/shard_map/pallas_call | solution.py:1136
  187.3 2.8 fusion.6
  191.8 3.9 %shard_map.421 = (bf16[4,384,384]{2,1,0:T(8,128)(2,1)S(1)}, bf16[4,384,768]{2,1,0:T(8,128)(2,1)S(1)}) custom-call(bf16[4,384,768]{2,1,0:T(8,128)(2,1)S(1)} %copy-done.6, bf16[4,384,384]{2,1,0:T(8,128)(2,1)S(1)} %copy-done.12, bf16[4,384,384]{2,1,0:T(8,128)(2,1)S(1)} %collective-permute-done.31.dkv_other, bf16[768,1152]{1,0:T(8,128)(2,1)S(1)} %copy-done.10), custom_call_target="tpu_custom_call" | custom-call | flops 8800000000 | bytes 8388608 | tf_op jit(solution)/shard_map/pallas_call | solution.py:1136
  195.8 6.4 %shard_map.422 = (bf16[4,112,1152]{2,1,0:T(8,128)(2,1)S(1)}, bf16[4,112,1152]{2,1,0:T(8,128)(2,1)S(1)}) custom-call(s32[3]{0:T(128)S(1)} %copy-done, bf16[4,400,768]{2,1,0:T(8,128)(2,1)S(1)} %copy-done.8, bf16[4,384,768]{2,1,0:T(8,128)(2,1)S(1)} %copy-done.6, bf16[4,384,384]{2,1,0:T(8,128)(2,1)S(1)} %get-tuple-element.198.dkv), custom_call_target="tpu_custom_call" | custom-call | flops 11000000512 | bytes 10485760 | tf_op jit(solution)/shard_map/pallas_call | solution.py:1136
  202.2 4.5 %collective-permute-done.32 = bf16[2,448,384]{2,1,0:T(8,128)(2,1)S(1)} collective-permute-done((bf16[2,448,384]{2,1,0:T(8,128)(2,1)S(1)}, bf16[2,448,384]{2,1,0:T(8,128)(2,1)S(1)}, u32[]{:S(2)}, u32[]{:S(2)}) %collective-permute-start.32) | collective-permute-done | bytes 688160 | tf_op jit(solution)/shard_map/ppermute | solution.py:484
  209.1 2.4 fusion.3
  214.1 17.7 %collective-permute-start.35 = (bf16[448,384]{1,0:T(8,128)(2,1)S(1)}, bf16[448,384]{1,0:T(8,128)(2,1)S(1)}, u32[]{:S(2)}, u32[]{:S(2)}) collective-permute-start(bf16[448,384]{1,0:T(8,128)(2,1)S(1)} %get-tuple-element.212), channel_id=1, source_target_pairs={{0,2},{1,3},{2,0},{3,1},{4,6},{5,7},{6,4},{7,5},{8,10},{9,11},{10,... | collective-permute-start | bytes 1032200 | tf_op jit(solution)/shard_map/ppermute | solution.py:489
  231.8 4.6 %collective-permute-done.34 = bf16[448,384]{1,0:T(8,128)(2,1)S(1)} collective-permute-done((bf16[448,384]{1,0:T(8,128)(2,1)S(1)}, bf16[448,384]{1,0:T(8,128)(2,1)S(1)}, u32[]{:S(2)}, u32[]{:S(2)}) %collective-permute-start.34) | collective-permute-done | bytes 344096 | tf_op jit(solution)/shard_map/ppermute | solution.py:489
  236.4 3.1 collective-permute-start.36
  239.5 13.7 %collective-permute-done.35 = bf16[448,384]{1,0:T(8,128)(2,1)S(1)} collective-permute-done((bf16[448,384]{1,0:T(8,128)(2,1)S(1)}, bf16[448,384]{1,0:T(8,128)(2,1)S(1)}, u32[]{:S(2)}, u32[]{:S(2)}) %collective-permute-start.35) | collective-permute-done | bytes 344096 | tf_op jit(solution)/shard_map/ppermute | solution.py:489
  253.2 7.5 %collective-permute-done.36 = bf16[448,384]{1,0:T(8,128)(2,1)S(1)} collective-permute-done((bf16[448,384]{1,0:T(8,128)(2,1)S(1)}, bf16[448,384]{1,0:T(8,128)(2,1)S(1)}, u32[]{:S(2)}, u32[]{:S(2)}) %collective-permute-start.36) | collective-permute-done | bytes 344096 | tf_op jit(solution)/shard_map/ppermute | solution.py:489
  261.6 3.6 %collective-permute-start.43 = (bf16[832,384]{1,0:T(8,128)(2,1)S(1)}, bf16[832,384]{1,0:T(8,128)(2,1)S(1)}, u32[]{:S(2)}, u32[]{:S(2)}) collective-permute-start(bf16[832,384]{1,0:T(8,128)(2,1)S(1)} %get-tuple-element.228), channel_id=1, source_target_pairs={{0,8},{4,12},{8,0},{12,4},{16,24},{20,28},{24,16},{28,20},{1,9},{5... | collective-permute-start | bytes 1916936 | tf_op jit(solution)/shard_map/ppermute | solution.py:484
  266.4 6.4 %collective-permute-done.40 = bf16[112,1152]{1,0:T(8,128)(2,1)S(1)} collective-permute-done((bf16[112,1152]{1,0:T(8,128)(2,1)S(1)}, bf16[112,1152]{1,0:T(8,128)(2,1)S(1)}, u32[]{:S(2)}, u32[]{:S(2)}) %collective-permute-start.40) | collective-permute-done | bytes 258080 | tf_op jit(solution)/shard_map/ppermute | solution.py:489
  272.8 14.7 %collective-permute-done.41 = bf16[112,1152]{1,0:T(8,128)(2,1)S(1)} collective-permute-done((bf16[112,1152]{1,0:T(8,128)(2,1)S(1)}, bf16[112,1152]{1,0:T(8,128)(2,1)S(1)}, u32[]{:S(2)}, u32[]{:S(2)}) %collective-permute-start.41) | collective-permute-done | bytes 258080 | tf_op jit(solution)/shard_map/ppermute | solution.py:489
  288.1 1.8 collective-permute-start.49
  295.1 3.3 %shard_map.423 = (f32[192,3072]{1,0:T(8,128)}, f32[768,768]{1,0:T(8,128)}, f32[192,768]{1,0:T(8,128)}, f32[16,384]{1,0:T(8,128)S(1)}) custom-call(s32[3]{0:T(128)S(1)} %copy-done, bf16[4,448,384]{2,1,0:T(8,128)(2,1)S(1)} %pad_maximum_fusion.own, bf16[4,448,384]{2,1,0:T(8,128)(2,1)S(1)} %collective-permute-done.49.other), custom_call_target="tpu_custom_call" | custom-call | flops 4400000000 | bytes 4194304 | tf_op jit(solution)/shard_map/pallas_call | solution.py:1136
  298.4 5.5 %collective-permute-done.48 = bf16[112,1152]{1,0:T(8,128)(2,1)S(1)} collective-permute-done((bf16[112,1152]{1,0:T(8,128)(2,1)S(1)}, bf16[112,1152]{1,0:T(8,128)(2,1)S(1)}, u32[]{:S(2)}, u32[]{:S(2)}) %collective-permute-start.48) | collective-permute-done | bytes 258080 | tf_op jit(solution)/shard_map/ppermute | solution.py:484
  307.2 3.1 shard_map.424
  (228 shorter events, 64.3 us)
Async XLA Ops:
  4.8 17.2 %collective-permute-start = (bf16[400,768]{1,0:T(8,128)(2,1)S(1)}, bf16[400,768]{1,0:T(8,128)(2,1)S(1)}, u32[]{:S(2)}, u32[]{:S(2)}) collective-permute-start(bf16[400,768]{1,0:T(8,128)(2,1)S(1)} %fusion.13.t0.text), channel_id=1, source_target_pairs={{0,8},{4,12},{8,0},{12,4},{16,24},{20,28},{24,16},{28,20},{1,9},{5... | collective-permute-start | bytes 1843208 | tf_op jit(solution)/shard_map/ppermute | solution.py:484
  6.1 16.0 %collective-permute-start.1 = (bf16[400,768]{1,0:T(8,128)(2,1)S(1)}, bf16[400,768]{1,0:T(8,128)(2,1)S(1)}, u32[]{:S(2)}, u32[]{:S(2)}) collective-permute-start(bf16[400,768]{1,0:T(8,128)(2,1)S(1)} %fusion.13.t0.text), channel_id=1, source_target_pairs={{0,16},{4,20},{8,24},{12,28},{16,0},{20,4},{24,8},{28,12},{1,17},{... | collective-permute-start | bytes 1843208 | tf_op jit(solution)/shard_map/ppermute | solution.py:484
  8.6 13.4 %collective-permute-start.3 = (bf16[112,1152]{1,0:T(8,128)(2,1)}, bf16[112,1152]{1,0:T(8,128)(2,1)S(1)}, u32[]{:S(2)}, u32[]{:S(2)}) collective-permute-start(bf16[112,1152]{1,0:T(8,128)(2,1)} %get-tuple-element.144), channel_id=1, source_target_pairs={{0,3},{1,0},{2,1},{3,2},{4,7},{5,4},{6,5},{7,6},{8,11},{9,8},{10,9... | collective-permute-start | bytes 774152 | tf_op jit(solution)/shard_map/ppermute | solution.py:489
  22.1 21.8 %collective-permute-start.7 = (bf16[624,384]{1,0:T(8,128)(2,1)S(1)}, bf16[624,384]{1,0:T(8,128)(2,1)S(1)}, u32[]{:S(2)}, u32[]{:S(2)}) collective-permute-start(bf16[624,384]{1,0:T(8,128)(2,1)S(1)} %pad_maximum_fusion.10), channel_id=1, source_target_pairs={{0,3},{1,0},{2,1},{3,2},{4,7},{5,4},{6,5},{7,6},{8,11},{9,8},{10,9... | collective-permute-start | bytes 1437704 | tf_op jit(solution)/shard_map/ppermute | solution.py:489
  22.3 21.6 %collective-permute-start.6 = (bf16[576,384]{1,0:T(8,128)(2,1)S(1)}, bf16[576,384]{1,0:T(8,128)(2,1)S(1)}, u32[]{:S(2)}, u32[]{:S(2)}) collective-permute-start(bf16[576,384]{1,0:T(8,128)(2,1)S(1)} %pad_maximum_fusion.11), channel_id=1, source_target_pairs={{0,1},{1,2},{2,3},{3,0},{4,5},{5,6},{6,7},{7,4},{8,9},{9,10},{10,1... | collective-permute-start | bytes 1327112 | tf_op jit(solution)/shard_map/ppermute | solution.py:489
  47.9 15.9 %collective-permute-start.11 = (bf16[2,432,384]{2,1,0:T(8,128)(2,1)S(1)}, bf16[2,432,384]{2,1,0:T(8,128)(2,1)S(1)}, u32[]{:S(2)}, u32[]{:S(2)}) collective-permute-start(bf16[2,432,384]{2,1,0:T(8,128)(2,1)S(1)} %pad_maximum_fusion.7), channel_id=1, source_target_pairs={{0,8},{4,12},{8,0},{12,4},{16,24},{20,28},{24,16},{28,20},{1,9},{5... | collective-permute-start | bytes 1990664 | tf_op jit(solution)/shard_map/ppermute | solution.py:484
  48.3 15.6 %collective-permute-start.12 = (bf16[2,432,384]{2,1,0:T(8,128)(2,1)S(1)}, bf16[2,432,384]{2,1,0:T(8,128)(2,1)S(1)}, u32[]{:S(2)}, u32[]{:S(2)}) collective-permute-start(bf16[2,432,384]{2,1,0:T(8,128)(2,1)S(1)} %pad_maximum_fusion.7), channel_id=1, source_target_pairs={{0,16},{4,20},{8,24},{12,28},{16,0},{20,4},{24,8},{28,12},{1,17},{... | collective-permute-start | bytes 1990664 | tf_op jit(solution)/shard_map/ppermute | solution.py:484
  65.6 25.9 %collective-permute-start.16 = (bf16[432,384]{1,0:T(8,128)(2,1)S(1)}, bf16[432,384]{1,0:T(8,128)(2,1)S(1)}, u32[]{:S(2)}, u32[]{:S(2)}) collective-permute-start(bf16[432,384]{1,0:T(8,128)(2,1)S(1)} %pad_maximum_fusion.12), channel_id=1, source_target_pairs={{0,24},{4,28},{8,16},{12,20},{16,8},{20,12},{24,0},{28,4},{1,25},{... | collective-permute-start | bytes 995336 | tf_op jit(solution)/shard_map/ppermute | solution.py:484
  69.4 22.1 %collective-permute-start.17 = (bf16[3024,384]{1,0:T(8,128)(2,1)S(1)}, bf16[3024,384]{1,0:T(8,128)(2,1)S(1)}, u32[]{:S(2)}, u32[]{:S(2)}) collective-permute-start(bf16[3024,384]{1,0:T(8,128)(2,1)S(1)} %constant_dynamic-update-slice_fusion.first_own), channel_id=1, source_target_pairs={{0,4},{4,0},{8,12},{12,8},{16,20},{20,16},{24,28},{28,24},{1,5},{5... | collective-permute-start | bytes 6967304 | tf_op jit(solution)/shard_map/ppermute | solution.py:484
  69.7 21.8 %collective-permute-start.14 = (bf16[864,384]{1,0:T(8,128)(2,1)S(1)}, bf16[864,384]{1,0:T(8,128)(2,1)S(1)}, u32[]{:S(2)}, u32[]{:S(2)}) collective-permute-start(bf16[864,384]{1,0:T(8,128)(2,1)S(1)} %get-tuple-element.166), channel_id=1, source_target_pairs={{0,8},{4,12},{8,0},{12,4},{16,24},{20,28},{24,16},{28,20},{1,9},{5... | collective-permute-start | bytes 1990664 | tf_op jit(solution)/shard_map/ppermute | solution.py:484
  70.0 21.5 %collective-permute-start.15 = (bf16[864,384]{1,0:T(8,128)(2,1)S(1)}, bf16[864,384]{1,0:T(8,128)(2,1)S(1)}, u32[]{:S(2)}, u32[]{:S(2)}) collective-permute-start(bf16[864,384]{1,0:T(8,128)(2,1)S(1)} %get-tuple-element.167), channel_id=1, source_target_pairs={{0,16},{4,20},{8,24},{12,28},{16,0},{20,4},{24,8},{28,12},{1,17},{... | collective-permute-start | bytes 1990664 | tf_op jit(solution)/shard_map/ppermute | solution.py:484
  94.5 13.0 %collective-permute-start.21 = (bf16[2160,384]{1,0:T(8,128)(2,1)}, bf16[2160,384]{1,0:T(8,128)(2,1)}, u32[]{:S(2)}, u32[]{:S(2)}) collective-permute-start(bf16[2160,384]{1,0:T(8,128)(2,1)} %constant_dynamic-update-slice_fusion.3.second_own), channel_id=1, source_target_pairs={{0,4},{4,0},{8,12},{12,8},{16,20},{20,16},{24,28},{28,24},{1,5},{5... | collective-permute-start | bytes 4976648 | tf_op jit(solution)/shard_map/ppermute | solution.py:484
  135.7 13.3 %collective-permute-start.22 = (bf16[384,192]{1,0:T(8,128)(2,1)S(1)}, bf16[384,192]{1,0:T(8,128)(2,1)S(1)}, u32[]{:S(2)}, u32[]{:S(2)}) collective-permute-start(bf16[384,192]{1,0:T(8,128)(2,1)S(1)} %get-tuple-element.289), channel_id=1, source_target_pairs={{0,8},{4,12},{8,0},{12,4},{16,24},{20,28},{24,16},{28,20},{1,9},{5... | collective-permute-start | bytes 442376 | tf_op jit(solution)/shard_map/ppermute | solution.py:484
  136.8 12.3 %collective-permute-start.23 = (bf16[384,192]{1,0:T(8,128)(2,1)S(1)}, bf16[384,192]{1,0:T(8,128)(2,1)S(1)}, u32[]{:S(2)}, u32[]{:S(2)}) collective-permute-start(bf16[384,192]{1,0:T(8,128)(2,1)S(1)} %get-tuple-element.288), channel_id=1, source_target_pairs={{0,16},{4,20},{8,24},{12,28},{16,0},{20,4},{24,8},{28,12},{1,17},{... | collective-permute-start | bytes 442376 | tf_op jit(solution)/shard_map/ppermute | solution.py:484
  149.0 36.8 %collective-permute-start.27 = (bf16[2,448,384]{2,1,0:T(8,128)(2,1)S(1)}, bf16[2,448,384]{2,1,0:T(8,128)(2,1)S(1)}, u32[]{:S(2)}, u32[]{:S(2)}) collective-permute-start(bf16[2,448,384]{2,1,0:T(8,128)(2,1)S(1)} %get-tuple-element.190), channel_id=1, source_target_pairs={{0,8},{4,12},{8,0},{12,4},{16,24},{20,28},{24,16},{28,20},{1,9},{5... | collective-permute-start | bytes 2064392 | tf_op jit(solution)/shard_map/ppermute | solution.py:484
  150.1 35.7 %collective-permute-start.28 = (bf16[2,448,384]{2,1,0:T(8,128)(2,1)S(1)}, bf16[2,448,384]{2,1,0:T(8,128)(2,1)S(1)}, u32[]{:S(2)}, u32[]{:S(2)}) collective-permute-start(bf16[2,448,384]{2,1,0:T(8,128)(2,1)S(1)} %get-tuple-element.191), channel_id=1, source_target_pairs={{0,16},{4,20},{8,24},{12,28},{16,0},{20,4},{24,8},{28,12},{1,17},{... | collective-permute-start | bytes 2064392 | tf_op jit(solution)/shard_map/ppermute | solution.py:484
  150.7 35.2 %collective-permute-start.29 = (bf16[2,448,384]{2,1,0:T(8,128)(2,1)S(1)}, bf16[2,448,384]{2,1,0:T(8,128)(2,1)S(1)}, u32[]{:S(2)}, u32[]{:S(2)}) collective-permute-start(bf16[2,448,384]{2,1,0:T(8,128)(2,1)S(1)} %get-tuple-element.192), channel_id=1, source_target_pairs={{0,8},{4,12},{8,0},{12,4},{16,24},{20,28},{24,16},{28,20},{1,9},{5... | collective-permute-start | bytes 2064392 | tf_op jit(solution)/shard_map/ppermute | solution.py:484
  151.8 34.0 %collective-permute-start.30 = (bf16[2,448,384]{2,1,0:T(8,128)(2,1)S(1)}, bf16[2,448,384]{2,1,0:T(8,128)(2,1)S(1)}, u32[]{:S(2)}, u32[]{:S(2)}) collective-permute-start(bf16[2,448,384]{2,1,0:T(8,128)(2,1)S(1)} %get-tuple-element.193), channel_id=1, source_target_pairs={{0,16},{4,20},{8,24},{12,28},{16,0},{20,4},{24,8},{28,12},{1,17},{... | collective-permute-start | bytes 2064392 | tf_op jit(solution)/shard_map/ppermute | solution.py:484
  190.2 16.6 %collective-permute-start.32 = (bf16[2,448,384]{2,1,0:T(8,128)(2,1)S(1)}, bf16[2,448,384]{2,1,0:T(8,128)(2,1)S(1)}, u32[]{:S(2)}, u32[]{:S(2)}) collective-permute-start(bf16[2,448,384]{2,1,0:T(8,128)(2,1)S(1)} %get-tuple-element.203), channel_id=1, source_target_pairs={{0,8},{4,12},{8,0},{12,4},{16,24},{20,28},{24,16},{28,20},{1,9},{5... | collective-permute-start | bytes 2064392 | tf_op jit(solution)/shard_map/ppermute | solution.py:484
  191.2 16.2 %collective-permute-start.33 = (bf16[2,448,384]{2,1,0:T(8,128)(2,1)S(1)}, bf16[2,448,384]{2,1,0:T(8,128)(2,1)S(1)}, u32[]{:S(2)}, u32[]{:S(2)}) collective-permute-start(bf16[2,448,384]{2,1,0:T(8,128)(2,1)S(1)} %get-tuple-element.204), channel_id=1, source_target_pairs={{0,16},{4,20},{8,24},{12,28},{16,0},{20,4},{24,8},{28,12},{1,17},{... | collective-permute-start | bytes 2064392 | tf_op jit(solution)/shard_map/ppermute | solution.py:484
  207.4 53.3 %collective-permute-start.39 = (bf16[4,112,1152]{2,1,0:T(8,128)(2,1)S(1)}, bf16[4,112,1152]{2,1,0:T(8,128)(2,1)S(1)}, u32[]{:S(2)}, u32[]{:S(2)}) collective-permute-start(bf16[4,112,1152]{2,1,0:T(8,128)(2,1)S(1)} %get-tuple-element.216), channel_id=1, source_target_pairs={{0,4},{4,0},{8,12},{12,8},{16,20},{20,16},{24,28},{28,24},{1,5},{5... | collective-permute-start | bytes 3096584 | tf_op jit(solution)/shard_map/ppermute | solution.py:484
  212.2 24.2 %collective-permute-start.34 = (bf16[448,384]{1,0:T(8,128)(2,1)S(1)}, bf16[448,384]{1,0:T(8,128)(2,1)S(1)}, u32[]{:S(2)}, u32[]{:S(2)}) collective-permute-start(bf16[448,384]{1,0:T(8,128)(2,1)S(1)} %get-tuple-element.211), channel_id=1, source_target_pairs={{0,1},{1,2},{2,3},{3,0},{4,5},{5,6},{6,7},{7,4},{8,9},{9,10},{10,1... | collective-permute-start | bytes 1032200 | tf_op jit(solution)/shard_map/ppermute | solution.py:489
  212.3 48.4 %collective-permute-start.37 = (bf16[2,192,768]{2,1,0:T(8,128)(2,1)S(1)}, bf16[2,192,768]{2,1,0:T(8,128)(2,1)S(1)}, u32[]{:S(2)}, u32[]{:S(2)}) collective-permute-start(bf16[2,192,768]{2,1,0:T(8,128)(2,1)S(1)} %pad_maximum_fusion.8), channel_id=1, source_target_pairs={{0,8},{4,12},{8,0},{12,4},{16,24},{20,28},{24,16},{28,20},{1,9},{5... | collective-permute-start | bytes 1769480 | tf_op jit(solution)/shard_map/ppermute | solution.py:484
  212.8 47.9 %collective-permute-start.38 = (bf16[2,192,768]{2,1,0:T(8,128)(2,1)S(1)}, bf16[2,192,768]{2,1,0:T(8,128)(2,1)S(1)}, u32[]{:S(2)}, u32[]{:S(2)}) collective-permute-start(bf16[2,192,768]{2,1,0:T(8,128)(2,1)S(1)} %pad_maximum_fusion.9), channel_id=1, source_target_pairs={{0,16},{4,20},{8,24},{12,28},{16,0},{20,4},{24,8},{28,12},{1,17},{... | collective-permute-start | bytes 1769480 | tf_op jit(solution)/shard_map/ppermute | solution.py:484
  214.1 39.1 %collective-permute-start.35 = (bf16[448,384]{1,0:T(8,128)(2,1)S(1)}, bf16[448,384]{1,0:T(8,128)(2,1)S(1)}, u32[]{:S(2)}, u32[]{:S(2)}) collective-permute-start(bf16[448,384]{1,0:T(8,128)(2,1)S(1)} %get-tuple-element.212), channel_id=1, source_target_pairs={{0,2},{1,3},{2,0},{3,1},{4,6},{5,7},{6,4},{7,5},{8,10},{9,11},{10,... | collective-permute-start | bytes 1032200 | tf_op jit(solution)/shard_map/ppermute | solution.py:489
  236.4 24.3 %collective-permute-start.36 = (bf16[448,384]{1,0:T(8,128)(2,1)S(1)}, bf16[448,384]{1,0:T(8,128)(2,1)S(1)}, u32[]{:S(2)}, u32[]{:S(2)}) collective-permute-start(bf16[448,384]{1,0:T(8,128)(2,1)S(1)} %get-tuple-element.213), channel_id=1, source_target_pairs={{0,3},{1,0},{2,1},{3,2},{4,7},{5,4},{6,5},{7,6},{8,11},{9,8},{10,9... | collective-permute-start | bytes 1032200 | tf_op jit(solution)/shard_map/ppermute | solution.py:489
  261.6 26.0 %collective-permute-start.43 = (bf16[832,384]{1,0:T(8,128)(2,1)S(1)}, bf16[832,384]{1,0:T(8,128)(2,1)S(1)}, u32[]{:S(2)}, u32[]{:S(2)}) collective-permute-start(bf16[832,384]{1,0:T(8,128)(2,1)S(1)} %get-tuple-element.228), channel_id=1, source_target_pairs={{0,8},{4,12},{8,0},{12,4},{16,24},{20,28},{24,16},{28,20},{1,9},{5... | collective-permute-start | bytes 1916936 | tf_op jit(solution)/shard_map/ppermute | solution.py:484
  265.2 22.4 %collective-permute-start.44 = (bf16[832,384]{1,0:T(8,128)(2,1)S(1)}, bf16[832,384]{1,0:T(8,128)(2,1)S(1)}, u32[]{:S(2)}, u32[]{:S(2)}) collective-permute-start(bf16[832,384]{1,0:T(8,128)(2,1)S(1)} %get-tuple-element.229), channel_id=1, source_target_pairs={{0,16},{4,20},{8,24},{12,28},{16,0},{20,4},{24,8},{28,12},{1,17},{... | collective-permute-start | bytes 1916936 | tf_op jit(solution)/shard_map/ppermute | solution.py:484
  266.1 21.4 %collective-permute-start.45 = (bf16[448,384]{1,0:T(8,128)(2,1)S(1)}, bf16[448,384]{1,0:T(8,128)(2,1)S(1)}, u32[]{:S(2)}, u32[]{:S(2)}) collective-permute-start(bf16[448,384]{1,0:T(8,128)(2,1)S(1)} %add_convert_fusion.2), channel_id=1, source_target_pairs={{0,24},{4,28},{8,16},{12,20},{16,8},{20,12},{24,0},{28,4},{1,25},{... | collective-permute-start | bytes 1032200 | tf_op jit(solution)/shard_map/ppermute | solution.py:484
  266.4 21.1 %collective-permute-start.41 = (bf16[112,1152]{1,0:T(8,128)(2,1)S(1)}, bf16[112,1152]{1,0:T(8,128)(2,1)S(1)}, u32[]{:S(2)}, u32[]{:S(2)}) collective-permute-start(bf16[112,1152]{1,0:T(8,128)(2,1)S(1)} %get-tuple-element.226), channel_id=1, source_target_pairs={{0,2},{1,3},{2,0},{3,1},{4,6},{5,7},{6,4},{7,5},{8,10},{9,11},{10,... | collective-permute-start | bytes 774152 | tf_op jit(solution)/shard_map/ppermute | solution.py:489
  272.8 14.7 %collective-permute-start.42 = (bf16[112,1152]{1,0:T(8,128)(2,1)S(1)}, bf16[112,1152]{1,0:T(8,128)(2,1)S(1)}, u32[]{:S(2)}, u32[]{:S(2)}) collective-permute-start(bf16[112,1152]{1,0:T(8,128)(2,1)S(1)} %get-tuple-element.227), channel_id=1, source_target_pairs={{0,3},{1,0},{2,1},{3,2},{4,7},{5,4},{6,5},{7,6},{8,11},{9,8},{10,9... | collective-permute-start | bytes 774152 | tf_op jit(solution)/shard_map/ppermute | solution.py:489
  291.1 12.8 %collective-permute-start.48 = (bf16[112,1152]{1,0:T(8,128)(2,1)S(1)}, bf16[112,1152]{1,0:T(8,128)(2,1)S(1)}, u32[]{:S(2)}, u32[]{:S(2)}) collective-permute-start(bf16[112,1152]{1,0:T(8,128)(2,1)S(1)} %add_convert_fusion.5), channel_id=1, source_target_pairs={{0,24},{4,28},{8,16},{12,20},{16,8},{20,12},{24,0},{28,4},{1,25},{... | collective-permute-start | bytes 774152 | tf_op jit(solution)/shard_map/ppermute | solution.py:484
  (51 other events, 343.3 us)
